TPU v7x, 128 devices: a whole 4x4x4 slice. The times are simulated.
128 devices in a mesh: row: 16 (over x_lo, z, core), col: 8 (over x_hi, y).
Axes of the slice: x: 4 (x_hi: 2, x_lo: 2; x = x_hi * 2 + x_lo), y: 4, z: 4, core: 2. Of those that a mesh axis runs over, the one named last changes fastest.
Arguments:
- eigvecs: float32 [512, 262144], P(('row', 'col')), may hold values from -6 to 6
- panels: bfloat16 [8, 262144, 128], P('col', 'row'), may hold values from -0.01171875 to 0.01171875
- tfactors: bfloat16 [8, 128, 128], P('col'), as said below
- owners: int32 [4], replicated, may hold values from 0 to 7, as said below
- offsets: int32 [4], replicated, may hold values from 0 to 65408, as said below
Outputs:
- back: float32 [512, 262144], P('col', 'row')
Inputs may be any that keep to these rules, and one draw needn't show every extreme that they name: `owners`: distinct grid columns. `offsets`: multiples of 128. `tfactors`: each matrix is upper triangular with its diagonal between 1 and 8.
All inputs are finite; a program needn't handle non-finite values.
Results may differ from a plain program's by a relative error of at most 0.0003.
Values may be sent and summed in bfloat16 or wider, within the bound.
No kernel may reach another device: no remote copies, remote signals or barrier semaphores. Data moves between devices by JAX's collectives and lax.ppermute only.
A program may use at most 128 MiB of HBM per device.

v0:
```python
import jax
import jax.numpy as jnp
from jax import lax
from jax.sharding import PartitionSpec as P

PANELS = 4


def from_root(value, axis, root):
    mine = lax.axis_index(axis) == root
    return lax.psum(jnp.where(mine, value, jnp.zeros_like(value)), axis)


def reflector_block(stored, offset, first_row):
    row_ids = first_row + lax.broadcasted_iota(jnp.int32, stored.shape, 0)
    col_ids = lax.broadcasted_iota(jnp.int32, stored.shape, 1)
    below = row_ids - col_ids - offset
    unit = jnp.where(below == 0, jnp.float32(1.0), jnp.float32(0.0))
    return jnp.where(below > 0, stored.astype(jnp.float32), unit)


def local(eigvecs, panels, tfactors, owners, offsets):
    highest = lax.Precision.HIGHEST
    spread = lax.all_to_all(eigvecs, ("row", "col"), split_axis=1, concat_axis=0, tiled=True)
    field = lax.all_to_all(spread, "col", split_axis=0, concat_axis=1, tiled=True)
    local_rows = field.shape[1]
    first_row = lax.axis_index("row") * local_rows
    for panel in reversed(range(PANELS)):
        stored, triangle = (
            from_root(panels[0], "col", owners[panel]),
            from_root(tfactors[0], "col", owners[panel]),
        )
        reflector = reflector_block(stored, offsets[panel], first_row)
        partial_sum = jnp.dot(
            field, reflector, precision=highest, preferred_element_type=jnp.float32
        )
        projection = lax.psum(partial_sum, "row")
        coeffs = jnp.dot(
            projection,
            triangle.astype(jnp.float32).T,
            precision=highest,
            preferred_element_type=jnp.float32,
        )
        field = field - jnp.dot(
            coeffs, reflector.T, precision=highest, preferred_element_type=jnp.float32
        )
    return field


def solution(mesh):
    in_specs = (P(("row", "col"), None), P("col", "row", None), P("col", None, None), P(), P())
    out_specs = P("col", "row")
    return jax.shard_map(local, mesh=mesh, in_specs=in_specs, out_specs=out_specs, check_vma=False)
```

profile of v0, /device:TPU:0, one launch (start us, length us, event | category | flops | bytes accessed | tf_op | source)
XLA Modules:
  0.0 801.4 jit_solution(956062788617892617)
XLA Ops:
  6.5 1.5 fusion.82
  10.5 7.4 select_bitcast_fusion
  18.0 221.5 %all_to_all.35 = f32[4,128,2048]{2,0,1:T(4,128)} all-to-all(f32[4,128,2048]{2,0,1:T(4,128)} %bitcast.48), channel_id=1, replica_groups=mesh['row'=16,'col'=8] {'row','col'}, dimensions={1} | all-to-all | bytes 8388608 | tf_op jit(solution)/shard_map/all_to_all | solution.py:24
  239.5 5.3 all_to_all.29
  244.8 4.7 all-to-all-start.1
  249.5 0.0 all-reduce.5.cloned.1.call-start
  249.6 0.7 select_bitcast_fusion.4
  250.2 0.0 all-reduce.5.cloned.1.call-update
  250.3 0.7 fusion.81
  251.0 99.6 %all-to-all-done.1 = f32[8,64,2048]{2,1,0:T(8,128)} async-done(((f32[8,64,2048]{2,1,0:T(8,128)}), f32[8,64,2048]{2,1,0:T(8,128)}, u32[]{:S(2)}, u32[]{:S(2)}) %all-to-all-start.1) | async-done | bytes 4194336 | tf_op jit(solution)/shard_map/all_to_all | solution.py:25
  350.6 4.7 copy.8
  355.3 106.0 %all-reduce.7.cloned.1.call-done = (bf16[16384,128]{1,0:T(8,128)(2,1)}, bf16[16384,128]{1,0:T(8,128)(2,1)}, bf16[16384,128]{1,0:T(8,128)(2,1)}, bf16[16384,128]{1,0:T(8,128)(2,1)}) async-done(((bf16[16384,128]{1,0:T(8,128)(2,1)}, bf16[16384,128]{1,0:T(8,128)(2,1)}, bf16[16384,128]{1,0:T(8,128)(2,1)}, bf16[16384,128]{1,0:T(8,128)(2,1)}), (bf16[16384,128]{1,0:T(8,128)(2,1)}, bf16[16384,128]{1,0:T(8,128)(2,1)}, ...) | async-done | bytes 16777232 | tf_op jit(solution)/shard_map/psum | solution.py:11
  461.3 16.5 %fusion.56 = f32[64,128]{0,1:T(8,128)S(1)} fusion(f32[64,16384]{1,0:T(8,128)} %bitcast.49, bf16[16384,128]{1,0:T(8,128)(2,1)} %get-tuple-element.9, s32[]{:T(128)} %bitcast.3, s32[16384]{0:T(1024)S(1)} %iota_add_fusion), kind=kOutput, calls=%fused_computation.69 | convolution fusion | flops 1625292800 | bytes 8486916 | tf_op jit(solution)/shard_map/dot_general | solution.py:34
  477.8 55.1 %psum.85 = f32[64,128]{0,1:T(8,128)S(1)} all-reduce(f32[64,128]{0,1:T(8,128)S(1)} %fusion.56), channel_id=1, replica_groups=mesh['row'=16,'col'=8] {'row'}, use_global_device_ids=true, to_apply=%region_1.2 | all-reduce | flops 8192 | bytes 65536 | tf_op jit(solution)/shard_map/psum | solution.py:37
  532.8 18.0 %all-reduce.5.cloned.1.call-done = (bf16[128,128]{1,0:T(8,128)(2,1)}, bf16[128,128]{1,0:T(8,128)(2,1)}, bf16[128,128]{1,0:T(8,128)(2,1)}, bf16[128,128]{1,0:T(8,128)(2,1)}) async-done(((bf16[128,128]{1,0:T(8,128)(2,1)}, bf16[128,128]{1,0:T(8,128)(2,1)}, bf16[128,128]{1,0:T(8,128)(2,1)}, bf16[128,128]{1,0:T(8,128)(2,1)}), (bf16[128,128]{1,0:T(8,128)(2,1)}, bf16[128,128]{1,0:T(8,128)(2,1)}, ...) | async-done | bytes 131088 | tf_op jit(solution)/shard_map/psum | solution.py:11
  550.8 1.0 fusion.83
  551.8 13.2 %convolution_subtract_fusion.3 = f32[64,16384]{1,0:T(8,128)S(1)} fusion(f32[64,16384]{1,0:T(8,128)} %bitcast.50, f32[64,128]{1,0:T(8,128)S(1)} %fusion.83, bf16[16384,128]{1,0:T(8,128)(2,1)} %get-tuple-element.9, s32[]{:T(128)} %bitcast.3, s32[16384]{0:T(1024)S(1)} %iota_add_fusion), kind=kOutput, calls=%fused_computation.3 | convolution fusion | flops 1626341376 | bytes 12681220 | tf_op jit(solution)/shard_map/dot_general | solution.py:44
  565.0 2.0 copy-done.9
  567.0 7.5 fusion.13
  574.5 53.1 %psum.88 = f32[64,128]{1,0:T(8,128)S(1)} all-reduce(f32[64,128]{1,0:T(8,128)S(1)} %fusion.13), channel_id=1, replica_groups=mesh['row'=16,'col'=8] {'row'}, use_global_device_ids=true, to_apply=%region_4.5 | all-reduce | flops 8192 | bytes 65536 | tf_op jit(solution)/shard_map/psum | solution.py:37
  627.7 0.2 fusion.84
  627.9 13.2 %convolution_subtract_fusion.2 = f32[64,16384]{1,0:T(8,128)S(1)} fusion(f32[64,16384]{1,0:T(8,128)} %copy-done.9, f32[64,128]{1,0:T(8,128)S(1)} %fusion.84, bf16[16384,128]{1,0:T(8,128)(2,1)} %get-tuple-element.10, s32[]{:T(128)} %bitcast.8, s32[16384]{0:T(1024)S(1)} %iota_add_fusion), kind=kOutput, calls=%fused_computation.2 | convolution fusion | flops 1626341376 | bytes 12681220 | tf_op jit(solution)/shard_map/dot_general | solution.py:44
  641.1 2.0 copy-done.10
  643.1 7.6 fusion.14
  650.7 53.2 %psum.91 = f32[64,128]{1,0:T(8,128)S(1)} all-reduce(f32[64,128]{1,0:T(8,128)S(1)} %fusion.14), channel_id=1, replica_groups=mesh['row'=16,'col'=8] {'row'}, use_global_device_ids=true, to_apply=%region_7.8 | all-reduce | flops 8192 | bytes 65536 | tf_op jit(solution)/shard_map/psum | solution.py:37
  703.9 0.2 fusion.85
  704.1 13.3 %convolution_subtract_fusion.1 = f32[64,16384]{1,0:T(8,128)S(1)} fusion(f32[64,16384]{1,0:T(8,128)} %copy-done.10, f32[64,128]{1,0:T(8,128)S(1)} %fusion.85, bf16[16384,128]{1,0:T(8,128)(2,1)} %get-tuple-element.11, s32[]{:T(128)} %bitcast.12, s32[16384]{0:T(1024)S(1)} %iota_add_fusion), kind=kOutput, calls=%fused_computation.1 | convolution fusion | flops 1626341376 | bytes 12681220 | tf_op jit(solution)/shard_map/dot_general | solution.py:44
  717.4 2.0 copy-done.8
  719.4 7.6 fusion.15
  727.0 52.9 %psum.94 = f32[64,128]{1,0:T(8,128)S(1)} all-reduce(f32[64,128]{1,0:T(8,128)S(1)} %fusion.15), channel_id=1, replica_groups=mesh['row'=16,'col'=8] {'row'}, use_global_device_ids=true, to_apply=%region_10.11 | all-reduce | flops 8192 | bytes 65536 | tf_op jit(solution)/shard_map/psum | solution.py:37
  779.9 0.2 fusion.86
  780.1 14.0 %convolution_subtract_fusion = f32[64,16384]{1,0:T(8,128)} fusion(f32[64,16384]{1,0:T(8,128)} %copy-done.8, f32[64,128]{1,0:T(8,128)S(1)} %fusion.86, bf16[16384,128]{1,0:T(8,128)(2,1)} %get-tuple-element.12, s32[]{:T(128)} %bitcast.16, s32[16384]{0:T(1024)S(1)} %iota_add_fusion), kind=kOutput, calls=%fused_computation | convolution fusion | flops 1626341376 | bytes 12681220 | tf_op jit(solution)/shard_map/dot_general | solution.py:44
  (22 shorter events, 0.1 us)
Async XLA Ops:
  6.5 454.8 %all-reduce.7.cloned.1.call-start = ((), (), s32[]{:S(2)}) async-start(), calls=%async_computation.3 | async-start | bytes 33554432 | tf_op jit(solution)/shard_map/psum | solution.py:11
  244.8 4.8 copy-start.3
  244.8 5.5 copy-start.4
  244.8 105.8 %all-to-all-start.1 = ((f32[8,64,2048]{2,1,0:T(8,128)}), f32[8,64,2048]{2,1,0:T(8,128)}, u32[]{:S(2)}, u32[]{:S(2)}) async-start(f32[8,64,2048]{2,1,0:T(8,128)} %all_to_all.29), calls=%async_computation.1 | async-start | bytes 8388608 | tf_op jit(solution)/shard_map/all_to_all | solution.py:25
  249.5 301.3 %all-reduce.5.cloned.1.call-start = ((), (), s32[]{:S(2)}) async-start(), calls=%async_computation.2 | async-start | bytes 262144 | tf_op jit(solution)/shard_map/psum | solution.py:11
  551.8 15.2 %copy-start.7 = (bf16[16384,128]{1,0:T(8,128)(2,1)S(1)}, bf16[16384,128]{1,0:T(8,128)(2,1)}, u32[]{:S(2)}) copy-start(bf16[16384,128]{1,0:T(8,128)(2,1)} %get-tuple-element.10) | copy-start | bytes 12582916
  565.0 2.0 copy-start.9
  567.0 60.7 %copy-start.2 = (bf16[128,128]{1,0:T(8,128)(2,1)S(1)}, bf16[128,128]{1,0:T(8,128)(2,1)}, u32[]{:S(2)}) copy-start(bf16[128,128]{1,0:T(8,128)(2,1)} %get-tuple-element.6) | copy-start | bytes 98308
  627.9 15.2 %copy-start.6 = (bf16[16384,128]{1,0:T(8,128)(2,1)S(1)}, bf16[16384,128]{1,0:T(8,128)(2,1)}, u32[]{:S(2)}) copy-start(bf16[16384,128]{1,0:T(8,128)(2,1)} %get-tuple-element.11) | copy-start | bytes 12582916
  641.1 2.0 copy-start.10
  643.1 60.8 %copy-start.1 = (bf16[128,128]{1,0:T(8,128)(2,1)S(1)}, bf16[128,128]{1,0:T(8,128)(2,1)}, u32[]{:S(2)}) copy-start(bf16[128,128]{1,0:T(8,128)(2,1)} %get-tuple-element.7) | copy-start | bytes 98308
  704.1 15.3 %copy-start.5 = (bf16[16384,128]{1,0:T(8,128)(2,1)S(1)}, bf16[16384,128]{1,0:T(8,128)(2,1)}, u32[]{:S(2)}) copy-start(bf16[16384,128]{1,0:T(8,128)(2,1)} %get-tuple-element.12) | copy-start | bytes 12582916
  717.4 2.0 copy-start.8
  719.4 60.6 %copy-start = (bf16[128,128]{1,0:T(8,128)(2,1)S(1)}, bf16[128,128]{1,0:T(8,128)(2,1)}, u32[]{:S(2)}) copy-start(bf16[128,128]{1,0:T(8,128)(2,1)} %get-tuple-element.8) | copy-start | bytes 98308
Sparse Core Ops, SparseCore 0:
  18.1 443.1 all-reduce.6
  464.0 86.7 all-reduce.4
where the time goes:
time: 812 us; the launch traced here: 801 us
  blocking collectives  436 us (54%)
  waiting for transfers between devices  224 us (28%)
  matrix products  94.4 us (12%)
  local copies, waits for them, and re-layouts  18.1 us (2%)
  between operations  16.5 us (2%)
    all_to_all x1, blocking collectives, local(): lax.all_to_all(eigvecs, ('row', 'col'), split_axis=1, concat_axis=0, tile...  222 us
    psum x4, blocking collectives, local(): projection = lax.psum(partial_sum, 'row')  214 us
    psum x2, waiting for transfers between devices, from_root(): return lax.psum(jnp.where(mine, value, jnp.zeros_like(value)), axis)  124 us
    all_to_all x1, waiting for transfers between devices, local(): lax.all_to_all(spread, 'col', split_axis=0, concat_axis=1, tiled=True)  99.6 us
    dot_general x4, matrix products, local(): jnp.dot(coeffs, reflector.T, precision=highest, preferred_element_type=jn...  53.6 us
    dot_general x4, matrix products, local(): jnp.dot(field, reflector, precision=highest, preferred_element_type=jnp.f...  39.2 us
  transfers between devices with their start and end apart: 3, of which 3 were waited for; matrix products, arithmetic and copies ran while one was open for 3% of the time, Pallas kernels for 0%

commit v1 on v0

v1 whole, which is shorter than its diff:
```python
import math

import jax
import jax.numpy as jnp
from jax import lax
from jax.experimental import pallas as pl
from jax.experimental.pallas import tpu as pltpu
from jax.sharding import PartitionSpec as P

PANELS = 4
NB = 128
K = 512
DEVS = 128
COLS = 8
OWN = 4
SUB = 2048
STEP = 512
STEPS = SUB // STEP
TILES = SUB // 128
WIDE = K // COLS
PACK = 24
PAIRS = [(q, p) for q in range(PANELS) for p in range(q)]
ALL = ("row", "col")
HIGHEST = lax.Precision.HIGHEST

MU = 2.0**18 / 6.0
LOG_SCALE = 32767.0 / math.log1p(2.0**18)


def encode_log(x):
    level = jnp.log(1.0 + MU * jnp.abs(x)) * LOG_SCALE + 0.5
    level = jnp.minimum(level, 32767.0).astype(jnp.int32)
    return jnp.where(x < 0.0, -level, level).astype(jnp.int16)


def decode_log(code):
    level = code.astype(jnp.int32).astype(jnp.float32)
    size = (jnp.exp(jnp.abs(level) * (1.0 / LOG_SCALE)) - 1.0) * (1.0 / MU)
    return jnp.where(level < 0.0, -size, size)


def dot32(a, b, dims=((1,), (0,)), precision=None):
    return lax.dot_general(
        a, b, (dims, ((), ())), precision=precision, preferred_element_type=jnp.float32
    )


def split(x):
    high = x.astype(jnp.bfloat16)
    return high, (x - high.astype(jnp.float32)).astype(jnp.bfloat16)


def encode_kernel(e_ref, out_ref):
    for d in range(out_ref.shape[0]):
        x = e_ref[:, d * SUB : (d + 1) * SUB]
        tall = jnp.concatenate([x[:, t * 128 : (t + 1) * 128] for t in range(TILES)], axis=0)
        out_ref[d] = encode_log(tall)


def encode(eigvecs):
    group = 8
    return pl.pallas_call(
        encode_kernel,
        out_shape=jax.ShapeDtypeStruct((DEVS, OWN * TILES, 128), jnp.int16),
        grid=(DEVS // group,),
        in_specs=[pl.BlockSpec((OWN, group * SUB), lambda g: (0, g))],
        out_specs=pl.BlockSpec((group, OWN * TILES, 128), lambda g: (g, 0, 0)),
        name="encode",
    )(eigvecs)


def decode_kernel(code_ref, high_ref, low_ref):
    def body(g, carry):
        x = decode_log(code_ref[pl.ds(g * 4, 4)])
        rows = pl.ds(pl.multiple_of(g * 16, 16), 16)
        for t in range(TILES):
            tile = jnp.concatenate([x[i, t * OWN : (t + 1) * OWN] for i in range(4)], axis=0)
            high, low = split(tile)
            high_ref[rows, t * 128 : (t + 1) * 128] = high
            low_ref[rows, t * 128 : (t + 1) * 128] = low
        return carry

    lax.fori_loop(0, code_ref.shape[0] // 4, body, 0)


def decode(codes):
    group = 32
    out = jax.ShapeDtypeStruct((K, SUB), jnp.bfloat16)
    return pl.pallas_call(
        decode_kernel,
        out_shape=(out, out),
        grid=(DEVS // group,),
        in_specs=[pl.BlockSpec((group, OWN * TILES, 128), lambda g: (g, 0, 0))],
        out_specs=(pl.BlockSpec((group * OWN, SUB), lambda g: (g, 0)),) * 2,
        name="decode",
    )(codes)


def project_kernel(s_ref, high_ref, low_ref, v0, v1, v2, v3, pack_ref, refl_ref, proj, gram):
    step = pl.program_id(0)

    @pl.when(step == 0)
    def _():
        proj[...] = jnp.zeros_like(proj)
        gram[...] = jnp.zeros_like(gram)

    row_ids = s_ref[8] + step * STEP + lax.broadcasted_iota(jnp.int32, (STEP, NB), 0)
    base = row_ids - lax.broadcasted_iota(jnp.int32, (STEP, NB), 1)
    for p, ref in enumerate((v0, v1, v2, v3)):
        below = base - s_ref[4 + p]
        unit = jnp.where(below == 0, jnp.float32(1.0), jnp.float32(0.0))
        block = jnp.where(below > 0, ref[0].astype(jnp.float32), unit)
        refl_ref[:, p * NB : (p + 1) * NB] = block.astype(jnp.bfloat16)
    v = refl_ref[...]
    proj[...] += dot32(high_ref[...], v) + dot32(low_ref[...], v)
    gram[...] += dot32(v, v, ((0,), (0,)))

    @pl.when(step == STEPS - 1)
    def _():
        for p in range(PANELS):
            pack_ref[p * 32 : (p + 1) * 32, 0:16, :] = proj[:, p * NB : (p + 1) * NB].reshape(32, 16, NB)
        for b, (q, p) in enumerate(PAIRS):
            block = gram[q * NB : (q + 1) * NB, p * NB : (p + 1) * NB]
            pack_ref[b * 16 : (b + 1) * 16, 16:24, :] = block.reshape(16, 8, NB)
        for b in range(len(PAIRS), 8):
            pack_ref[b * 16 : (b + 1) * 16, 16:24, :] = jnp.zeros((16, 8, NB), jnp.float32)


def slot_spec(p, rows, index):
    return pl.BlockSpec((1, rows, NB), lambda k, s: (s[p], index(k), 0))


def project(scalars, high, low, slots):
    return pl.pallas_call(
        project_kernel,
        out_shape=(
            jax.ShapeDtypeStruct((DEVS, PACK, NB), jnp.float32),
            jax.ShapeDtypeStruct((SUB, PANELS * NB), jnp.bfloat16),
        ),
        grid_spec=pltpu.PrefetchScalarGridSpec(
            num_scalar_prefetch=1,
            grid=(STEPS,),
            in_specs=[pl.BlockSpec((K, STEP), lambda k, s: (0, k))] * 2
            + [slot_spec(p, STEP, lambda k: k) for p in range(PANELS)],
            out_specs=(
                pl.BlockSpec((DEVS, PACK, NB), lambda k, s: (0, 0, 0)),
                pl.BlockSpec((STEP, PANELS * NB), lambda k, s: (k, 0)),
            ),
            scratch_shapes=[
                pltpu.VMEM((K, PANELS * NB), jnp.float32),
                pltpu.VMEM((PANELS * NB, PANELS * NB), jnp.float32),
            ],
        ),
        name="project",
    )(scalars, high, low, slots, slots, slots, slots)


def total_kernel(in_ref, out_ref):
    total = jnp.sum(in_ref[...], axis=0)
    out_ref[...] = jnp.broadcast_to(total[None], out_ref.shape)


def total(parts):
    return pl.pallas_call(
        total_kernel,
        out_shape=jax.ShapeDtypeStruct(parts.shape, parts.dtype),
        name="total",
    )(parts)


def update_kernel(s_ref, sums_ref, t0, t1, t2, t3, high_ref, low_ref, refl_ref, out_ref, c_high, c_low, coef):
    step = pl.program_id(0)

    @pl.when(step == 0)
    def _():
        triangles = (t0, t1, t2, t3)
        gram = {}
        for b, pair in enumerate(PAIRS):
            gram[pair] = sums_ref[b * 16 : (b + 1) * 16, 16:24, :].reshape(NB, NB)
        for p in reversed(range(PANELS)):
            rest = sums_ref[p * 32 : (p + 1) * 32, 0:16, :].reshape(K, NB)
            for q in range(p + 1, PANELS):
                rest -= dot32(coef[:, q * NB : (q + 1) * NB], gram[(q, p)], precision=HIGHEST)
            triangle = triangles[p][0].astype(jnp.float32)
            coef[:, p * NB : (p + 1) * NB] = dot32(rest, triangle, ((1,), (1,)), HIGHEST)
        high, low = split(coef[...])
        c_high[...] = high
        c_low[...] = low

    v = refl_ref[...]
    change = dot32(c_high[...], v, ((1,), (1,))) + dot32(c_low[...], v, ((1,), (1,)))
    back = high_ref[...].astype(jnp.float32) + (low_ref[...].astype(jnp.float32) - change)
    for c in range(COLS):
        block = back[c * WIDE : (c + 1) * WIDE]
        most = jnp.max(jnp.abs(block), axis=(0, 1), keepdims=True)
        power = jnp.ceil(jnp.log(jnp.maximum(most, 1e-30)) * (1.0 / math.log(2.0)) + 0.001)
        scale = jnp.exp(power * -math.log(2.0))
        level = (jnp.sqrt(jnp.abs(block) * scale) * 32767.0 + 0.5).astype(jnp.int32)
        code = jnp.where(block < 0.0, -level, level).astype(jnp.int16)
        for t in range(STEP // 128):
            at = pl.multiple_of((step * (STEP // 128) + t) * WIDE, WIDE)
            out_ref[c, pl.ds(at, WIDE), :] = code[:, t * 128 : (t + 1) * 128]
        at = pl.multiple_of(TILES * WIDE + step * 8, 8)
        out_ref[c, pl.ds(at, 8), :] = jnp.broadcast_to(power, (8, 128)).astype(jnp.int32).astype(jnp.int16)


def update(scalars, sums, slots, high, low, refl):
    rows = TILES * WIDE + 8 * STEPS
    return pl.pallas_call(
        update_kernel,
        out_shape=jax.ShapeDtypeStruct((COLS, rows, 128), jnp.int16),
        grid_spec=pltpu.PrefetchScalarGridSpec(
            num_scalar_prefetch=1,
            grid=(STEPS,),
            in_specs=[pl.BlockSpec((DEVS, PACK, NB), lambda k, s: (0, 0, 0))]
            + [slot_spec(p, NB, lambda k: SUB // NB) for p in range(PANELS)]
            + [pl.BlockSpec((K, STEP), lambda k, s: (0, k))] * 2
            + [pl.BlockSpec((STEP, PANELS * NB), lambda k, s: (k, 0))],
            out_specs=pl.BlockSpec((COLS, rows, 128), lambda k, s: (0, 0, 0)),
            scratch_shapes=[
                pltpu.VMEM((K, PANELS * NB), jnp.bfloat16),
                pltpu.VMEM((K, PANELS * NB), jnp.bfloat16),
                pltpu.VMEM((K, PANELS * NB), jnp.float32),
            ],
        ),
        name="update",
    )(scalars, sums, slots, slots, slots, slots, high, low, refl)


def finish_kernel(code_ref, out_ref):
    for k in range(STEPS):
        at = TILES * WIDE + 8 * k
        power = code_ref[0, at : at + 8, :].astype(jnp.int32).astype(jnp.float32)
        unit = jnp.exp(power * math.log(2.0)) * (1.0 / 32767.0**2)
        unit = jnp.concatenate([unit] * (WIDE // 8), axis=0)
        for t in range(k * (STEP // 128), (k + 1) * (STEP // 128)):
            level = code_ref[0, t * WIDE : (t + 1) * WIDE, :].astype(jnp.int32).astype(jnp.float32)
            out_ref[:, t * 128 : (t + 1) * 128] = level * jnp.abs(level) * unit


def finish(codes):
    rows = codes.shape[1]
    return pl.pallas_call(
        finish_kernel,
        out_shape=jax.ShapeDtypeStruct((WIDE, COLS * SUB), jnp.float32),
        grid=(COLS,),
        in_specs=[pl.BlockSpec((1, rows, 128), lambda g: (g, 0, 0))],
        out_specs=pl.BlockSpec((WIDE, SUB), lambda g: (0, g)),
        name="finish",
    )(codes)


def exchange(x, axis):
    return lax.all_to_all(x, axis, split_axis=0, concat_axis=0, tiled=True)


def local(eigvecs, panels, tfactors, owners, offsets):
    device = lax.axis_index("row") * COLS + lax.axis_index("col")
    scalars = jnp.concatenate([owners, offsets, jnp.full((1,), device * SUB, jnp.int32)])
    codes = exchange(encode(eigvecs), ALL)
    triangles = jnp.broadcast_to(tfactors, (COLS, NB, NB))
    stored = jnp.concatenate([panels.reshape(COLS, SUB, NB), triangles], axis=1)
    slots = exchange(stored, "col")
    high, low = decode(codes)
    pack, refl = project(scalars, high, low, slots)
    sums = exchange(total(exchange(pack, ALL)), ALL)
    out = update(scalars, sums, slots, high, low, refl)
    return finish(exchange(out, "col"))


def solution(mesh):
    in_specs = (P(ALL, None), P("col", "row", None), P("col", None, None), P(), P())
    out_specs = P("col", "row")
    return jax.shard_map(local, mesh=mesh, in_specs=in_specs, out_specs=out_specs, check_vma=False)
```

time: 812 us -> 235 us (0.29); the launches traced: 801 us -> 234 us
  blocking collectives: 436 us -> 93.5 us
  waiting for transfers between devices: 224 us -> 69.9 us
  matrix products: 94.4 us -> 0 us
  Pallas kernels: 0 us -> 47.9 us
  local copies, waits for them, and re-layouts: 18.1 us -> 1.37 us
  between operations: 16.5 us -> 0.06 us
  starting transfers between devices: 4.77 us -> 15.7 us
    psum x4 -> x0, blocking collectives: 214 us -> none  [local(): projection = lax.psum(partial_sum, 'row')]
    all_to_all x1 -> x3, blocking collectives: 222 us -> 93.5 us  [exchange(): return lax.all_to_all(x, axis, split_axis=0, concat_axis=0, tiled=True)]
    psum x2 -> x0, waiting for transfers between devices: 124 us -> none  [from_root(): return lax.psum(jnp.where(mine, value, jnp.zeros_like(value)), axis)]
    dot_general x12 -> x0, matrix products: 94.4 us -> none  [the longest x4 53.6 us: local(): jnp.dot(coeffs, reflector.T, precision=highest, preferred_element_type=jn...]
    pallas_call x0 -> x6, Pallas kernels: none -> 47.9 us  [the longest x1 14.1 us: update(): pl.pallas_call(update_kernel, out_shape=jax.ShapeDtypeStruct((COLS, rows,...]
    all_to_all x1 -> x2, waiting for transfers between devices: 99.6 us -> 69.9 us  [exchange(): return lax.all_to_all(x, axis, split_axis=0, concat_axis=0, tiled=True)]
    all_to_all x1 -> x2, starting transfers between devices: 4.72 us -> 15.7 us  [exchange(): return lax.all_to_all(x, axis, split_axis=0, concat_axis=0, tiled=True)]
    all_to_all x2 -> x0, local copies, waits for them, and re-layouts: 9.97 us -> none  [local(): lax.all_to_all(spread, 'col', split_axis=0, concat_axis=1, tiled=True)]
  transfers between devices with their start and end apart: 3 -> 2, of which waited for: 3 -> 2; matrix products, arithmetic and copies ran while one was open for 3% -> 2% of each run, Pallas kernels for 0% -> 2%
where the time goes in v1:
time: 235 us; the launch traced here: 234 us
  blocking collectives  93.5 us (40%)
  waiting for transfers between devices  69.9 us (30%)
  Pallas kernels  47.9 us (20%)
  starting transfers between devices  15.7 us (7%)
  other arithmetic  5.25 us (2%)
    all_to_all x3, blocking collectives, exchange(): return lax.all_to_all(x, axis, split_axis=0, concat_axis=0, tiled=True)  93.5 us
    all_to_all x2, waiting for transfers between devices, exchange(): return lax.all_to_all(x, axis, split_axis=0, concat_axis=0, tiled=True)  69.9 us
    all_to_all x2, starting transfers between devices, exchange(): return lax.all_to_all(x, axis, split_axis=0, concat_axis=0, tiled=True)  15.7 us
    pallas_call x1, Pallas kernels, update(): pl.pallas_call(update_kernel, out_shape=jax.ShapeDtypeStruct((COLS, rows,...  14.1 us
    pallas_call x1, Pallas kernels, encode(): pl.pallas_call(encode_kernel, out_shape=jax.ShapeDtypeStruct((DEVS, OWN *...  10.5 us
    pallas_call x1, Pallas kernels, project(): pl.pallas_call(project_kernel, out_shape=(jax.ShapeDtypeStruct((DEVS, PAC...  8.82 us
    pallas_call x1, Pallas kernels, finish(): pl.pallas_call(finish_kernel, out_shape=jax.ShapeDtypeStruct((WIDE, COLS...  6.2 us
    pallas_call x1, Pallas kernels, decode(): pl.pallas_call(decode_kernel, out_shape=(out, out), grid=(DEVS // group,)...  5.44 us
  transfers between devices with their start and end apart: 2, of which 2 were waited for; matrix products, arithmetic and copies ran while one was open for 2% of the time, Pallas kernels for 2%

profile of v1, /device:TPU:0, one launch (start us, length us, event | category | flops | bytes accessed | tf_op | source)
XLA Modules:
  0.0 233.6 jit_solution(939463505855318439)
XLA Ops:
  0.0 0.0 copy-start.1
  0.0 10.5 %encode.1 = s16[128,64,128]{2,1,0:T(8,128)(2,1)} custom-call(f32[4,262144]{1,0:T(4,128)} %e_ref.1), custom_call_target="tpu_custom_call" | custom-call | tf_op jit(solution)/shard_map/encode/pallas_call | solution.py:62
  10.5 11.2 %all-to-all-start = ((s16[128,64,128]{2,1,0:T(8,128)(2,1)}), s16[128,64,128]{2,1,0:T(8,128)(2,1)S(1)}, u32[]{:S(2)}, u32[]{:S(2)}) async-start(s16[128,64,128]{2,1,0:T(8,128)(2,1)} %encode.1), calls=%async_computation | async-start | bytes 4194304 | tf_op jit(solution)/shard_map/all_to_all | solution.py:254
  21.7 0.0 copy-done.1
  21.7 4.6 %pad_maximum_fusion = bf16[8,2176,128]{2,1,0:T(8,128)(2,1)} fusion(bf16[8,128,128]{2,1,0:T(8,128)(2,1)S(1)} %broadcast_in_dim.12, bf16[8,2048,128]{2,1,0:T(8,128)(2,1)} %bitcast.3), kind=kLoop, calls=%fused_computation | loop fusion | flops 8912896 | bytes 8912896 | tf_op jit(solution)/shard_map/concatenate | solution.py:262
  26.4 0.0 copy-start.2
  26.4 0.0 copy-start.3
  26.4 24.0 %all-to-all-done.code_ref = s16[128,64,128]{2,1,0:T(8,128)(2,1)S(1)} async-done(((s16[128,64,128]{2,1,0:T(8,128)(2,1)}), s16[128,64,128]{2,1,0:T(8,128)(2,1)S(1)}, u32[]{:S(2)}, u32[]{:S(2)}) %all-to-all-start) | async-done | bytes 2097184 | tf_op jit(solution)/shard_map/all_to_all | solution.py:254
  50.3 0.0 copy-start
  50.3 1.3 copy-done
  51.7 4.6 %all-to-all-start.1 = ((bf16[8,2176,128]{2,1,0:T(8,128)(2,1)}), bf16[8,2176,128]{2,1,0:T(8,128)(2,1)}, u32[]{:S(2)}, u32[]{:S(2)}) async-start(bf16[8,2176,128]{2,1,0:T(8,128)(2,1)} %pad_maximum_fusion), calls=%async_computation.1 | async-start | bytes 8912896 | tf_op jit(solution)/shard_map/all_to_all | solution.py:254
  56.2 0.0 copy-done.2
  56.3 0.0 copy-done.3
  56.3 0.6 pad_add_fusion.s_ref
  56.9 5.4 %decode.1 = (bf16[512,2048]{1,0:T(8,128)(2,1)}, bf16[512,2048]{1,0:T(8,128)(2,1)}) custom-call(s16[128,64,128]{2,1,0:T(8,128)(2,1)} %copy-done), custom_call_target="tpu_custom_call" | custom-call | tf_op jit(solution)/shard_map/decode/pallas_call | solution.py:89
  62.3 45.9 %all-to-all-done.1.v0.v1.v2.v3.t0.t1.t2.t3 = bf16[8,2176,128]{2,1,0:T(8,128)(2,1)} async-done(((bf16[8,2176,128]{2,1,0:T(8,128)(2,1)}), bf16[8,2176,128]{2,1,0:T(8,128)(2,1)}, u32[]{:S(2)}, u32[]{:S(2)}) %all-to-all-start.1) | async-done | bytes 4456480 | tf_op jit(solution)/shard_map/all_to_all | solution.py:254
  108.2 8.8 %project.1 = (f32[128,24,128]{2,1,0:T(8,128)}, bf16[2048,512]{1,0:T(8,128)(2,1)}) custom-call(s32[9]{0:T(128)} %pad_add_fusion.s_ref, bf16[512,2048]{1,0:T(8,128)(2,1)} %get-tuple-element.9.high_ref, bf16[512,2048]{1,0:T(8,128)(2,1)} %get-tuple-element.10.low_ref, bf16[8,2176,128]{2,1,0:T(8,128)(2,1)} %all-to-all-done.1.v0.v1.v2.v3.t0.t1.t2.t3, ...), custom_call_target="tpu_custom_call" | custom-call | tf_op jit(solution)/shard_map/project/pallas_call | solution.py:134
  117.0 30.0 %all_to_all.25.in_ref = f32[128,24,128]{2,1,0:T(8,128)} all-to-all(f32[128,24,128]{2,1,0:T(8,128)} %get-tuple-element.11), channel_id=1, replica_groups=mesh['row'=16,'col'=8] {'row','col'}, dimensions={0} | all-to-all | bytes 3145728 | tf_op jit(solution)/shard_map/all_to_all | solution.py:254
  147.0 2.8 %total.1 = f32[128,24,128]{2,1,0:T(8,128)} custom-call(f32[128,24,128]{2,1,0:T(8,128)} %all_to_all.25.in_ref), custom_call_target="tpu_custom_call" | custom-call | tf_op jit(solution)/shard_map/total/pallas_call | solution.py:164
  149.8 29.3 %all_to_all.26.sums_ref = f32[128,24,128]{2,1,0:T(8,128)} all-to-all(f32[128,24,128]{2,1,0:T(8,128)} %total.1), channel_id=1, replica_groups=mesh['row'=16,'col'=8] {'row','col'}, dimensions={0} | all-to-all | bytes 3145728 | tf_op jit(solution)/shard_map/all_to_all | solution.py:254
  179.2 14.1 %update.1 = s16[8,1056,128]{2,1,0:T(8,128)(2,1)} custom-call(s32[9]{0:T(128)} %pad_add_fusion.s_ref, f32[128,24,128]{2,1,0:T(8,128)} %all_to_all.26.sums_ref, bf16[8,2176,128]{2,1,0:T(8,128)(2,1)} %all-to-all-done.1.v0.v1.v2.v3.t0.t1.t2.t3, bf16[8,2176,128]{2,1,0:T(8,128)(2,1)} %all-to-all-done.1.v0.v1.v2.v3.t0.t1.t2.t3, ...), custom_call_target="tpu_custom_call" | custom-call | tf_op jit(solution)/shard_map/update/pallas_call | solution.py:209
  193.3 34.1 %all_to_all.27.code_ref = s16[8,1056,128]{2,1,0:T(8,128)(2,1)} all-to-all(s16[8,1056,128]{2,1,0:T(8,128)(2,1)} %update.1), channel_id=1, replica_groups=mesh['row'=16,'col'=8] {'col'}, dimensions={0} | all-to-all | bytes 4325376 | tf_op jit(solution)/shard_map/all_to_all | solution.py:254
  227.4 6.2 %finish.1 = f32[64,16384]{1,0:T(8,128)} custom-call(s16[8,1056,128]{2,1,0:T(8,128)(2,1)} %all_to_all.27.code_ref), custom_call_target="tpu_custom_call" | custom-call | tf_op jit(solution)/shard_map/finish/pallas_call | solution.py:243
  (1 shorter events, 0.0 us)
Async XLA Ops:
  0.0 21.7 %copy-start.1 = (bf16[1,128,128]{2,1,0:T(8,128)(2,1)S(1)}, bf16[1,128,128]{2,1,0:T(8,128)(2,1)}, u32[]{:S(2)}) copy-start(bf16[1,128,128]{2,1,0:T(8,128)(2,1)} %param.7) | copy-start | bytes 98308
  10.5 39.9 %all-to-all-start = ((s16[128,64,128]{2,1,0:T(8,128)(2,1)}), s16[128,64,128]{2,1,0:T(8,128)(2,1)S(1)}, u32[]{:S(2)}, u32[]{:S(2)}) async-start(s16[128,64,128]{2,1,0:T(8,128)(2,1)} %encode.1), calls=%async_computation | async-start | bytes 4194304 | tf_op jit(solution)/shard_map/all_to_all | solution.py:254
  26.4 29.9 %copy-start.2 = (s32[4]{0:T(128)S(1)}, s32[4]{0:T(128)}, u32[]{:S(2)}) copy-start(s32[4]{0:T(128)} %param.9) | copy-start | bytes 52
  26.4 29.9 %copy-start.3 = (s32[4]{0:T(128)S(1)}, s32[4]{0:T(128)}, u32[]{:S(2)}) copy-start(s32[4]{0:T(128)} %param.8) | copy-start | bytes 52
  50.3 1.3 copy-start
  51.7 56.5 %all-to-all-start.1 = ((bf16[8,2176,128]{2,1,0:T(8,128)(2,1)}), bf16[8,2176,128]{2,1,0:T(8,128)(2,1)}, u32[]{:S(2)}, u32[]{:S(2)}) async-start(bf16[8,2176,128]{2,1,0:T(8,128)(2,1)} %pad_maximum_fusion), calls=%async_computation.1 | async-start | bytes 8912896 | tf_op jit(solution)/shard_map/all_to_all | solution.py:254

commit v2 on v1

v2 whole, which is shorter than its diff:
```python
import math

import jax
import jax.numpy as jnp
from jax import lax
from jax.experimental import pallas as pl
from jax.experimental.pallas import tpu as pltpu
from jax.sharding import PartitionSpec as P

PANELS = 4
NB = 128
K = 512
DEVS = 128
COLS = 8
OWN = 4
SUB = 2048
STEP = 512
STEPS = SUB // STEP
TILES = SUB // 128
WIDE = K // COLS
PACK = 24
PAIRS = [(q, p) for q in range(PANELS) for p in range(q)]
ALL = ("row", "col")

MU = 2.0**18 / 6.0
LOG_SCALE = 32767.0 / math.log1p(2.0**18)
LN2 = math.log(2.0)
T_STEPS = 258.0
T_ZERO = 50.0 * T_STEPS
ROWS = OWN * TILES + 8
GROUP = 32


def signed(level, like):
    return jnp.where(like < 0.0, -level, level)


def to_float(code):
    return code.astype(jnp.int32).astype(jnp.float32)


def encode_log(x):
    level = jnp.log(1.0 + MU * jnp.abs(x)) * LOG_SCALE + 0.5
    return signed(jnp.minimum(level, 32767.0).astype(jnp.int32), x).astype(jnp.int16)


def decode_log(code):
    level = to_float(code)
    return signed((jnp.exp(jnp.abs(level) * (1.0 / LOG_SCALE)) - 1.0) * (1.0 / MU), level)


def encode_triangle(x):
    level = jnp.log(jnp.maximum(jnp.abs(x), 1e-30)) * (T_STEPS / LN2) + (T_ZERO + 0.5)
    level = jnp.clip(level, 0.0, 32767.0).astype(jnp.int32)
    return signed(level, x).astype(jnp.int16)


def decode_triangle(code):
    level = to_float(code)
    size = jnp.exp((jnp.abs(level) - T_ZERO) * (LN2 / T_STEPS))
    return jnp.where(level == 0.0, 0.0, signed(size, level)).astype(jnp.bfloat16)


def power_of(most):
    return jnp.ceil(jnp.log(jnp.maximum(most, 1e-30)) * (8.0 / LN2) + 0.01)


def levels(x, power):
    size = jnp.sqrt(jnp.abs(x) * jnp.exp(power * (-LN2 / 8.0))) * 32767.0 + 0.5
    return signed(size.astype(jnp.int32), x)


def unit_of(power):
    return jnp.exp(power * (LN2 / 8.0)) * (1.0 / 32767.0**2)


def dot32(a, b, dims=((1,), (0,))):
    return lax.dot_general(a, b, (dims, ((), ())), preferred_element_type=jnp.float32)


def split(x):
    high = x.astype(jnp.bfloat16)
    return high, (x - high.astype(jnp.float32)).astype(jnp.bfloat16)


def encode_kernel(e_ref, t_ref, out_ref):
    triangle = encode_triangle(t_ref[...].astype(jnp.float32))
    for d in range(out_ref.shape[0]):
        x = e_ref[:, d * SUB : (d + 1) * SUB]
        tall = jnp.concatenate([x[:, t * 128 : (t + 1) * 128] for t in range(TILES)], axis=0)
        out_ref[d, 0 : OWN * TILES, :] = encode_log(tall)
        out_ref[d, OWN * TILES : ROWS, :] = triangle


def encode(eigvecs, triangle):
    group = 8
    return pl.pallas_call(
        encode_kernel,
        out_shape=jax.ShapeDtypeStruct((DEVS, ROWS, 128), jnp.int16),
        grid=(DEVS // group,),
        in_specs=[
            pl.BlockSpec((OWN, group * SUB), lambda g: (0, g)),
            pl.BlockSpec((8, NB), lambda g: (0, 0)),
        ],
        out_specs=pl.BlockSpec((group, ROWS, 128), lambda g: (g, 0, 0)),
        name="encode",
    )(eigvecs, triangle)


def gram_kernel(s_ref, v0, v1, v2, v3, gram_ref, refl_ref, gram):
    step = pl.program_id(0)

    @pl.when(step == 0)
    def _():
        gram[...] = jnp.zeros_like(gram)

    row_ids = s_ref[8] + step * STEP + lax.broadcasted_iota(jnp.int32, (STEP, NB), 0)
    base = row_ids - lax.broadcasted_iota(jnp.int32, (STEP, NB), 1)
    for p, ref in enumerate((v0, v1, v2, v3)):
        below = base - s_ref[4 + p]
        unit = jnp.where(below == 0, jnp.float32(1.0), jnp.float32(0.0))
        block = jnp.where(below > 0, ref[0].astype(jnp.float32), unit)
        refl_ref[:, p * NB : (p + 1) * NB] = block.astype(jnp.bfloat16)
    v = refl_ref[...]
    gram[...] += dot32(v, v, ((0,), (0,)))

    @pl.when(step == STEPS - 1)
    def _():
        blocks = [gram[q * NB : (q + 1) * NB, p * NB : (p + 1) * NB] for q, p in PAIRS]
        most = jnp.zeros((1, 1), jnp.float32)
        for block in blocks:
            most = jnp.maximum(most, jnp.max(jnp.abs(block), axis=(0, 1), keepdims=True))
        power = power_of(most)
        rows = [levels(block, power).astype(jnp.float32) for block in blocks]
        rows += [jnp.zeros((NB, NB), jnp.float32), jnp.broadcast_to(power, (NB, NB))]
        gram_ref[...] = jnp.swapaxes(jnp.stack(rows), 0, 1)


def gram_of(scalars, slots):
    slot = [pl.BlockSpec((1, STEP, NB), lambda k, s, p=p: (s[p], k, 0)) for p in range(PANELS)]
    return pl.pallas_call(
        gram_kernel,
        out_shape=(
            jax.ShapeDtypeStruct((DEVS, 8, NB), jnp.float32),
            jax.ShapeDtypeStruct((SUB, PANELS * NB), jnp.bfloat16),
        ),
        grid_spec=pltpu.PrefetchScalarGridSpec(
            num_scalar_prefetch=1,
            grid=(STEPS,),
            in_specs=slot,
            out_specs=(
                pl.BlockSpec((DEVS, 8, NB), lambda k, s: (0, 0, 0)),
                pl.BlockSpec((STEP, PANELS * NB), lambda k, s: (k, 0)),
            ),
            scratch_shapes=[pltpu.VMEM((PANELS * NB, PANELS * NB), jnp.float32)],
        ),
        name="gram",
    )(scalars, slots, slots, slots, slots)


def project_kernel(code_ref, refl_ref, gram_ref, pack_ref, high_ref, low_ref):
    group = pl.program_id(0)

    def body(g, carry):
        x = decode_log(code_ref[pl.ds(g * 4, 4), 0 : OWN * TILES, :])
        rows = pl.ds(pl.multiple_of(g * 16, 16), 16)
        for t in range(TILES):
            tile = jnp.concatenate([x[i, t * OWN : (t + 1) * OWN] for i in range(4)], axis=0)
            high, low = split(tile)
            high_ref[rows, t * 128 : (t + 1) * 128] = high
            low_ref[rows, t * 128 : (t + 1) * 128] = low
        return carry

    lax.fori_loop(0, GROUP // 4, body, 0)
    v = refl_ref[...]
    part = dot32(high_ref[...], v) + dot32(low_ref[...], v)
    each = GROUP * OWN // 16
    row = lax.broadcasted_iota(jnp.int32, (each, 8, NB), 1)
    for p in range(PANELS):
        block = part[:, p * NB : (p + 1) * NB].reshape(each, 16, NB)
        power = power_of(jnp.max(jnp.abs(block), axis=(1, 2), keepdims=True))
        where = pl.ds(p * (K // 16) + group * each, each)
        pack_ref[where, 0:16, :] = levels(block, power).astype(jnp.int16)
        tail = jnp.where(row == 6, power, gram_ref[where])
        pack_ref[where, 16:24, :] = tail.astype(jnp.int32).astype(jnp.int16)


def project(codes, refl, gram):
    wide = jax.ShapeDtypeStruct((K, SUB), jnp.bfloat16)
    return pl.pallas_call(
        project_kernel,
        out_shape=(jax.ShapeDtypeStruct((DEVS, PACK, NB), jnp.int16), wide, wide),
        grid=(DEVS // GROUP,),
        in_specs=[
            pl.BlockSpec((GROUP, ROWS, 128), lambda g: (g, 0, 0)),
            pl.BlockSpec((SUB, PANELS * NB), lambda g: (0, 0)),
            pl.BlockSpec((DEVS, 8, NB), lambda g: (0, 0, 0)),
        ],
        out_specs=(pl.BlockSpec((DEVS, PACK, NB), lambda g: (0, 0, 0)),)
        + (pl.BlockSpec((GROUP * OWN, SUB), lambda g: (g, 0)),) * 2,
        name="project",
    )(codes, refl, gram)


def total_kernel(in_ref, out_ref):
    level = to_float(in_ref[...])
    value = level * jnp.abs(level)
    proj = jnp.sum(value[:, 0:16] * unit_of(level[:, 22:23]), axis=0)
    gram = jnp.sum(value[:, 16:24] * unit_of(level[:, 23:24]), axis=0)
    row = lax.broadcasted_iota(jnp.int32, (8, NB), 0)
    gram = jnp.where(row < 6, gram, 0.0)
    proj_power = power_of(jnp.max(jnp.abs(proj), axis=(0, 1), keepdims=True))
    gram_power = power_of(jnp.max(jnp.abs(gram), axis=(0, 1), keepdims=True))
    tail = jnp.where(row == 6, proj_power, jnp.where(row == 7, gram_power, levels(gram, gram_power).astype(jnp.float32)))
    code = jnp.concatenate([levels(proj, proj_power), tail.astype(jnp.int32)], axis=0)
    out_ref[...] = jnp.broadcast_to(code[None], out_ref.shape).astype(jnp.int16)


def total(parts):
    return pl.pallas_call(
        total_kernel,
        out_shape=jax.ShapeDtypeStruct(parts.shape, parts.dtype),
        name="total",
    )(parts)


def update_kernel(s_ref, sums_ref, t0, t1, t2, t3, high_ref, low_ref, refl_ref, out_ref, c_high, c_low):
    step = pl.program_id(0)

    @pl.when(step == 0)
    def _():
        level = to_float(sums_ref[...])
        value = level * jnp.abs(level)
        proj = value[:, 0:16] * unit_of(level[:, 22:23])
        blocks = jnp.swapaxes(value[:, 16:24] * unit_of(level[:, 23:24]), 0, 1)
        gram = {pair: split(blocks[b]) for b, pair in enumerate(PAIRS)}
        found = {}
        for p in reversed(range(PANELS)):
            rest = proj[p * 32 : (p + 1) * 32].reshape(K, NB)
            for q in range(p + 1, PANELS):
                (c1, c2), (g1, g2) = found[q], gram[(q, p)]
                rest -= dot32(c1, g1) + (dot32(c1, g2) + dot32(c2, g1))
            triangle = decode_triangle((t0, t1, t2, t3)[p][...]).reshape(NB, NB)
            r1, r2 = split(rest)
            dims = ((1,), (1,))
            found[p] = split(dot32(r1, triangle, dims) + dot32(r2, triangle, dims))
            c_high[:, p * NB : (p + 1) * NB] = found[p][0]
            c_low[:, p * NB : (p + 1) * NB] = found[p][1]

    v = refl_ref[...]
    change = dot32(c_high[...], v, ((1,), (1,))) + dot32(c_low[...], v, ((1,), (1,)))
    back = high_ref[...].astype(jnp.float32) + (low_ref[...].astype(jnp.float32) - change)
    for c in range(COLS):
        block = back[c * WIDE : (c + 1) * WIDE]
        power = power_of(jnp.max(jnp.abs(block), axis=(0, 1), keepdims=True))
        code = levels(block, power).astype(jnp.int16)
        for t in range(STEP // 128):
            at = pl.multiple_of((step * (STEP // 128) + t) * WIDE, WIDE)
            out_ref[c, pl.ds(at, WIDE), :] = code[:, t * 128 : (t + 1) * 128]
        at = pl.multiple_of(TILES * WIDE + step * 8, 8)
        out_ref[c, pl.ds(at, 8), :] = jnp.broadcast_to(power, (8, 128)).astype(jnp.int32).astype(jnp.int16)


def update(scalars, sums, codes, high, low, refl):
    rows = TILES * WIDE + 8 * STEPS
    codes = codes.reshape(DEVS // COLS, COLS, ROWS, 128)
    triangle = [
        pl.BlockSpec((DEVS // COLS, pl.Squeezed(), 8, NB), lambda k, s, p=p: (0, s[p], OWN * TILES // 8, 0))
        for p in range(PANELS)
    ]
    return pl.pallas_call(
        update_kernel,
        out_shape=jax.ShapeDtypeStruct((COLS, rows, 128), jnp.int16),
        grid_spec=pltpu.PrefetchScalarGridSpec(
            num_scalar_prefetch=1,
            grid=(STEPS,),
            in_specs=[pl.BlockSpec((DEVS, PACK, NB), lambda k, s: (0, 0, 0))]
            + triangle
            + [pl.BlockSpec((K, STEP), lambda k, s: (0, k))] * 2
            + [pl.BlockSpec((STEP, PANELS * NB), lambda k, s: (k, 0))],
            out_specs=pl.BlockSpec((COLS, rows, 128), lambda k, s: (0, 0, 0)),
            scratch_shapes=[pltpu.VMEM((K, PANELS * NB), jnp.bfloat16)] * 2,
        ),
        name="update",
    )(scalars, sums, codes, codes, codes, codes, high, low, refl)


def finish_kernel(code_ref, out_ref):
    for k in range(STEPS):
        at = TILES * WIDE + 8 * k
        unit = unit_of(to_float(code_ref[0, at : at + 8, :]))
        unit = jnp.concatenate([unit] * (WIDE // 8), axis=0)
        for t in range(k * (STEP // 128), (k + 1) * (STEP // 128)):
            level = to_float(code_ref[0, t * WIDE : (t + 1) * WIDE, :])
            out_ref[:, t * 128 : (t + 1) * 128] = level * jnp.abs(level) * unit


def finish(codes):
    rows = codes.shape[1]
    return pl.pallas_call(
        finish_kernel,
        out_shape=jax.ShapeDtypeStruct((WIDE, COLS * SUB), jnp.float32),
        grid=(COLS,),
        in_specs=[pl.BlockSpec((1, rows, 128), lambda g: (g, 0, 0))],
        out_specs=pl.BlockSpec((WIDE, SUB), lambda g: (0, g)),
        name="finish",
    )(codes)


def exchange(x, axis):
    return lax.all_to_all(x, axis, split_axis=0, concat_axis=0, tiled=True)


def local(eigvecs, panels, tfactors, owners, offsets):
    row, col = lax.axis_index("row"), lax.axis_index("col")
    first = (row * COLS + col) * SUB
    scalars = jnp.concatenate([owners, offsets, jnp.full((1,), first, jnp.int32)])
    slots = exchange(panels.reshape(COLS, SUB, NB), "col")
    triangle = lax.dynamic_slice_in_dim(tfactors[0], row * 8, 8, 0)
    sent, slots = lax.optimization_barrier((encode(eigvecs, triangle), slots))
    codes = exchange(sent, ALL)
    gram, refl = gram_of(scalars, slots)
    pack, high, low = project(codes, refl, gram)
    sums = exchange(total(exchange(pack, ALL)), ALL)
    out = update(scalars, sums, codes, high, low, refl)
    return finish(exchange(out, "col"))


def solution(mesh):
    in_specs = (P(ALL, None), P("col", "row", None), P("col", None, None), P(), P())
    out_specs = P("col", "row")
    return jax.shard_map(local, mesh=mesh, in_specs=in_specs, out_specs=out_specs, check_vma=False)
```

time: 235 us -> 206 us (0.88)
  blocking collectives: 93.5 us -> 76.1 us
  waiting for transfers between devices: 69.9 us -> 62 us
  other arithmetic: 5.25 us -> 0.64 us
    all_to_all x3, blocking collectives: 93.5 us -> 76.1 us  [exchange(): return lax.all_to_all(x, axis, split_axis=0, concat_axis=0, tiled=True)]
    all_to_all x2, waiting for transfers between devices: 69.9 us -> 62 us  [exchange(): return lax.all_to_all(x, axis, split_axis=0, concat_axis=0, tiled=True)]
    concatenate x2 -> x1, other arithmetic: 5.25 us -> 0.64 us  [local(): jnp.concatenate([owners, offsets, jnp.full((1,), first, jnp.int32)])]
  transfers between devices with their start and end apart: 2 -> 2, of which waited for: 2 -> 2; matrix products, arithmetic and copies ran while one was open for 2% -> 1% of each run, Pallas kernels for 2% -> 8%
where the time goes in v2:
time: 206 us; the launch traced here: 205 us
  blocking collectives  76.1 us (37%)
  waiting for transfers between devices  62 us (30%)
  Pallas kernels  47.8 us (23%)
  starting transfers between devices  16.1 us (8%)
    all_to_all x3, blocking collectives, exchange(): return lax.all_to_all(x, axis, split_axis=0, concat_axis=0, tiled=True)  76.1 us
    all_to_all x2, waiting for transfers between devices, exchange(): return lax.all_to_all(x, axis, split_axis=0, concat_axis=0, tiled=True)  62 us
    all_to_all x2, starting transfers between devices, exchange(): return lax.all_to_all(x, axis, split_axis=0, concat_axis=0, tiled=True)  16.1 us
    pallas_call x1, Pallas kernels, update(): pl.pallas_call(update_kernel, out_shape=jax.ShapeDtypeStruct((COLS, rows,...  12.1 us
    pallas_call x1, Pallas kernels, encode(): pl.pallas_call(encode_kernel, out_shape=jax.ShapeDtypeStruct((DEVS, ROWS,...  10.6 us
    pallas_call x1, Pallas kernels, project(): pl.pallas_call(project_kernel, out_shape=(jax.ShapeDtypeStruct((DEVS, PAC...  9.4 us
    pallas_call x1, Pallas kernels, gram_of(): pl.pallas_call(gram_kernel, out_shape=(jax.ShapeDtypeStruct((DEVS, 8, NB)...  6.67 us
    pallas_call x1, Pallas kernels, finish(): pl.pallas_call(finish_kernel, out_shape=jax.ShapeDtypeStruct((WIDE, COLS...  6.2 us
  transfers between devices with their start and end apart: 2, of which 2 were waited for; matrix products, arithmetic and copies ran while one was open for 1% of the time, Pallas kernels for 8%

profile of v2, /device:TPU:0, one launch (start us, length us, event | category | flops | bytes accessed | tf_op | source)
XLA Modules:
  0.0 204.6 jit_solution(3192955280454033972)
XLA Ops:
  0.0 0.0 copy-start
  0.0 7.2 %all-to-all-start = ((bf16[8,2048,128]{2,1,0:T(8,128)(2,1)}), bf16[8,2048,128]{2,1,0:T(8,128)(2,1)}, u32[]{:S(2)}, u32[]{:S(2)}) async-start(bf16[8,2048,128]{2,1,0:T(8,128)(2,1)} %bitcast.9), calls=%async_computation | async-start | bytes 8388608 | tf_op jit(solution)/shard_map/all_to_all | solution.py:311
  7.2 0.0 copy-done
  7.2 0.6 dynamic-slice_bitcast_fusion.t_ref
  7.8 10.6 %encode.1 = s16[128,72,128]{2,1,0:T(8,128)(2,1)} custom-call(f32[4,262144]{1,0:T(4,128)} %e_ref.1, bf16[8,128]{1,0:T(8,128)(2,1)} %dynamic-slice_bitcast_fusion.t_ref), custom_call_target="tpu_custom_call" | custom-call | tf_op jit(solution)/shard_map/encode/pallas_call | solution.py:97
  18.3 0.0 copy-start.2
  18.3 0.0 copy-start.3
  18.3 37.9 %all-to-all-done.v0.v1.v2.v3 = bf16[8,2048,128]{2,1,0:T(8,128)(2,1)} async-done(((bf16[8,2048,128]{2,1,0:T(8,128)(2,1)}), bf16[8,2048,128]{2,1,0:T(8,128)(2,1)}, u32[]{:S(2)}, u32[]{:S(2)}) %all-to-all-start) | async-done | bytes 4194336 | tf_op jit(solution)/shard_map/all_to_all | solution.py:311
  56.2 8.9 %all-to-all-start.1 = ((s16[128,72,128]{2,1,0:T(8,128)(2,1)}), s16[128,72,128]{2,1,0:T(8,128)(2,1)S(1)}, u32[]{:S(2)}, u32[]{:S(2)}) async-start(s16[128,72,128]{2,1,0:T(8,128)(2,1)} %encode.1), calls=%async_computation.1 | async-start | bytes 4718592 | tf_op jit(solution)/shard_map/all_to_all | solution.py:311
  65.1 0.0 copy-done.2
  65.1 0.0 copy-done.3
  65.1 0.6 pad_add_fusion.s_ref
  65.7 6.7 %gram.1 = (f32[128,8,128]{2,1,0:T(8,128)}, bf16[2048,512]{1,0:T(8,128)(2,1)}) custom-call(s32[9]{0:T(128)} %pad_add_fusion.s_ref, bf16[8,2048,128]{2,1,0:T(8,128)(2,1)} %all-to-all-done.v0.v1.v2.v3, bf16[8,2048,128]{2,1,0:T(8,128)(2,1)} %all-to-all-done.v0.v1.v2.v3, bf16[8,2048,128]{2,1,0:T(8,128)(2,1)} %all-to-all-done.v0.v1.v2.v3, ...), custom_call_target="tpu_custom_call" | custom-call | tf_op jit(solution)/shard_map/gram/pallas_call | solution.py:141
  72.4 24.1 %all-to-all-done.1.code_ref = s16[128,72,128]{2,1,0:T(8,128)(2,1)S(1)} async-done(((s16[128,72,128]{2,1,0:T(8,128)(2,1)}), s16[128,72,128]{2,1,0:T(8,128)(2,1)S(1)}, u32[]{:S(2)}, u32[]{:S(2)}) %all-to-all-start.1) | async-done | bytes 2359328 | tf_op jit(solution)/shard_map/all_to_all | solution.py:311
  96.5 0.0 copy-start.1
  96.5 1.4 copy-done.1
  97.9 9.4 %project.1 = (s16[128,24,128]{2,1,0:T(8,128)(2,1)}, bf16[512,2048]{1,0:T(8,128)(2,1)}, bf16[512,2048]{1,0:T(8,128)(2,1)}) custom-call(s16[128,72,128]{2,1,0:T(8,128)(2,1)} %copy-done.1, bf16[2048,512]{1,0:T(8,128)(2,1)} %get-tuple-element.14.refl_ref, f32[128,8,128]{2,1,0:T(8,128)} %get-tuple-element.15.gram_ref), custom_call_target="tpu_custom_call" | custom-call | tf_op jit(solution)/shard_map/project/pallas_call | solution.py:190
  107.3 21.5 %all_to_all.25.in_ref = s16[128,24,128]{2,1,0:T(8,128)(2,1)} all-to-all(s16[128,24,128]{2,1,0:T(8,128)(2,1)} %get-tuple-element.16), channel_id=1, replica_groups=mesh['row'=16,'col'=8] {'row','col'}, dimensions={0} | all-to-all | bytes 1572864 | tf_op jit(solution)/shard_map/all_to_all | solution.py:311
  128.8 2.9 %total.1 = s16[128,24,128]{2,1,0:T(8,128)(2,1)} custom-call(s16[128,24,128]{2,1,0:T(8,128)(2,1)} %all_to_all.25.in_ref), custom_call_target="tpu_custom_call" | custom-call | tf_op jit(solution)/shard_map/total/pallas_call | solution.py:220
  131.7 21.0 %all_to_all.26.sums_ref = s16[128,24,128]{2,1,0:T(8,128)(2,1)} all-to-all(s16[128,24,128]{2,1,0:T(8,128)(2,1)} %total.1), channel_id=1, replica_groups=mesh['row'=16,'col'=8] {'row','col'}, dimensions={0} | all-to-all | bytes 1572864 | tf_op jit(solution)/shard_map/all_to_all | solution.py:311
  152.7 12.1 %update.1 = s16[8,1056,128]{2,1,0:T(8,128)(2,1)} custom-call(s32[9]{0:T(128)} %pad_add_fusion.s_ref, s16[128,24,128]{2,1,0:T(8,128)(2,1)} %all_to_all.26.sums_ref, s16[16,8,72,128]{3,2,1,0:T(8,128)(2,1)} %bitcast.5, s16[16,8,72,128]{3,2,1,0:T(8,128)(2,1)} %bitcast.6, s16[16,8,72,128]{3,2,1,0:T(8,128)(2,1)} %bitcast.7, s16[16,8,72,128]{3,2,1,0:T(8,128)(2,1)} %bitcast.8, ...), custom_call_target="tpu_custom_call" | custom-call | tf_op jit(solution)/shard_map/update/pallas_call | solution.py:271
  164.8 33.5 %all_to_all.27.code_ref = s16[8,1056,128]{2,1,0:T(8,128)(2,1)} all-to-all(s16[8,1056,128]{2,1,0:T(8,128)(2,1)} %update.1), channel_id=1, replica_groups=mesh['row'=16,'col'=8] {'col'}, dimensions={0} | all-to-all | bytes 4325376 | tf_op jit(solution)/shard_map/all_to_all | solution.py:311
  198.4 6.2 %finish.1 = f32[64,16384]{1,0:T(8,128)} custom-call(s16[8,1056,128]{2,1,0:T(8,128)(2,1)} %all_to_all.27.code_ref), custom_call_target="tpu_custom_call" | custom-call | tf_op jit(solution)/shard_map/finish/pallas_call | solution.py:300
Async XLA Ops:
  0.0 7.2 %copy-start = (bf16[1,128,128]{2,1,0:T(8,128)(2,1)S(1)}, bf16[1,128,128]{2,1,0:T(8,128)(2,1)}, u32[]{:S(2)}) copy-start(bf16[1,128,128]{2,1,0:T(8,128)(2,1)} %param.7) | copy-start | bytes 98308
  0.0 56.2 %all-to-all-start = ((bf16[8,2048,128]{2,1,0:T(8,128)(2,1)}), bf16[8,2048,128]{2,1,0:T(8,128)(2,1)}, u32[]{:S(2)}, u32[]{:S(2)}) async-start(bf16[8,2048,128]{2,1,0:T(8,128)(2,1)} %bitcast.9), calls=%async_computation | async-start | bytes 8388608 | tf_op jit(solution)/shard_map/all_to_all | solution.py:311
  18.3 46.8 %copy-start.2 = (s32[4]{0:T(128)S(1)}, s32[4]{0:T(128)}, u32[]{:S(2)}) copy-start(s32[4]{0:T(128)} %param.9) | copy-start | bytes 52
  18.3 46.8 %copy-start.3 = (s32[4]{0:T(128)S(1)}, s32[4]{0:T(128)}, u32[]{:S(2)}) copy-start(s32[4]{0:T(128)} %param.8) | copy-start | bytes 52
  56.2 40.4 %all-to-all-start.1 = ((s16[128,72,128]{2,1,0:T(8,128)(2,1)}), s16[128,72,128]{2,1,0:T(8,128)(2,1)S(1)}, u32[]{:S(2)}, u32[]{:S(2)}) async-start(s16[128,72,128]{2,1,0:T(8,128)(2,1)} %encode.1), calls=%async_computation.1 | async-start | bytes 4718592 | tf_op jit(solution)/shard_map/all_to_all | solution.py:311
  96.5 1.4 copy-start.1

commit v3 on v0

v3 whole, which is shorter than its diff:
```python
import math

import jax
import jax.numpy as jnp
from jax import lax
from jax.experimental import pallas as pl
from jax.experimental.pallas import tpu as pltpu
from jax.sharding import PartitionSpec as P

PANELS = 4
NB = 128
K = 512
DEVS = 128
COLS = 8
OWN = 4
SUB = 2048
STEP = 512
STEPS = SUB // STEP
TILES = SUB // 128
WIDE = K // COLS
PACK = 24
PAIRS = [(q, p) for q in range(PANELS) for p in range(q)]
ALL = ("row", "col")
ROOM = 24 << 20

ASINH_TOP = 12.5
KNEE = 6.0 / math.sinh(ASINH_TOP)
ASINH_SCALE = 32767.0 / ASINH_TOP
LN2 = math.log(2.0)
T_STEPS = 258.0
T_ZERO = 50.0 * T_STEPS
ROWS = OWN * TILES + 8


def signed(level, like):
    return jnp.where(like < 0.0, -level, level)


def to_float(code):
    return code.astype(jnp.int32).astype(jnp.float32)


def encode_value(x):
    y = jnp.abs(x) * (1.0 / KNEE)
    level = jnp.log(y + jnp.sqrt(y * y + 1.0)) * ASINH_SCALE + 0.5
    return signed(jnp.minimum(level, 32767.0).astype(jnp.int32), x).astype(jnp.int16)


def decode_value(code):
    angle = to_float(code) * (1.0 / ASINH_SCALE)
    return (jnp.exp(angle) - jnp.exp(-angle)) * (0.5 * KNEE)


def encode_triangle(x):
    level = jnp.log(jnp.maximum(jnp.abs(x), 1e-30)) * (T_STEPS / LN2) + (T_ZERO + 0.5)
    level = jnp.clip(level, 0.0, 32767.0).astype(jnp.int32)
    return signed(level, x).astype(jnp.int16)


def decode_triangle(code):
    level = to_float(code)
    size = jnp.exp((jnp.abs(level) - T_ZERO) * (LN2 / T_STEPS))
    return jnp.where(level == 0.0, 0.0, signed(size, level)).astype(jnp.bfloat16)


def power_of(most):
    return jnp.ceil(jnp.log(jnp.maximum(most, 1e-30)) * (8.0 / LN2) + 0.01)


def levels(x, power):
    size = jnp.sqrt(jnp.abs(x) * jnp.exp(power * (-LN2 / 8.0))) * 32767.0 + 0.5
    return signed(size.astype(jnp.int32), x)


def unit_of(power):
    return jnp.exp(power * (LN2 / 8.0)) * (1.0 / 32767.0**2)


def dot32(a, b, dims=((1,), (0,))):
    return lax.dot_general(a, b, (dims, ((), ())), preferred_element_type=jnp.float32)


def split(x):
    high = x.astype(jnp.bfloat16)
    return high, (x - high.astype(jnp.float32)).astype(jnp.bfloat16)


def encode_kernel(e_ref, t_ref, out_ref):
    triangle = encode_triangle(t_ref[...].astype(jnp.float32))
    for d in range(out_ref.shape[0]):
        x = e_ref[:, d * SUB : (d + 1) * SUB]
        tall = jnp.concatenate([x[:, t * 128 : (t + 1) * 128] for t in range(TILES)], axis=0)
        out_ref[d, 0 : OWN * TILES, :] = encode_value(tall)
        out_ref[d, OWN * TILES : ROWS, :] = triangle


def encode(eigvecs, triangle):
    group = 8
    return pl.pallas_call(
        encode_kernel,
        out_shape=jax.ShapeDtypeStruct((DEVS, ROWS, 128), jnp.int16),
        grid=(DEVS // group,),
        in_specs=[
            pl.BlockSpec((OWN, group * SUB), lambda g: (0, g)),
            pl.BlockSpec((8, NB), lambda g: (0, 0)),
        ],
        out_specs=pl.BlockSpec((group, ROWS, 128), lambda g: (g, 0, 0)),
        compiler_params=pltpu.CompilerParams(vmem_limit_bytes=ROOM),
        name="encode",
    )(eigvecs, triangle)


def gram_kernel(s_ref, slot_ref, gram_ref, refl_ref):
    gram = jnp.zeros((PANELS * NB, PANELS * NB), jnp.float32)
    for step in range(STEPS):
        row_ids = s_ref[8] + step * STEP + lax.broadcasted_iota(jnp.int32, (STEP, NB), 0)
        base = row_ids - lax.broadcasted_iota(jnp.int32, (STEP, NB), 1)
        rows = slice(step * STEP, (step + 1) * STEP)
        for p in range(PANELS):
            below = base - s_ref[4 + p]
            unit = jnp.where(below == 0, jnp.float32(1.0), jnp.float32(0.0))
            block = jnp.where(below > 0, slot_ref[s_ref[p], rows, :].astype(jnp.float32), unit)
            refl_ref[rows, p * NB : (p + 1) * NB] = block.astype(jnp.bfloat16)
        v = refl_ref[rows, :]
        gram += dot32(v, v, ((0,), (0,)))
    blocks = [gram[q * NB : (q + 1) * NB, p * NB : (p + 1) * NB] for q, p in PAIRS]
    most = jnp.zeros((1, 1), jnp.float32)
    for block in blocks:
        most = jnp.maximum(most, jnp.max(jnp.abs(block), axis=(0, 1), keepdims=True))
    power = power_of(most)
    rows = [levels(block, power).astype(jnp.float32) for block in blocks]
    rows += [jnp.zeros((NB, NB), jnp.float32), jnp.broadcast_to(power, (NB, NB))]
    gram_ref[...] = jnp.swapaxes(jnp.stack(rows), 0, 1)


def call(kernel, outs, ins, name, scalars=None, scratch=()):
    spec = pl.BlockSpec(memory_space=pltpu.VMEM)
    kept = [pltpu.with_memory_space_constraint(x, pltpu.VMEM) for x in ins]
    head = [] if scalars is None else [scalars]
    return pl.pallas_call(
        kernel,
        out_shape=tuple(pltpu.VMEM(*out) for out in outs),
        in_specs=[pl.BlockSpec(memory_space=pltpu.SMEM)] * len(head) + [spec] * len(kept),
        out_specs=(spec,) * len(outs),
        scratch_shapes=list(scratch),
        compiler_params=pltpu.CompilerParams(vmem_limit_bytes=ROOM),
        name=name,
    )(*head, *kept)


def gram_of(scalars, slots):
    outs = (((DEVS, 8, NB), jnp.float32), ((SUB, PANELS * NB), jnp.bfloat16))
    return call(gram_kernel, outs, (slots,), "gram", scalars)


def project_kernel(code_ref, refl_ref, gram_ref, pack_ref, high_ref, low_ref):
    upper = lax.broadcasted_iota(jnp.int32, (DEVS // 2, 8, 128), 1) < OWN
    for t in range(0, TILES, 2):
        x = decode_value(code_ref[:, t * OWN : (t + 2) * OWN, :]).reshape(DEVS // 2, 2, 8, 128)
        even, odd = x[:, 0], x[:, 1]
        first = jnp.where(upper, even, pltpu.roll(odd, OWN, 1))
        second = jnp.where(upper, pltpu.roll(even, OWN, 1), odd)
        for k, tile in ((t, first), (t + 1, second)):
            high, low = split(tile.reshape(K, 128))
            high_ref[:, k * 128 : (k + 1) * 128] = high
            low_ref[:, k * 128 : (k + 1) * 128] = low
    v = refl_ref[...]
    part = dot32(high_ref[...], v) + dot32(low_ref[...], v)
    each = K // 16
    row = lax.broadcasted_iota(jnp.int32, (each, 8, NB), 1)
    for p in range(PANELS):
        block = part[:, p * NB : (p + 1) * NB].reshape(each, 16, NB)
        power = power_of(jnp.max(jnp.abs(block), axis=(1, 2), keepdims=True))
        where = slice(p * each, (p + 1) * each)
        pack_ref[where, 0:16, :] = levels(block, power).astype(jnp.int16)
        tail = jnp.where(row == 6, power, gram_ref[where])
        pack_ref[where, 16:24, :] = tail.astype(jnp.int32).astype(jnp.int16)


def project(codes, refl, gram):
    outs = (((DEVS, PACK, NB), jnp.int16),) + (((K, SUB), jnp.bfloat16),) * 2
    return call(project_kernel, outs, (codes, refl, gram), "project")


def total_kernel(in_ref, out_ref):
    level = to_float(in_ref[...])
    value = level * jnp.abs(level)
    proj = jnp.sum(value[:, 0:16] * unit_of(level[:, 22:23]), axis=0)
    gram = jnp.sum(value[:, 16:24] * unit_of(level[:, 23:24]), axis=0)
    row = lax.broadcasted_iota(jnp.int32, (8, NB), 0)
    gram = jnp.where(row < 6, gram, 0.0)
    proj_power = power_of(jnp.max(jnp.abs(proj), axis=(0, 1), keepdims=True))
    gram_power = power_of(jnp.max(jnp.abs(gram), axis=(0, 1), keepdims=True))
    tail = jnp.where(row == 6, proj_power, jnp.where(row == 7, gram_power, levels(gram, gram_power).astype(jnp.float32)))
    code = jnp.concatenate([levels(proj, proj_power), tail.astype(jnp.int32)], axis=0)
    out_ref[...] = jnp.broadcast_to(code[None], out_ref.shape).astype(jnp.int16)


def total(parts):
    return call(total_kernel, ((parts.shape, parts.dtype),), (parts,), "total")[0]


def update_kernel(s_ref, sums_ref, code_ref, high_ref, low_ref, refl_ref, out_ref, c_high, c_low):
    level = to_float(sums_ref[...])
    value = level * jnp.abs(level)
    proj = value[:, 0:16] * unit_of(level[:, 22:23])
    blocks = jnp.swapaxes(value[:, 16:24] * unit_of(level[:, 23:24]), 0, 1)
    gram = {pair: split(blocks[b]) for b, pair in enumerate(PAIRS)}
    found = {}
    for p in reversed(range(PANELS)):
        rest = proj[p * 32 : (p + 1) * 32].reshape(K, NB)
        for q in range(p + 1, PANELS):
            (c1, c2), (g1, g2) = found[q], gram[(q, p)]
            rest -= dot32(c1, g1) + (dot32(c1, g2) + dot32(c2, g1))
        kept = [code_ref[r * COLS + s_ref[p], OWN * TILES : ROWS, :] for r in range(DEVS // COLS)]
        triangle = decode_triangle(jnp.concatenate(kept, axis=0))
        r1, r2 = split(rest)
        dims = ((1,), (1,))
        found[p] = split(dot32(r1, triangle, dims) + dot32(r2, triangle, dims))
        c_high[:, p * NB : (p + 1) * NB] = found[p][0]
        c_low[:, p * NB : (p + 1) * NB] = found[p][1]
    for step in range(STEPS):
        cols = slice(step * STEP, (step + 1) * STEP)
        v = refl_ref[cols, :]
        change = dot32(c_high[...], v, ((1,), (1,))) + dot32(c_low[...], v, ((1,), (1,)))
        back = high_ref[:, cols].astype(jnp.float32) + (low_ref[:, cols].astype(jnp.float32) - change)
        for c in range(COLS):
            block = back[c * WIDE : (c + 1) * WIDE]
            power = power_of(jnp.max(jnp.abs(block), axis=(0, 1), keepdims=True))
            code = levels(block, power).astype(jnp.int16)
            for t in range(STEP // 128):
                at = (step * (STEP // 128) + t) * WIDE
                out_ref[c, at : at + WIDE, :] = code[:, t * 128 : (t + 1) * 128]
            at = TILES * WIDE + step * 8
            out_ref[c, at : at + 8, :] = jnp.broadcast_to(power, (8, 128)).astype(jnp.int32).astype(jnp.int16)


def update(scalars, sums, codes, high, low, refl):
    outs = (((COLS, TILES * WIDE + 8 * STEPS, 128), jnp.int16),)
    scratch = [pltpu.VMEM((K, PANELS * NB), jnp.bfloat16)] * 2
    return call(update_kernel, outs, (sums, codes, high, low, refl), "update", scalars, scratch)[0]


def finish_kernel(code_ref, out_ref, rows, sems):
    copies = []
    for c in range(COLS):
        for k in range(STEPS):
            at = TILES * WIDE + 8 * k
            unit = unit_of(to_float(code_ref[c, at : at + 8, :]))
            unit = jnp.concatenate([unit] * (WIDE // 8), axis=0)
            for t in range(k * (STEP // 128), (k + 1) * (STEP // 128)):
                level = to_float(code_ref[c, t * WIDE : (t + 1) * WIDE, :])
                rows[:, c * SUB + t * 128 : c * SUB + (t + 1) * 128] = level * jnp.abs(level) * unit
        part = (slice(None), pl.ds(c * SUB, SUB))
        copies.append(pltpu.make_async_copy(rows.at[part], out_ref.at[part], sems.at[c]))
        copies[-1].start()
    for copy in copies:
        copy.wait()


def finish(codes):
    return pl.pallas_call(
        finish_kernel,
        out_shape=jax.ShapeDtypeStruct((WIDE, COLS * SUB), jnp.float32),
        in_specs=[pl.BlockSpec(memory_space=pltpu.VMEM)],
        out_specs=pl.BlockSpec(memory_space=pl.ANY),
        scratch_shapes=[pltpu.VMEM((WIDE, COLS * SUB), jnp.float32), pltpu.SemaphoreType.DMA((COLS,))],
        compiler_params=pltpu.CompilerParams(vmem_limit_bytes=ROOM),
        name="finish",
    )(pltpu.with_memory_space_constraint(codes, pltpu.VMEM))


def exchange(x, axis):
    return lax.all_to_all(x, axis, split_axis=0, concat_axis=0, tiled=True)


def local(eigvecs, panels, tfactors, owners, offsets):
    row, col = lax.axis_index("row"), lax.axis_index("col")
    first = (row * COLS + col) * SUB
    scalars = jnp.concatenate([owners, offsets, jnp.full((1,), first, jnp.int32)])
    slots = exchange(panels.reshape(COLS, SUB, NB), "col")
    triangle = lax.dynamic_slice_in_dim(tfactors[0], row * 8, 8, 0)
    sent, slots = lax.optimization_barrier((encode(eigvecs, triangle), slots))
    codes = exchange(sent, ALL)
    gram, refl = gram_of(scalars, slots)
    pack, high, low = project(codes, refl, gram)
    sums = exchange(total(exchange(pack, ALL)), ALL)
    out = update(scalars, sums, codes, high, low, refl)
    return finish(exchange(out, "col"))


def solution(mesh):
    in_specs = (P(ALL, None), P("col", "row", None), P("col", None, None), P(), P())
    out_specs = P("col", "row")
    return jax.shard_map(local, mesh=mesh, in_specs=in_specs, out_specs=out_specs, check_vma=False)
```

time: 812 us -> 189 us (0.23); the launches traced: 801 us -> 188 us
  blocking collectives: 436 us -> 75.1 us
  waiting for transfers between devices: 224 us -> 67.4 us
  matrix products: 94.4 us -> 0 us
  Pallas kernels: 0 us -> 22.7 us
  between operations: 16.5 us -> 0.28 us
  local copies, waits for them, and re-layouts: 18.1 us -> 6.52 us
  starting transfers between devices: 4.77 us -> 16.1 us
    psum x4 -> x0, blocking collectives: 214 us -> none  [local(): projection = lax.psum(partial_sum, 'row')]
    all_to_all x1 -> x3, blocking collectives: 222 us -> 75.1 us  [exchange(): return lax.all_to_all(x, axis, split_axis=0, concat_axis=0, tiled=True)]
    psum x2 -> x0, waiting for transfers between devices: 124 us -> none  [from_root(): return lax.psum(jnp.where(mine, value, jnp.zeros_like(value)), axis)]
    dot_general x12 -> x0, matrix products: 94.4 us -> none  [the longest x4 53.6 us: local(): jnp.dot(coeffs, reflector.T, precision=highest, preferred_element_type=jn...]
    all_to_all x1 -> x2, waiting for transfers between devices: 99.6 us -> 67.4 us  [exchange(): return lax.all_to_all(x, axis, split_axis=0, concat_axis=0, tiled=True)]
    pallas_call x0 -> x6, Pallas kernels: none -> 22.7 us  [the longest x4 17 us: call(): pl.pallas_call(kernel, out_shape=tuple((pltpu.VMEM(*out) for out in outs)...]
    all_to_all x1 -> x2, starting transfers between devices: 4.72 us -> 16.1 us  [exchange(): return lax.all_to_all(x, axis, split_axis=0, concat_axis=0, tiled=True)]
    all_to_all x2 -> x0, local copies, waits for them, and re-layouts: 9.97 us -> none  [local(): lax.all_to_all(spread, 'col', split_axis=0, concat_axis=1, tiled=True)]
  transfers between devices with their start and end apart: 3 -> 2, of which waited for: 3 -> 2; matrix products, arithmetic and copies ran while one was open for 3% -> 0% of each run, Pallas kernels for 0% -> 4%
where the time goes in v3:
time: 189 us; the launch traced here: 188 us
  blocking collectives  75.1 us (40%)
  waiting for transfers between devices  67.4 us (36%)
  Pallas kernels  22.7 us (12%)
  starting transfers between devices  16.1 us (9%)
  local copies, waits for them, and re-layouts  6.52 us (3%)
    all_to_all x3, blocking collectives, exchange(): return lax.all_to_all(x, axis, split_axis=0, concat_axis=0, tiled=True)  75.1 us
    all_to_all x2, waiting for transfers between devices, exchange(): return lax.all_to_all(x, axis, split_axis=0, concat_axis=0, tiled=True)  67.4 us
    pallas_call x4, Pallas kernels, call(): pl.pallas_call(kernel, out_shape=tuple((pltpu.VMEM(*out) for out in outs)...  17 us
    all_to_all x2, starting transfers between devices, exchange(): return lax.all_to_all(x, axis, split_axis=0, concat_axis=0, tiled=True)  16.1 us
    unnamed x16, local copies, waits for them, and re-layouts  6.51 us
  transfers between devices with their start and end apart: 2, of which 2 were waited for; matrix products, arithmetic and copies ran while one was open for 0% of the time, Pallas kernels for 4%

profile of v3, /device:TPU:0, one launch (start us, length us, event | category | flops | bytes accessed | tf_op | source)
XLA Modules:
  0.0 188.2 jit_solution(11633036466839468573)
XLA Ops:
  0.0 0.0 copy-start
  0.0 7.2 %all-to-all-start = ((bf16[8,2048,128]{2,1,0:T(8,128)(2,1)}), bf16[8,2048,128]{2,1,0:T(8,128)(2,1)}, u32[]{:S(2)}, u32[]{:S(2)}) async-start(bf16[8,2048,128]{2,1,0:T(8,128)(2,1)} %bitcast.4), calls=%async_computation | async-start | bytes 8388608 | tf_op jit(solution)/shard_map/all_to_all | solution.py:274
  7.2 0.0 copy-done
  7.2 0.0 copy-start.5
  7.2 2.2 %copy-done.5 = f32[4,262144]{1,0:T(4,128)S(1)} copy-done((f32[4,262144]{1,0:T(4,128)S(1)}, f32[4,262144]{1,0:T(4,128)}, u32[]{:S(2)}) %copy-start.5) | copy-done | bytes 4194328
  9.4 3.6 %encode.1 = s16[128,72,128]{2,1,0:T(8,128)(2,1)S(1)} custom-call(f32[4,262144]{1,0:T(4,128)S(1)} %copy-done.5, bf16[8,128]{1,0:T(8,128)(2,1)S(1)} %dynamic-slice_bitcast_fusion.t_ref), custom_call_target="tpu_custom_call" | custom-call | tf_op jit(solution)/shard_map/encode/pallas_call | solution.py:99
  13.0 0.0 copy-start.1
  13.0 1.4 copy-done.1
  14.4 0.0 copy-start.6
  14.4 0.0 copy-start.7
  14.4 41.8 %all-to-all-done.slot_ref = bf16[8,2048,128]{2,1,0:T(8,128)(2,1)} async-done(((bf16[8,2048,128]{2,1,0:T(8,128)(2,1)}), bf16[8,2048,128]{2,1,0:T(8,128)(2,1)}, u32[]{:S(2)}, u32[]{:S(2)}) %all-to-all-start) | async-done | bytes 4194336 | tf_op jit(solution)/shard_map/all_to_all | solution.py:274
  56.2 8.9 %all-to-all-start.1 = ((s16[128,72,128]{2,1,0:T(8,128)(2,1)}), s16[128,72,128]{2,1,0:T(8,128)(2,1)S(1)}, u32[]{:S(2)}, u32[]{:S(2)}) async-start(s16[128,72,128]{2,1,0:T(8,128)(2,1)} %copy-done.1), calls=%async_computation.1 | async-start | bytes 4718592 | tf_op jit(solution)/shard_map/all_to_all | solution.py:274
  65.1 0.0 copy-done.6
  65.1 0.0 copy-done.7
  65.1 0.1 pad_add_fusion.s_ref
  65.2 4.4 %gram.1 = (f32[128,8,128]{2,1,0:T(8,128)S(1)}, bf16[2048,512]{1,0:T(8,128)(2,1)S(1)}) custom-call(s32[9]{0:T(128)S(1)} %pad_add_fusion.s_ref, bf16[8,2048,128]{2,1,0:T(8,128)(2,1)} %all-to-all-done.slot_ref), custom_call_target="tpu_custom_call" | custom-call | tf_op jit(solution)/shard_map/gram/pallas_call | solution.py:140
  69.6 0.0 copy-start.2
  69.6 1.3 copy-done.2
  70.9 25.6 %all-to-all-done.1.code_ref = s16[128,72,128]{2,1,0:T(8,128)(2,1)S(1)} async-done(((s16[128,72,128]{2,1,0:T(8,128)(2,1)}), s16[128,72,128]{2,1,0:T(8,128)(2,1)S(1)}, u32[]{:S(2)}, u32[]{:S(2)}) %all-to-all-start.1) | async-done | bytes 2359328 | tf_op jit(solution)/shard_map/all_to_all | solution.py:274
  96.5 0.0 copy-start.3
  96.5 1.6 copy-done.3
  98.1 4.8 %project.1 = (s16[128,24,128]{2,1,0:T(8,128)(2,1)S(1)}, bf16[512,2048]{1,0:T(8,128)(2,1)S(1)}, bf16[512,2048]{1,0:T(8,128)(2,1)S(1)}) custom-call(s16[128,72,128]{2,1,0:T(8,128)(2,1)S(1)} %all-to-all-done.1.code_ref, bf16[2048,512]{1,0:T(8,128)(2,1)S(1)} %copy-done.3, f32[128,8,128]{2,1,0:T(8,128)S(1)} %get-tuple-element.15.gram_ref), custom_call_target="tpu_custom_call" | custom-call | tf_op jit(solution)/shard_map/project/pallas_call | solution.py:140
  103.0 0.0 copy-start.4
  103.0 21.1 %all_to_all.25.in_ref = s16[128,24,128]{2,1,0:T(8,128)(2,1)S(1)} all-to-all(s16[128,24,128]{2,1,0:T(8,128)(2,1)S(1)} %get-tuple-element.16), channel_id=1, replica_groups=mesh['row'=16,'col'=8] {'row','col'}, dimensions={0} | all-to-all | bytes 1572864 | tf_op jit(solution)/shard_map/all_to_all | solution.py:274
  124.1 0.9 total.1
  125.0 20.7 %all_to_all.26.sums_ref = s16[128,24,128]{2,1,0:T(8,128)(2,1)S(1)} all-to-all(s16[128,24,128]{2,1,0:T(8,128)(2,1)S(1)} %total.1), channel_id=1, replica_groups=mesh['row'=16,'col'=8] {'row','col'}, dimensions={0} | all-to-all | bytes 1572864 | tf_op jit(solution)/shard_map/all_to_all | solution.py:274
  145.7 0.0 copy-done.4
  145.7 6.9 %update.1 = s16[8,1056,128]{2,1,0:T(8,128)(2,1)S(1)} custom-call(s32[9]{0:T(128)S(1)} %pad_add_fusion.s_ref, s16[128,24,128]{2,1,0:T(8,128)(2,1)S(1)} %all_to_all.26.sums_ref, s16[128,72,128]{2,1,0:T(8,128)(2,1)S(1)} %all-to-all-done.1.code_ref, bf16[512,2048]{1,0:T(8,128)(2,1)S(1)} %get-tuple-element.17.high_ref, ...), custom_call_target="tpu_custom_call" | custom-call | tf_op jit(solution)/shard_map/update/pallas_call | solution.py:140
  152.6 33.2 %all_to_all.27.code_ref = s16[8,1056,128]{2,1,0:T(8,128)(2,1)S(1)} all-to-all(s16[8,1056,128]{2,1,0:T(8,128)(2,1)S(1)} %update.1), channel_id=1, replica_groups=mesh['row'=16,'col'=8] {'col'}, dimensions={0} | all-to-all | bytes 4325376 | tf_op jit(solution)/shard_map/all_to_all | solution.py:274
  185.9 2.2 %finish.1 = f32[64,16384]{1,0:T(8,128)} custom-call(s16[8,1056,128]{2,1,0:T(8,128)(2,1)S(1)} %all_to_all.27.code_ref), custom_call_target="tpu_custom_call" | custom-call | tf_op jit(solution)/shard_map/finish/pallas_call | solution.py:262
  (1 shorter events, 0.0 us)
Async XLA Ops:
  0.0 7.2 %copy-start = (bf16[1,128,128]{2,1,0:T(8,128)(2,1)S(1)}, bf16[1,128,128]{2,1,0:T(8,128)(2,1)}, u32[]{:S(2)}) copy-start(bf16[1,128,128]{2,1,0:T(8,128)(2,1)} %param.7) | copy-start | bytes 98308
  0.0 56.2 %all-to-all-start = ((bf16[8,2048,128]{2,1,0:T(8,128)(2,1)}), bf16[8,2048,128]{2,1,0:T(8,128)(2,1)}, u32[]{:S(2)}, u32[]{:S(2)}) async-start(bf16[8,2048,128]{2,1,0:T(8,128)(2,1)} %bitcast.4), calls=%async_computation | async-start | bytes 8388608 | tf_op jit(solution)/shard_map/all_to_all | solution.py:274
  7.2 2.2 %copy-start.5 = (f32[4,262144]{1,0:T(4,128)S(1)}, f32[4,262144]{1,0:T(4,128)}, u32[]{:S(2)}) copy-start(f32[4,262144]{1,0:T(4,128)} %e_ref.1) | copy-start | bytes 12582916
  13.0 1.4 copy-start.1
  14.4 50.7 %copy-start.6 = (s32[4]{0:T(128)S(1)}, s32[4]{0:T(128)}, u32[]{:S(2)}) copy-start(s32[4]{0:T(128)} %param.9) | copy-start | bytes 52
  14.4 50.7 %copy-start.7 = (s32[4]{0:T(128)S(1)}, s32[4]{0:T(128)}, u32[]{:S(2)}) copy-start(s32[4]{0:T(128)} %param.8) | copy-start | bytes 52
  56.2 40.4 %all-to-all-start.1 = ((s16[128,72,128]{2,1,0:T(8,128)(2,1)}), s16[128,72,128]{2,1,0:T(8,128)(2,1)S(1)}, u32[]{:S(2)}, u32[]{:S(2)}) async-start(s16[128,72,128]{2,1,0:T(8,128)(2,1)} %copy-done.1), calls=%async_computation.1 | async-start | bytes 4718592 | tf_op jit(solution)/shard_map/all_to_all | solution.py:274
  69.6 1.3 copy-start.2
  96.5 1.6 copy-start.3
  103.0 42.8 %copy-start.4 = (bf16[2048,512]{1,0:T(8,128)(2,1)S(1)}, bf16[2048,512]{1,0:T(8,128)(2,1)}, u32[]{:S(2)}) copy-start(bf16[2048,512]{1,0:T(8,128)(2,1)} %copy-done.2) | copy-start | bytes 6291460

commit v4 on v3

--- a/solution.py
+++ b/solution.py
@@ -6,6 +6,7 @@
 from jax.experimental import pallas as pl
 from jax.experimental.pallas import tpu as pltpu
 from jax.sharding import PartitionSpec as P
+
 
 PANELS = 4
 NB = 128
@@ -27,9 +28,9 @@
 KNEE = 6.0 / math.sinh(ASINH_TOP)
 ASINH_SCALE = 32767.0 / ASINH_TOP
 LN2 = math.log(2.0)
-T_STEPS = 258.0
-T_ZERO = 50.0 * T_STEPS
-ROWS = OWN * TILES + 8
+PLANES = 4
+HALVES = 2
+PLANE = DEVS // PLANES
 
 
 def signed(level, like):
@@ -51,25 +52,14 @@
     return (jnp.exp(angle) - jnp.exp(-angle)) * (0.5 * KNEE)
 
 
-def encode_triangle(x):
-    level = jnp.log(jnp.maximum(jnp.abs(x), 1e-30)) * (T_STEPS / LN2) + (T_ZERO + 0.5)
-    level = jnp.clip(level, 0.0, 32767.0).astype(jnp.int32)
-    return signed(level, x).astype(jnp.int16)
-
-
-def decode_triangle(code):
-    level = to_float(code)
-    size = jnp.exp((jnp.abs(level) - T_ZERO) * (LN2 / T_STEPS))
-    return jnp.where(level == 0.0, 0.0, signed(size, level)).astype(jnp.bfloat16)
-
-
 def power_of(most):
     return jnp.ceil(jnp.log(jnp.maximum(most, 1e-30)) * (8.0 / LN2) + 0.01)
 
 
 def levels(x, power):
-    size = jnp.sqrt(jnp.abs(x) * jnp.exp(power * (-LN2 / 8.0))) * 32767.0 + 0.5
-    return signed(size.astype(jnp.int32), x)
+    scaled = x * (jnp.exp(power * (-LN2 / 8.0)) * 32767.0**2)
+    root = scaled * lax.rsqrt(jnp.abs(scaled) + 1e-30)
+    return jnp.round(root).astype(jnp.int32)
 
 
 def unit_of(power):
@@ -85,32 +75,40 @@
     return high, (x - high.astype(jnp.float32)).astype(jnp.bfloat16)
 
 
-def encode_kernel(e_ref, t_ref, out_ref):
-    triangle = encode_triangle(t_ref[...].astype(jnp.float32))
-    for d in range(out_ref.shape[0]):
+def encode_kernel(z_ref, e_ref, out_ref):
+    for d in range(COLS):
         x = e_ref[:, d * SUB : (d + 1) * SUB]
         tall = jnp.concatenate([x[:, t * 128 : (t + 1) * 128] for t in range(TILES)], axis=0)
-        out_ref[d, 0 : OWN * TILES, :] = encode_value(tall)
-        out_ref[d, OWN * TILES : ROWS, :] = triangle
-
-
-def encode(eigvecs, triangle):
-    group = 8
+        out_ref[0, d] = encode_value(tall)
+
+
+def encode(eigvecs, z):
+    size = COLS * SUB
+
+    def source(k, a, b, z_ref):
+        return 0, (a * PLANES + lax.rem(z_ref[0] + k, PLANES)) * HALVES + b
+
     return pl.pallas_call(
         encode_kernel,
-        out_shape=jax.ShapeDtypeStruct((DEVS, ROWS, 128), jnp.int16),
-        grid=(DEVS // group,),
-        in_specs=[
-            pl.BlockSpec((OWN, group * SUB), lambda g: (0, g)),
-            pl.BlockSpec((8, NB), lambda g: (0, 0)),
-        ],
-        out_specs=pl.BlockSpec((group, ROWS, 128), lambda g: (g, 0, 0)),
+        out_shape=jax.ShapeDtypeStruct((PLANES, PLANE, OWN * TILES, 128), jnp.int16),
+        grid_spec=pltpu.PrefetchScalarGridSpec(
+            num_scalar_prefetch=1,
+            grid=(PLANES, HALVES, HALVES),
+            in_specs=[pl.BlockSpec((OWN, size), source)],
+            out_specs=pl.BlockSpec((1, COLS, OWN * TILES, 128), lambda k, a, b, z_ref: (k, a * HALVES + b, 0, 0)),
+        ),
         compiler_params=pltpu.CompilerParams(vmem_limit_bytes=ROOM),
         name="encode",
-    )(eigvecs, triangle)
-
-
-def gram_kernel(s_ref, slot_ref, gram_ref, refl_ref):
+    )(z, eigvecs)
+
+
+def gram_kernel(s_ref, slot_ref, *refs):
+    arrived, (gram_ref, out_ref, t_ref, refl_ref, held, sems) = refs[:COLS], refs[COLS:]
+    for k in range(COLS):
+        held[k] = arrived[k][0]
+    for p in range(PANELS):
+        t_ref[p] = held[s_ref[9 + p]]
+    copies = []
     gram = jnp.zeros((PANELS * NB, PANELS * NB), jnp.float32)
     for step in range(STEPS):
         row_ids = s_ref[8] + step * STEP + lax.broadcasted_iota(jnp.int32, (STEP, NB), 0)
@@ -122,6 +120,9 @@
             block = jnp.where(below > 0, slot_ref[s_ref[p], rows, :].astype(jnp.float32), unit)
             refl_ref[rows, p * NB : (p + 1) * NB] = block.astype(jnp.bfloat16)
         v = refl_ref[rows, :]
+        part = pl.ds(step * STEP, STEP)
+        copies.append(pltpu.make_async_copy(refl_ref.at[part], out_ref.at[part], sems.at[step]))
+        copies[-1].start()
         gram += dot32(v, v, ((0,), (0,)))
     blocks = [gram[q * NB : (q + 1) * NB, p * NB : (p + 1) * NB] for q, p in PAIRS]
     most = jnp.zeros((1, 1), jnp.float32)
@@ -131,39 +132,57 @@
     rows = [levels(block, power).astype(jnp.float32) for block in blocks]
     rows += [jnp.zeros((NB, NB), jnp.float32), jnp.broadcast_to(power, (NB, NB))]
     gram_ref[...] = jnp.swapaxes(jnp.stack(rows), 0, 1)
-
-
-def call(kernel, outs, ins, name, scalars=None, scratch=()):
-    spec = pl.BlockSpec(memory_space=pltpu.VMEM)
-    kept = [pltpu.with_memory_space_constraint(x, pltpu.VMEM) for x in ins]
+    for copy in copies:
+        copy.wait()
+
+
+def call(kernel, outs, ins, scalars=None, scratch=(), hbm_in=(), hbm_out=()):
+    spec, raw = pl.BlockSpec(memory_space=pltpu.VMEM), pl.BlockSpec(memory_space=pltpu.HBM)
+    kept = [pltpu.with_memory_space_constraint(x, pltpu.HBM if i in hbm_in else pltpu.VMEM) for i, x in enumerate(ins)]
     head = [] if scalars is None else [scalars]
     return pl.pallas_call(
         kernel,
-        out_shape=tuple(pltpu.VMEM(*out) for out in outs),
-        in_specs=[pl.BlockSpec(memory_space=pltpu.SMEM)] * len(head) + [spec] * len(kept),
-        out_specs=(spec,) * len(outs),
+        out_shape=tuple(pltpu.HBM(*out) if i in hbm_out else pltpu.VMEM(*out) for i, out in enumerate(outs)),
+        in_specs=[pl.BlockSpec(memory_space=pltpu.SMEM)] * len(head) + [raw if i in hbm_in else spec for i in range(len(ins))],
+        out_specs=tuple(raw if i in hbm_out else spec for i in range(len(outs))),
         scratch_shapes=list(scratch),
         compiler_params=pltpu.CompilerParams(vmem_limit_bytes=ROOM),
-        name=name,
     )(*head, *kept)
 
 
-def gram_of(scalars, slots):
-    outs = (((DEVS, 8, NB), jnp.float32), ((SUB, PANELS * NB), jnp.bfloat16))
-    return call(gram_kernel, outs, (slots,), "gram", scalars)
-
-
-def project_kernel(code_ref, refl_ref, gram_ref, pack_ref, high_ref, low_ref):
-    upper = lax.broadcasted_iota(jnp.int32, (DEVS // 2, 8, 128), 1) < OWN
-    for t in range(0, TILES, 2):
-        x = decode_value(code_ref[:, t * OWN : (t + 2) * OWN, :]).reshape(DEVS // 2, 2, 8, 128)
-        even, odd = x[:, 0], x[:, 1]
-        first = jnp.where(upper, even, pltpu.roll(odd, OWN, 1))
-        second = jnp.where(upper, pltpu.roll(even, OWN, 1), odd)
-        for k, tile in ((t, first), (t + 1, second)):
-            high, low = split(tile.reshape(K, 128))
-            high_ref[:, k * 128 : (k + 1) * 128] = high
-            low_ref[:, k * 128 : (k + 1) * 128] = low
+def gram_of(scalars, slots, triangles):
+    outs = (
+        ((DEVS, 8, NB), jnp.float32),
+        ((SUB, PANELS * NB), jnp.bfloat16),
+        ((PANELS, NB, NB), jnp.bfloat16),
+    )
+    scratch = [
+        pltpu.VMEM((SUB, PANELS * NB), jnp.bfloat16),
+        pltpu.VMEM((COLS, NB, NB), jnp.bfloat16),
+        pltpu.SemaphoreType.DMA((STEPS,)),
+    ]
+    return call(gram_kernel, outs, (slots, *triangles), scalars, scratch, hbm_out=(1,))
+
+
+def project_kernel(s_ref, code_ref, refl_hbm, gram_ref, pack_ref, high_ref, low_ref, refl_ref, sem):
+    fetch = pltpu.make_async_copy(refl_hbm, refl_ref, sem.at[0])
+    fetch.start()
+    upper = lax.broadcasted_iota(jnp.int32, (COLS // 2, 8, 128), 1) < OWN
+    for r in range(DEVS // COLS):
+        a, source, b = r // (PLANES * HALVES), r // HALVES % PLANES, r % HALVES
+        turn = lax.rem(s_ref[13] + (PLANES - source), PLANES)
+        rows = slice(r * COLS * OWN, (r + 1) * COLS * OWN)
+        for t in range(0, TILES, 2):
+            code = code_ref[(a * HALVES + b) * COLS : (a * HALVES + b + 1) * COLS, turn, t * OWN : (t + 2) * OWN, :]
+            x = decode_value(code).reshape(COLS // 2, 2, 8, 128)
+            even, odd = x[:, 0], x[:, 1]
+            first = jnp.where(upper, even, pltpu.roll(odd, OWN, 1))
+            second = jnp.where(upper, pltpu.roll(even, OWN, 1), odd)
+            for k, tile in ((t, first), (t + 1, second)):
+                high, low = split(tile.reshape(COLS * OWN, 128))
+                high_ref[rows, k * 128 : (k + 1) * 128] = high
+                low_ref[rows, k * 128 : (k + 1) * 128] = low
+    fetch.wait()
     v = refl_ref[...]
     part = dot32(high_ref[...], v) + dot32(low_ref[...], v)
     each = K // 16
@@ -177,9 +196,10 @@
         pack_ref[where, 16:24, :] = tail.astype(jnp.int32).astype(jnp.int16)
 
 
-def project(codes, refl, gram):
+def project(scalars, codes, refl, gram):
     outs = (((DEVS, PACK, NB), jnp.int16),) + (((K, SUB), jnp.bfloat16),) * 2
-    return call(project_kernel, outs, (codes, refl, gram), "project")
+    scratch = [pltpu.VMEM((SUB, PANELS * NB), jnp.bfloat16), pltpu.SemaphoreType.DMA((1,))]
+    return call(project_kernel, outs, (codes, refl, gram), scalars, scratch, hbm_in=(1,))
 
 
 def total_kernel(in_ref, out_ref):
@@ -197,10 +217,10 @@
 
 
 def total(parts):
-    return call(total_kernel, ((parts.shape, parts.dtype),), (parts,), "total")[0]
-
-
-def update_kernel(s_ref, sums_ref, code_ref, high_ref, low_ref, refl_ref, out_ref, c_high, c_low):
+    return call(total_kernel, ((parts.shape, parts.dtype),), (parts,))[0]
+
+
+def update_kernel(sums_ref, t_ref, high_ref, low_ref, refl_ref, out_ref, c_high, c_low):
     level = to_float(sums_ref[...])
     value = level * jnp.abs(level)
     proj = value[:, 0:16] * unit_of(level[:, 22:23])
@@ -212,8 +232,7 @@
         for q in range(p + 1, PANELS):
             (c1, c2), (g1, g2) = found[q], gram[(q, p)]
             rest -= dot32(c1, g1) + (dot32(c1, g2) + dot32(c2, g1))
-        kept = [code_ref[r * COLS + s_ref[p], OWN * TILES : ROWS, :] for r in range(DEVS // COLS)]
-        triangle = decode_triangle(jnp.concatenate(kept, axis=0))
+        triangle = t_ref[p]
         r1, r2 = split(rest)
         dims = ((1,), (1,))
         found[p] = split(dot32(r1, triangle, dims) + dot32(r2, triangle, dims))
@@ -235,10 +254,10 @@
             out_ref[c, at : at + 8, :] = jnp.broadcast_to(power, (8, 128)).astype(jnp.int32).astype(jnp.int16)
 
 
-def update(scalars, sums, codes, high, low, refl):
+def update(sums, triangles, high, low, refl):
     outs = (((COLS, TILES * WIDE + 8 * STEPS, 128), jnp.int16),)
     scratch = [pltpu.VMEM((K, PANELS * NB), jnp.bfloat16)] * 2
-    return call(update_kernel, outs, (sums, codes, high, low, refl), "update", scalars, scratch)[0]
+    return call(update_kernel, outs, (sums, triangles, high, low, refl), None, scratch)[0]
 
 
 def finish_kernel(code_ref, out_ref, rows, sems):
@@ -274,18 +293,47 @@
     return lax.all_to_all(x, axis, split_axis=0, concat_axis=0, tiled=True)
 
 
+def spread(x):
+    blocks = [x]
+    for k in range(1, COLS):
+        blocks.append(lax.ppermute(x, "col", [(c, c ^ k) for c in range(COLS)]))
+    return blocks
+
+
+def along_z(sent):
+    planes = [sent[0]]
+    for k in range(1, PLANES):
+        pairs = []
+        for r in range(DEVS // COLS):
+            z = r // HALVES % PLANES
+            pairs.append((r, r + ((z + k) % PLANES - z) * HALVES))
+        planes.append(lax.ppermute(sent[k], "row", pairs))
+    packed = jnp.concatenate(planes, axis=1)
+    return packed.reshape(PLANE, PLANES, OWN * TILES, 128)
+
+
+def within_plane(x):
+    groups = []
+    for z in range(PLANES):
+        rows = [r for r in range(DEVS // COLS) if r // HALVES % PLANES == z]
+        groups.append([r * COLS + c for r in rows for c in range(COLS)])
+    return lax.all_to_all(x, ALL, split_axis=0, concat_axis=0, tiled=True, axis_index_groups=groups)
+
+
 def local(eigvecs, panels, tfactors, owners, offsets):
     row, col = lax.axis_index("row"), lax.axis_index("col")
-    first = (row * COLS + col) * SUB
-    scalars = jnp.concatenate([owners, offsets, jnp.full((1,), first, jnp.int32)])
+    z = row // HALVES % PLANES
+    own = jnp.stack([(row * COLS + col) * SUB])
+    scalars = jnp.concatenate([owners, offsets, own, owners ^ col, jnp.stack([z])])
     slots = exchange(panels.reshape(COLS, SUB, NB), "col")
-    triangle = lax.dynamic_slice_in_dim(tfactors[0], row * 8, 8, 0)
-    sent, slots = lax.optimization_barrier((encode(eigvecs, triangle), slots))
-    codes = exchange(sent, ALL)
-    gram, refl = gram_of(scalars, slots)
-    pack, high, low = project(codes, refl, gram)
+    triangles = spread(tfactors)
+    planes = encode(eigvecs, jnp.stack([z]))
+    sent, slots = lax.optimization_barrier((along_z(planes), slots))
+    codes = within_plane(sent)
+    gram, refl, triangles = gram_of(scalars, slots, triangles)
+    pack, high, low = project(scalars, codes, refl, gram)
     sums = exchange(total(exchange(pack, ALL)), ALL)
-    out = update(scalars, sums, codes, high, low, refl)
+    out = update(sums, triangles, high, low, refl)
     return finish(exchange(out, "col"))
 
 

time: 189 us -> 197 us (1.042)
  starting transfers between devices: 16.1 us -> 33.7 us
  waiting for transfers between devices: 67.4 us -> 59.1 us
  local copies, waits for them, and re-layouts: 6.52 us -> 2.5 us
  blocking collectives: 75.1 us -> 77.1 us
    all_to_all x2 -> x1, waiting for transfers between devices: 67.4 us -> 11.8 us  [exchange(): return lax.all_to_all(x, axis, split_axis=0, concat_axis=0, tiled=True)]
    ppermute x0 -> x10, waiting for transfers between devices: none -> 47.3 us  [the longest x3 24.3 us: along_z(): planes.append(lax.ppermute(sent[k], 'row', pairs))]
    ppermute x0 -> x10, starting transfers between devices: none -> 21.3 us  [the longest x7 16 us: spread(): blocks.append(lax.ppermute(x, 'col', [(c, c ^ k) for c in range(COLS)]))]
    all_to_all x2 -> x1, starting transfers between devices: 16.1 us -> 7.04 us  [exchange(): return lax.all_to_all(x, axis, split_axis=0, concat_axis=0, tiled=True)]
    all_to_all x0 -> x1, starting transfers between devices: none -> 5.28 us  [within_plane(): lax.all_to_all(x, ALL, split_axis=0, concat_axis=0, tiled=True, axis_inde...]
    unnamed x16 -> x10, local copies, waits for them, and re-layouts: 6.51 us -> 2.2 us
  transfers between devices with their start and end apart: 2 -> 12, of which waited for: 2 -> 6; matrix products, arithmetic and copies ran while one was open for 0% -> 1% of each run, Pallas kernels for 4% -> 4%
where the time goes in v4:
time: 197 us; the launch traced here: 196 us
  blocking collectives  77.1 us (39%)
  waiting for transfers between devices  59.1 us (30%)
  starting transfers between devices  33.7 us (17%)
  Pallas kernels  22 us (11%)
  local copies, waits for them, and re-layouts  2.5 us (1%)
    all_to_all x3, blocking collectives, exchange(): return lax.all_to_all(x, axis, split_axis=0, concat_axis=0, tiled=True)  77.1 us
    ppermute x3, waiting for transfers between devices, along_z(): planes.append(lax.ppermute(sent[k], 'row', pairs))  24.3 us
    ppermute x7, waiting for transfers between devices, spread(): blocks.append(lax.ppermute(x, 'col', [(c, c ^ k) for c in range(COLS)]))  23 us
    pallas_call x4, Pallas kernels, call(): pl.pallas_call(kernel, out_shape=tuple((pltpu.HBM(*out) if i in hbm_out e...  16.3 us
    ppermute x7, starting transfers between devices, spread(): blocks.append(lax.ppermute(x, 'col', [(c, c ^ k) for c in range(COLS)]))  16 us
    all_to_all x1, waiting for transfers between devices, exchange(): return lax.all_to_all(x, axis, split_axis=0, concat_axis=0, tiled=True)  11.8 us
    all_to_all x1, starting transfers between devices, exchange(): return lax.all_to_all(x, axis, split_axis=0, concat_axis=0, tiled=True)  7.04 us
    ppermute x3, starting transfers between devices, along_z(): planes.append(lax.ppermute(sent[k], 'row', pairs))  5.37 us
  transfers between devices with their start and end apart: 12, of which 6 were waited for; matrix products, arithmetic and copies ran while one was open for 1% of the time, Pallas kernels for 4%

profile of v4, /device:TPU:0, one launch (start us, length us, event | category | flops | bytes accessed | tf_op | source)
XLA Modules:
  0.0 196.1 jit_solution(6392632580410628521)
XLA Ops:
  0.0 7.0 %all-to-all-start = ((bf16[8,2048,128]{2,1,0:T(8,128)(2,1)}), bf16[8,2048,128]{2,1,0:T(8,128)(2,1)}, u32[]{:S(2)}, u32[]{:S(2)}) async-start(bf16[8,2048,128]{2,1,0:T(8,128)(2,1)} %bitcast.13), calls=%async_computation | async-start | bytes 8388608 | tf_op jit(solution)/shard_map/all_to_all | solution.py:293
  7.0 2.2 %copy-done.1 = f32[4,262144]{1,0:T(4,128)S(1)} copy-done((f32[4,262144]{1,0:T(4,128)S(1)}, f32[4,262144]{1,0:T(4,128)}, u32[]{:S(2)}) %copy-start.1) | copy-done | bytes 4194328
  9.2 3.6 %encode.1 = s16[4,32,64,128]{3,2,1,0:T(8,128)(2,1)S(1)} custom-call(s32[1]{0:T(128)} %bitcast.1.z_ref, f32[4,262144]{1,0:T(4,128)S(1)} %copy-done.1), custom_call_target="tpu_custom_call" | custom-call | tf_op jit(solution)/shard_map/encode/pallas_call | solution.py:91
  12.9 0.2 slice_bitcast_fusion.3
  13.1 4.1 %collective-permute-start.2 = (s16[32,64,128]{2,1,0:T(8,128)(2,1)S(1)}, s16[32,64,128]{2,1,0:T(8,128)(2,1)S(1)}, u32[]{:S(2)}, u32[]{:S(2)}) collective-permute-start(s16[32,64,128]{2,1,0:T(8,128)(2,1)S(1)} %get-tuple-element.22), channel_id=1, source_target_pairs={{0,48},{8,56},{16,0},{24,8},{32,16},{40,24},{48,32},{56,40},{64,11... | collective-permute-start | bytes 1572872 | tf_op jit(solution)/shard_map/ppermute | solution.py:310
  17.2 0.0 collective-permute-start.1
  17.2 1.3 collective-permute-start
  18.5 20.9 %collective-permute-done.2 = s16[32,64,128]{2,1,0:T(8,128)(2,1)S(1)} collective-permute-done((s16[32,64,128]{2,1,0:T(8,128)(2,1)S(1)}, s16[32,64,128]{2,1,0:T(8,128)(2,1)S(1)}, u32[]{:S(2)}, u32[]{:S(2)}) %collective-permute-start.2) | collective-permute-done | bytes 524320 | tf_op jit(solution)/shard_map/ppermute | solution.py:310
  39.3 0.0 collective-permute-done.1
  39.3 3.4 %collective-permute-done = s16[32,64,128]{2,1,0:T(8,128)(2,1)S(1)} collective-permute-done((s16[32,64,128]{2,1,0:T(8,128)(2,1)S(1)}, s16[32,64,128]{2,1,0:T(8,128)(2,1)S(1)}, u32[]{:S(2)}, u32[]{:S(2)}) %collective-permute-start) | collective-permute-done | bytes 524320 | tf_op jit(solution)/shard_map/ppermute | solution.py:310
  42.7 1.5 pad_add_fusion
  44.2 11.8 %all-to-all-done.slot_ref = bf16[8,2048,128]{2,1,0:T(8,128)(2,1)} async-done(((bf16[8,2048,128]{2,1,0:T(8,128)(2,1)}), bf16[8,2048,128]{2,1,0:T(8,128)(2,1)}, u32[]{:S(2)}, u32[]{:S(2)}) %all-to-all-start) | async-done | bytes 4194336 | tf_op jit(solution)/shard_map/all_to_all | solution.py:293
  56.0 5.3 %all-to-all-start.1 = ((s16[32,4,64,128]{3,2,1,0:T(8,128)(2,1)}), s16[32,4,64,128]{3,2,1,0:T(8,128)(2,1)S(1)}, u32[]{:S(2)}, u32[]{:S(2)}) async-start(s16[32,4,64,128]{3,2,1,0:T(8,128)(2,1)} %bitcast.12), calls=%async_computation.1 | async-start | bytes 4194304 | tf_op jit(solution)/shard_map/all_to_all | solution.py:320
  61.3 5.8 %collective-permute-start.8 = (bf16[1,128,128]{2,1,0:T(8,128)(2,1)S(1)}, bf16[1,128,128]{2,1,0:T(8,128)(2,1)S(1)}, u32[]{:S(2)}, u32[]{:S(2)}) collective-permute-start(bf16[1,128,128]{2,1,0:T(8,128)(2,1)S(1)} %copy-done.2), channel_id=1, source_target_pairs={{0,6},{1,7},{2,4},{3,5},{4,2},{5,3},{6,0},{7,1},{8,14},{9,15},{10,... | collective-permute-start | bytes 98312 | tf_op jit(solution)/shard_map/ppermute | solution.py:299
  67.1 0.6 collective-permute-start.7
  67.7 3.0 %collective-permute-start.6 = (bf16[1,128,128]{2,1,0:T(8,128)(2,1)S(1)}, bf16[1,128,128]{2,1,0:T(8,128)(2,1)S(1)}, u32[]{:S(2)}, u32[]{:S(2)}) collective-permute-start(bf16[1,128,128]{2,1,0:T(8,128)(2,1)S(1)} %copy-done.2), channel_id=1, source_target_pairs={{0,4},{1,5},{2,6},{3,7},{4,0},{5,1},{6,2},{7,3},{8,12},{9,13},{10,... | collective-permute-start | bytes 98312 | tf_op jit(solution)/shard_map/ppermute | solution.py:299
  70.7 0.6 collective-permute-start.5
  71.2 3.0 %collective-permute-start.4 = (bf16[1,128,128]{2,1,0:T(8,128)(2,1)S(1)}, bf16[1,128,128]{2,1,0:T(8,128)(2,1)S(1)}, u32[]{:S(2)}, u32[]{:S(2)}) collective-permute-start(bf16[1,128,128]{2,1,0:T(8,128)(2,1)S(1)} %copy-done.2), channel_id=1, source_target_pairs={{0,2},{1,3},{2,0},{3,1},{4,6},{5,7},{6,4},{7,5},{8,10},{9,11},{10,... | collective-permute-start | bytes 98312 | tf_op jit(solution)/shard_map/ppermute | solution.py:299
  74.2 17.7 %collective-permute-done.8.refs_6_ = bf16[1,128,128]{2,1,0:T(8,128)(2,1)S(1)} collective-permute-done((bf16[1,128,128]{2,1,0:T(8,128)(2,1)S(1)}, bf16[1,128,128]{2,1,0:T(8,128)(2,1)S(1)}, u32[]{:S(2)}, u32[]{:S(2)}) %collective-permute-start.8) | collective-permute-done | bytes 32800 | tf_op jit(solution)/shard_map/ppermute | solution.py:299
  91.9 1.0 collective-permute-start.3
  92.9 2.1 %collective-permute-start.9 = (bf16[1,128,128]{2,1,0:T(8,128)(2,1)S(1)}, bf16[1,128,128]{2,1,0:T(8,128)(2,1)S(1)}, u32[]{:S(2)}, u32[]{:S(2)}) collective-permute-start(bf16[1,128,128]{2,1,0:T(8,128)(2,1)S(1)} %copy-done.2), channel_id=1, source_target_pairs={{0,7},{1,6},{2,5},{3,4},{4,3},{5,2},{6,1},{7,0},{8,15},{9,14},{10,... | collective-permute-start | bytes 98312 | tf_op jit(solution)/shard_map/ppermute | solution.py:299
  95.1 0.1 concatenate.6.s_ref
  95.2 0.7 collective-permute-done.3.refs_1_
  95.8 4.6 %collective-permute-done.9.refs_7_ = bf16[1,128,128]{2,1,0:T(8,128)(2,1)S(1)} collective-permute-done((bf16[1,128,128]{2,1,0:T(8,128)(2,1)S(1)}, bf16[1,128,128]{2,1,0:T(8,128)(2,1)S(1)}, u32[]{:S(2)}, u32[]{:S(2)}) %collective-permute-start.9) | collective-permute-done | bytes 32800 | tf_op jit(solution)/shard_map/ppermute | solution.py:299
  100.4 4.7 %shard_map.55 = (f32[128,8,128]{2,1,0:T(8,128)S(1)}, bf16[2048,512]{1,0:T(8,128)(2,1)}, bf16[4,128,128]{2,1,0:T(8,128)(2,1)S(1)}) custom-call(s32[14]{0:T(128)S(1)} %concatenate.6.s_ref, bf16[8,2048,128]{2,1,0:T(8,128)(2,1)} %all-to-all-done.slot_ref, bf16[1,128,128]{2,1,0:T(8,128)(2,1)S(1)} %copy-done.2, ...), custom_call_target="tpu_custom_call" | custom-call | tf_op jit(solution)/shard_map/pallas_call | solution.py:143
  105.2 5.7 %shard_map.56 = (s16[128,24,128]{2,1,0:T(8,128)(2,1)S(1)}, bf16[512,2048]{1,0:T(8,128)(2,1)S(1)}, bf16[512,2048]{1,0:T(8,128)(2,1)S(1)}) custom-call(s32[14]{0:T(128)S(1)} %concatenate.6.s_ref, s16[32,4,64,128]{3,2,1,0:T(8,128)(2,1)S(1)} %all-to-all-done.1.code_ref, bf16[2048,512]{1,0:T(8,128)(2,1)} %get-tuple-element.15.refl_hbm.refl_ref, ...), custom_call_target="tpu_custom_call" | custom-call | tf_op jit(solution)/shard_map/pallas_call | solution.py:143
  110.9 23.1 %all_to_all.25.in_ref = s16[128,24,128]{2,1,0:T(8,128)(2,1)S(1)} all-to-all(s16[128,24,128]{2,1,0:T(8,128)(2,1)S(1)} %get-tuple-element.17), channel_id=1, replica_groups=mesh['row'=16,'col'=8] {'row','col'}, dimensions={0} | all-to-all | bytes 1572864 | tf_op jit(solution)/shard_map/all_to_all | solution.py:293
  134.0 0.9 shard_map.57
  134.9 20.7 %all_to_all.26.sums_ref = s16[128,24,128]{2,1,0:T(8,128)(2,1)S(1)} all-to-all(s16[128,24,128]{2,1,0:T(8,128)(2,1)S(1)} %shard_map.57), channel_id=1, replica_groups=mesh['row'=16,'col'=8] {'row','col'}, dimensions={0} | all-to-all | bytes 1572864 | tf_op jit(solution)/shard_map/all_to_all | solution.py:293
  155.6 4.9 %shard_map.58 = s16[8,1056,128]{2,1,0:T(8,128)(2,1)S(1)} custom-call(s16[128,24,128]{2,1,0:T(8,128)(2,1)S(1)} %all_to_all.26.sums_ref, bf16[4,128,128]{2,1,0:T(8,128)(2,1)S(1)} %get-tuple-element.18.t_ref, bf16[512,2048]{1,0:T(8,128)(2,1)S(1)} %get-tuple-element.19.high_ref, bf16[512,2048]{1,0:T(8,128)(2,1)S(1)} %get-tuple-element.20.low_ref, ...), custom_call_target="tpu_custom_call" | custom-call | tf_op jit(solution)/shard_map/pallas_call | solution.py:143
  160.6 33.2 %all_to_all.27.code_ref = s16[8,1056,128]{2,1,0:T(8,128)(2,1)S(1)} all-to-all(s16[8,1056,128]{2,1,0:T(8,128)(2,1)S(1)} %shard_map.58), channel_id=1, replica_groups=mesh['row'=16,'col'=8] {'col'}, dimensions={0} | all-to-all | bytes 4325376 | tf_op jit(solution)/shard_map/all_to_all | solution.py:293
  193.8 2.2 %finish.1 = f32[64,16384]{1,0:T(8,128)} custom-call(s16[8,1056,128]{2,1,0:T(8,128)(2,1)S(1)} %all_to_all.27.code_ref), custom_call_target="tpu_custom_call" | custom-call | tf_op jit(solution)/shard_map/finish/pallas_call | solution.py:281
  (15 shorter events, 0.0 us)
Async XLA Ops:
  0.0 56.0 %all-to-all-start = ((bf16[8,2048,128]{2,1,0:T(8,128)(2,1)}), bf16[8,2048,128]{2,1,0:T(8,128)(2,1)}, u32[]{:S(2)}, u32[]{:S(2)}) async-start(bf16[8,2048,128]{2,1,0:T(8,128)(2,1)} %bitcast.13), calls=%async_computation | async-start | bytes 8388608 | tf_op jit(solution)/shard_map/all_to_all | solution.py:293
  7.0 2.2 %copy-start.1 = (f32[4,262144]{1,0:T(4,128)S(1)}, f32[4,262144]{1,0:T(4,128)}, u32[]{:S(2)}) copy-start(f32[4,262144]{1,0:T(4,128)} %e_ref.1) | copy-start | bytes 12582916
  13.1 26.2 %collective-permute-start.2 = (s16[32,64,128]{2,1,0:T(8,128)(2,1)S(1)}, s16[32,64,128]{2,1,0:T(8,128)(2,1)S(1)}, u32[]{:S(2)}, u32[]{:S(2)}) collective-permute-start(s16[32,64,128]{2,1,0:T(8,128)(2,1)S(1)} %get-tuple-element.22), channel_id=1, source_target_pairs={{0,48},{8,56},{16,0},{24,8},{32,16},{40,24},{48,32},{56,40},{64,11... | collective-permute-start | bytes 1572872 | tf_op jit(solution)/shard_map/ppermute | solution.py:310
  17.2 22.1 %collective-permute-start.1 = (s16[32,64,128]{2,1,0:T(8,128)(2,1)S(1)}, s16[32,64,128]{2,1,0:T(8,128)(2,1)S(1)}, u32[]{:S(2)}, u32[]{:S(2)}) collective-permute-start(s16[32,64,128]{2,1,0:T(8,128)(2,1)S(1)} %get-tuple-element.23), channel_id=1, source_target_pairs={{0,32},{8,40},{16,48},{24,56},{32,0},{40,8},{48,16},{56,24},{64,96... | collective-permute-start | bytes 1572872 | tf_op jit(solution)/shard_map/ppermute | solution.py:310
  17.2 25.5 %collective-permute-start = (s16[32,64,128]{2,1,0:T(8,128)(2,1)S(1)}, s16[32,64,128]{2,1,0:T(8,128)(2,1)S(1)}, u32[]{:S(2)}, u32[]{:S(2)}) collective-permute-start(s16[32,64,128]{2,1,0:T(8,128)(2,1)S(1)} %get-tuple-element.24), channel_id=1, source_target_pairs={{0,16},{8,24},{16,32},{24,40},{32,48},{40,56},{48,0},{56,8},{64,80... | collective-permute-start | bytes 1572872 | tf_op jit(solution)/shard_map/ppermute | solution.py:310
  56.0 5.3 %copy-start.2 = (bf16[1,128,128]{2,1,0:T(8,128)(2,1)S(1)}, bf16[1,128,128]{2,1,0:T(8,128)(2,1)}, u32[]{:S(2)}) copy-start(bf16[1,128,128]{2,1,0:T(8,128)(2,1)} %refs_0_.1) | copy-start | bytes 98308
  56.0 39.0 %copy-start.3 = (s32[4]{0:T(128)S(1)}, s32[4]{0:T(128)}, u32[]{:S(2)}) copy-start(s32[4]{0:T(128)} %param.8) | copy-start | bytes 52
  56.0 39.0 %copy-start.4 = (s32[4]{0:T(128)S(1)}, s32[4]{0:T(128)}, u32[]{:S(2)}) copy-start(s32[4]{0:T(128)} %param.9) | copy-start | bytes 52
  56.0 49.1 %all-to-all-start.1 = ((s16[32,4,64,128]{3,2,1,0:T(8,128)(2,1)}), s16[32,4,64,128]{3,2,1,0:T(8,128)(2,1)S(1)}, u32[]{:S(2)}, u32[]{:S(2)}) async-start(s16[32,4,64,128]{3,2,1,0:T(8,128)(2,1)} %bitcast.12), calls=%async_computation.1 | async-start | bytes 4194304 | tf_op jit(solution)/shard_map/all_to_all | solution.py:320
  61.3 30.6 %collective-permute-start.8 = (bf16[1,128,128]{2,1,0:T(8,128)(2,1)S(1)}, bf16[1,128,128]{2,1,0:T(8,128)(2,1)S(1)}, u32[]{:S(2)}, u32[]{:S(2)}) collective-permute-start(bf16[1,128,128]{2,1,0:T(8,128)(2,1)S(1)} %copy-done.2), channel_id=1, source_target_pairs={{0,6},{1,7},{2,4},{3,5},{4,2},{5,3},{6,0},{7,1},{8,14},{9,15},{10,... | collective-permute-start | bytes 98312 | tf_op jit(solution)/shard_map/ppermute | solution.py:299
  67.1 25.8 %collective-permute-start.7 = (bf16[1,128,128]{2,1,0:T(8,128)(2,1)S(1)}, bf16[1,128,128]{2,1,0:T(8,128)(2,1)S(1)}, u32[]{:S(2)}, u32[]{:S(2)}) collective-permute-start(bf16[1,128,128]{2,1,0:T(8,128)(2,1)S(1)} %copy-done.2), channel_id=1, source_target_pairs={{0,5},{1,4},{2,7},{3,6},{4,1},{5,0},{6,3},{7,2},{8,13},{9,12},{10,... | collective-permute-start | bytes 98312 | tf_op jit(solution)/shard_map/ppermute | solution.py:299
  67.7 27.5 %collective-permute-start.6 = (bf16[1,128,128]{2,1,0:T(8,128)(2,1)S(1)}, bf16[1,128,128]{2,1,0:T(8,128)(2,1)S(1)}, u32[]{:S(2)}, u32[]{:S(2)}) collective-permute-start(bf16[1,128,128]{2,1,0:T(8,128)(2,1)S(1)} %copy-done.2), channel_id=1, source_target_pairs={{0,4},{1,5},{2,6},{3,7},{4,0},{5,1},{6,2},{7,3},{8,12},{9,13},{10,... | collective-permute-start | bytes 98312 | tf_op jit(solution)/shard_map/ppermute | solution.py:299
  70.7 24.5 %collective-permute-start.5 = (bf16[1,128,128]{2,1,0:T(8,128)(2,1)S(1)}, bf16[1,128,128]{2,1,0:T(8,128)(2,1)S(1)}, u32[]{:S(2)}, u32[]{:S(2)}) collective-permute-start(bf16[1,128,128]{2,1,0:T(8,128)(2,1)S(1)} %copy-done.2), channel_id=1, source_target_pairs={{0,3},{1,2},{2,1},{3,0},{4,7},{5,6},{6,5},{7,4},{8,11},{9,10},{10,... | collective-permute-start | bytes 98312 | tf_op jit(solution)/shard_map/ppermute | solution.py:299
  71.2 23.9 %collective-permute-start.4 = (bf16[1,128,128]{2,1,0:T(8,128)(2,1)S(1)}, bf16[1,128,128]{2,1,0:T(8,128)(2,1)S(1)}, u32[]{:S(2)}, u32[]{:S(2)}) collective-permute-start(bf16[1,128,128]{2,1,0:T(8,128)(2,1)S(1)} %copy-done.2), channel_id=1, source_target_pairs={{0,2},{1,3},{2,0},{3,1},{4,6},{5,7},{6,4},{7,5},{8,10},{9,11},{10,... | collective-permute-start | bytes 98312 | tf_op jit(solution)/shard_map/ppermute | solution.py:299
  91.9 3.9 %collective-permute-start.3 = (bf16[1,128,128]{2,1,0:T(8,128)(2,1)S(1)}, bf16[1,128,128]{2,1,0:T(8,128)(2,1)S(1)}, u32[]{:S(2)}, u32[]{:S(2)}) collective-permute-start(bf16[1,128,128]{2,1,0:T(8,128)(2,1)S(1)} %copy-done.2), channel_id=1, source_target_pairs={{0,1},{1,0},{2,3},{3,2},{4,5},{5,4},{6,7},{7,6},{8,9},{9,8},{10,11... | collective-permute-start | bytes 98312 | tf_op jit(solution)/shard_map/ppermute | solution.py:299
  92.9 7.5 %collective-permute-start.9 = (bf16[1,128,128]{2,1,0:T(8,128)(2,1)S(1)}, bf16[1,128,128]{2,1,0:T(8,128)(2,1)S(1)}, u32[]{:S(2)}, u32[]{:S(2)}) collective-permute-start(bf16[1,128,128]{2,1,0:T(8,128)(2,1)S(1)} %copy-done.2), channel_id=1, source_target_pairs={{0,7},{1,6},{2,5},{3,4},{4,3},{5,2},{6,1},{7,0},{8,15},{9,14},{10,... | collective-permute-start | bytes 98312 | tf_op jit(solution)/shard_map/ppermute | solution.py:299
  110.9 44.7 %copy-start = (bf16[2048,512]{1,0:T(8,128)(2,1)S(1)}, bf16[2048,512]{1,0:T(8,128)(2,1)}, u32[]{:S(2)}) copy-start(bf16[2048,512]{1,0:T(8,128)(2,1)} %get-tuple-element.15.refl_hbm.refl_ref) | copy-start | bytes 6291460

commit v5 on v4

--- a/solution.py
+++ b/solution.py
@@ -27,10 +27,12 @@
 ASINH_TOP = 12.5
 KNEE = 6.0 / math.sinh(ASINH_TOP)
 ASINH_SCALE = 32767.0 / ASINH_TOP
+GAIN = 2.0 / KNEE
 LN2 = math.log(2.0)
 PLANES = 4
 HALVES = 2
-PLANE = DEVS // PLANES
+SHARES = PLANES * HALVES
+SHEET = DEVS // SHARES
 
 
 def signed(level, like):
@@ -48,8 +50,8 @@
 
 
 def decode_value(code):
-    angle = to_float(code) * (1.0 / ASINH_SCALE)
-    return (jnp.exp(angle) - jnp.exp(-angle)) * (0.5 * KNEE)
+    angle = to_float(code) * (1.0 / (ASINH_SCALE * LN2))
+    return jnp.exp2(angle) - jnp.exp2(-angle)
 
 
 def power_of(most):
@@ -75,31 +77,32 @@
     return high, (x - high.astype(jnp.float32)).astype(jnp.bfloat16)
 
 
-def encode_kernel(z_ref, e_ref, out_ref):
+def encode_kernel(place_ref, e_ref, out_ref):
     for d in range(COLS):
         x = e_ref[:, d * SUB : (d + 1) * SUB]
         tall = jnp.concatenate([x[:, t * 128 : (t + 1) * 128] for t in range(TILES)], axis=0)
         out_ref[0, d] = encode_value(tall)
 
 
-def encode(eigvecs, z):
+def encode(eigvecs, place):
     size = COLS * SUB
 
-    def source(k, a, b, z_ref):
-        return 0, (a * PLANES + lax.rem(z_ref[0] + k, PLANES)) * HALVES + b
+    def source(k, h, a, place_ref):
+        z = lax.rem(place_ref[0] + k, PLANES)
+        return 0, (a * PLANES + z) * HALVES + lax.rem(place_ref[1] + h, HALVES)
 
     return pl.pallas_call(
         encode_kernel,
-        out_shape=jax.ShapeDtypeStruct((PLANES, PLANE, OWN * TILES, 128), jnp.int16),
+        out_shape=jax.ShapeDtypeStruct((SHARES, SHEET, OWN * TILES, 128), jnp.int16),
         grid_spec=pltpu.PrefetchScalarGridSpec(
             num_scalar_prefetch=1,
-            grid=(PLANES, HALVES, HALVES),
+            grid=(PLANES, HALVES, SHEET // COLS),
             in_specs=[pl.BlockSpec((OWN, size), source)],
-            out_specs=pl.BlockSpec((1, COLS, OWN * TILES, 128), lambda k, a, b, z_ref: (k, a * HALVES + b, 0, 0)),
+            out_specs=pl.BlockSpec((1, COLS, OWN * TILES, 128), lambda k, h, a, place_ref: (k * HALVES + h, a, 0, 0)),
         ),
         compiler_params=pltpu.CompilerParams(vmem_limit_bytes=ROOM),
         name="encode",
-    )(z, eigvecs)
+    )(place, eigvecs)
 
 
 def gram_kernel(s_ref, slot_ref, *refs):
@@ -169,11 +172,11 @@
     fetch.start()
     upper = lax.broadcasted_iota(jnp.int32, (COLS // 2, 8, 128), 1) < OWN
     for r in range(DEVS // COLS):
-        a, source, b = r // (PLANES * HALVES), r // HALVES % PLANES, r % HALVES
-        turn = lax.rem(s_ref[13] + (PLANES - source), PLANES)
+        a, source, b = r // SHARES, r // HALVES % PLANES, r % HALVES
+        share = lax.rem(s_ref[13] + (PLANES - source), PLANES) * HALVES + lax.rem(s_ref[14] + b, HALVES)
         rows = slice(r * COLS * OWN, (r + 1) * COLS * OWN)
         for t in range(0, TILES, 2):
-            code = code_ref[(a * HALVES + b) * COLS : (a * HALVES + b + 1) * COLS, turn, t * OWN : (t + 2) * OWN, :]
+            code = code_ref[a * COLS : (a + 1) * COLS, share, t * OWN : (t + 2) * OWN, :]
             x = decode_value(code).reshape(COLS // 2, 2, 8, 128)
             even, odd = x[:, 0], x[:, 1]
             first = jnp.where(upper, even, pltpu.roll(odd, OWN, 1))
@@ -217,11 +220,15 @@
 
 
 def total(parts):
-    return call(total_kernel, ((parts.shape, parts.dtype),), (parts,))[0]
-
-
-def update_kernel(sums_ref, t_ref, high_ref, low_ref, refl_ref, out_ref, c_high, c_low):
-    level = to_float(sums_ref[...])
+    return call(total_kernel, (((DEVS // HALVES, PACK, NB), parts.dtype),), (parts,))[0]
+
+
+def update_kernel(s_ref, mine_ref, other_ref, t_ref, high_ref, low_ref, refl_ref, out_ref, c_high, c_low):
+    mine, other = to_float(mine_ref[...]), to_float(other_ref[...])
+    first = s_ref[14] == 0
+    halves = (jnp.where(first, mine, other), jnp.where(first, other, mine))
+    shape = (DEVS // COLS // HALVES, COLS, PACK, NB)
+    level = jnp.stack([half.reshape(shape) for half in halves], axis=1).reshape(DEVS, PACK, NB)
     value = level * jnp.abs(level)
     proj = value[:, 0:16] * unit_of(level[:, 22:23])
     blocks = jnp.swapaxes(value[:, 16:24] * unit_of(level[:, 23:24]), 0, 1)
@@ -254,10 +261,10 @@
             out_ref[c, at : at + 8, :] = jnp.broadcast_to(power, (8, 128)).astype(jnp.int32).astype(jnp.int16)
 
 
-def update(sums, triangles, high, low, refl):
+def update(scalars, mine, other, triangles, high, low, refl):
     outs = (((COLS, TILES * WIDE + 8 * STEPS, 128), jnp.int16),)
     scratch = [pltpu.VMEM((K, PANELS * NB), jnp.bfloat16)] * 2
-    return call(update_kernel, outs, (sums, triangles, high, low, refl), None, scratch)[0]
+    return call(update_kernel, outs, (mine, other, triangles, high, low, refl), scalars, scratch)[0]
 
 
 def finish_kernel(code_ref, out_ref, rows, sems):
@@ -265,7 +272,7 @@
     for c in range(COLS):
         for k in range(STEPS):
             at = TILES * WIDE + 8 * k
-            unit = unit_of(to_float(code_ref[c, at : at + 8, :]))
+            unit = unit_of(to_float(code_ref[c, at : at + 8, :])) * (1.0 / GAIN)
             unit = jnp.concatenate([unit] * (WIDE // 8), axis=0)
             for t in range(k * (STEP // 128), (k + 1) * (STEP // 128)):
                 level = to_float(code_ref[c, t * WIDE : (t + 1) * WIDE, :])
@@ -300,40 +307,42 @@
     return blocks
 
 
-def along_z(sent):
-    planes = [sent[0]]
-    for k in range(1, PLANES):
+def across(sent):
+    shares = [sent[0]]
+    for share in range(1, SHARES):
+        k, h = share // HALVES, share % HALVES
         pairs = []
         for r in range(DEVS // COLS):
-            z = r // HALVES % PLANES
-            pairs.append((r, r + ((z + k) % PLANES - z) * HALVES))
-        planes.append(lax.ppermute(sent[k], "row", pairs))
-    packed = jnp.concatenate(planes, axis=1)
-    return packed.reshape(PLANE, PLANES, OWN * TILES, 128)
-
-
-def within_plane(x):
+            z, core = r // HALVES % PLANES, r % HALVES
+            pairs.append((r, r + ((z + k) % PLANES - z) * HALVES + (core + h) % HALVES - core))
+        shares.append(lax.ppermute(sent[share], "row", pairs))
+    packed = jnp.concatenate(shares, axis=1)
+    return packed.reshape(SHEET, SHARES, OWN * TILES, 128)
+
+
+def within(x, size):
     groups = []
-    for z in range(PLANES):
-        rows = [r for r in range(DEVS // COLS) if r // HALVES % PLANES == z]
+    for share in range(size):
+        rows = [r for r in range(DEVS // COLS) if r % size == share]
         groups.append([r * COLS + c for r in rows for c in range(COLS)])
     return lax.all_to_all(x, ALL, split_axis=0, concat_axis=0, tiled=True, axis_index_groups=groups)
 
 
 def local(eigvecs, panels, tfactors, owners, offsets):
     row, col = lax.axis_index("row"), lax.axis_index("col")
-    z = row // HALVES % PLANES
+    place = jnp.stack([row // HALVES % PLANES, row % HALVES])
     own = jnp.stack([(row * COLS + col) * SUB])
-    scalars = jnp.concatenate([owners, offsets, own, owners ^ col, jnp.stack([z])])
+    scalars = jnp.concatenate([owners, offsets, own, owners ^ col, place])
     slots = exchange(panels.reshape(COLS, SUB, NB), "col")
     triangles = spread(tfactors)
-    planes = encode(eigvecs, jnp.stack([z]))
-    sent, slots = lax.optimization_barrier((along_z(planes), slots))
-    codes = within_plane(sent)
+    planes = encode(eigvecs, place)
+    sent, slots = lax.optimization_barrier((across(planes), slots))
+    codes = within(sent, SHARES)
     gram, refl, triangles = gram_of(scalars, slots, triangles)
     pack, high, low = project(scalars, codes, refl, gram)
-    sums = exchange(total(exchange(pack, ALL)), ALL)
-    out = update(sums, triangles, high, low, refl)
+    mine = within(total(exchange(pack, ALL)), HALVES)
+    other = lax.ppermute(mine, "row", [(r, r ^ 1) for r in range(DEVS // COLS)])
+    out = update(scalars, mine, other, triangles, high, low, refl)
     return finish(exchange(out, "col"))
 
 

time: 197 us -> 190 us (0.964)
  blocking collectives: 77.1 us -> 71.1 us
  starting transfers between devices: 33.7 us -> 36.2 us
  waiting for transfers between devices: 59.1 us -> 56.9 us
    all_to_all x3 -> x2, blocking collectives: 77.1 us -> 54.2 us  [exchange(): return lax.all_to_all(x, axis, split_axis=0, concat_axis=0, tiled=True)]
    all_to_all x0 -> x1, blocking collectives: none -> 16.9 us  [within(): lax.all_to_all(x, ALL, split_axis=0, concat_axis=0, tiled=True, axis_inde...]
    ppermute x3 -> x8, starting transfers between devices: 5.37 us -> 9.11 us  [the longest x7 9.11 us: across(): shares.append(lax.ppermute(sent[share], 'row', pairs))]
    ppermute x3 -> x8, waiting for transfers between devices: 24.3 us -> 21.1 us  [the longest x7 19.4 us: across(): shares.append(lax.ppermute(sent[share], 'row', pairs))]
  transfers between devices with their start and end apart: 12 -> 17, of which waited for: 6 -> 10; matrix products, arithmetic and copies ran while one was open for 1% -> 0% of each run, Pallas kernels for 4% -> 5%
where the time goes in v5:
time: 190 us
  blocking collectives  71.1 us (37%)
  waiting for transfers between devices  56.9 us (30%)
  starting transfers between devices  36.2 us (19%)
  Pallas kernels  22.7 us (12%)
  local copies, waits for them, and re-layouts  2.72 us (1%)
    all_to_all x2, blocking collectives, exchange(): return lax.all_to_all(x, axis, split_axis=0, concat_axis=0, tiled=True)  54.2 us
    ppermute x7, waiting for transfers between devices, spread(): blocks.append(lax.ppermute(x, 'col', [(c, c ^ k) for c in range(COLS)]))  22.2 us
    ppermute x7, waiting for transfers between devices, across(): shares.append(lax.ppermute(sent[share], 'row', pairs))  19.4 us
    all_to_all x1, blocking collectives, within(): lax.all_to_all(x, ALL, split_axis=0, concat_axis=0, tiled=True, axis_inde...  16.9 us
    pallas_call x4, Pallas kernels, call(): pl.pallas_call(kernel, out_shape=tuple((pltpu.HBM(*out) if i in hbm_out e...  16.3 us
    ppermute x7, starting transfers between devices, spread(): blocks.append(lax.ppermute(x, 'col', [(c, c ^ k) for c in range(COLS)]))  15 us
    all_to_all x1, waiting for transfers between devices, exchange(): return lax.all_to_all(x, axis, split_axis=0, concat_axis=0, tiled=True)  13.5 us
    ppermute x7, starting transfers between devices, across(): shares.append(lax.ppermute(sent[share], 'row', pairs))  9.11 us
  transfers between devices with their start and end apart: 17, of which 10 were waited for; matrix products, arithmetic and copies ran while one was open for 0% of the time, Pallas kernels for 5%

profile of v5, /device:TPU:0, one launch (start us, length us, event | category | flops | bytes accessed | tf_op | source)
XLA Modules:
  0.0 190.0 jit_solution(14143946857374226782)
XLA Ops:
  0.0 7.0 %all-to-all-start = ((bf16[8,2048,128]{2,1,0:T(8,128)(2,1)}), bf16[8,2048,128]{2,1,0:T(8,128)(2,1)}, u32[]{:S(2)}, u32[]{:S(2)}) async-start(bf16[8,2048,128]{2,1,0:T(8,128)(2,1)} %bitcast.23), calls=%async_computation | async-start | bytes 8388608 | tf_op jit(solution)/shard_map/all_to_all | solution.py:300
  7.1 2.2 %copy-done.1 = f32[4,262144]{1,0:T(4,128)S(1)} copy-done((f32[4,262144]{1,0:T(4,128)S(1)}, f32[4,262144]{1,0:T(4,128)}, u32[]{:S(2)}) %copy-start.1) | copy-done | bytes 4194328
  9.3 4.2 %encode.1 = s16[8,16,64,128]{3,2,1,0:T(8,128)(2,1)S(1)} custom-call(s32[2]{0:T(128)S(1)} %pad_add_fusion.place_ref, f32[4,262144]{1,0:T(4,128)S(1)} %copy-done.1), custom_call_target="tpu_custom_call" | custom-call | tf_op jit(solution)/shard_map/encode/pallas_call | solution.py:94
  13.8 2.0 %collective-permute-start.1 = (s16[16,64,128]{2,1,0:T(8,128)(2,1)S(1)}, s16[16,64,128]{2,1,0:T(8,128)(2,1)S(1)}, u32[]{:S(2)}, u32[]{:S(2)}) collective-permute-start(s16[16,64,128]{2,1,0:T(8,128)(2,1)S(1)} %get-tuple-element.26), channel_id=1, source_target_pairs={{0,16},{8,24},{16,32},{24,40},{32,48},{40,56},{48,0},{56,8},{64,80... | collective-permute-start | bytes 786440 | tf_op jit(solution)/shard_map/ppermute | solution.py:318
  15.8 1.7 collective-permute-start.2
  17.4 1.9 %collective-permute-start.3 = (s16[16,64,128]{2,1,0:T(8,128)(2,1)S(1)}, s16[16,64,128]{2,1,0:T(8,128)(2,1)S(1)}, u32[]{:S(2)}, u32[]{:S(2)}) collective-permute-start(s16[16,64,128]{2,1,0:T(8,128)(2,1)S(1)} %get-tuple-element.24), channel_id=1, source_target_pairs={{0,32},{8,40},{16,48},{24,56},{32,0},{40,8},{48,16},{56,24},{64,96... | collective-permute-start | bytes 786440 | tf_op jit(solution)/shard_map/ppermute | solution.py:318
  19.4 1.3 collective-permute-start.4
  20.7 1.4 collective-permute-start.5
  22.1 2.9 %collective-permute-done.1 = s16[16,64,128]{2,1,0:T(8,128)(2,1)S(1)} collective-permute-done((s16[16,64,128]{2,1,0:T(8,128)(2,1)S(1)}, s16[16,64,128]{2,1,0:T(8,128)(2,1)S(1)}, u32[]{:S(2)}, u32[]{:S(2)}) %collective-permute-start.1) | collective-permute-done | bytes 262176 | tf_op jit(solution)/shard_map/ppermute | solution.py:318
  25.0 0.8 collective-permute-start.6
  25.8 4.3 %collective-permute-done.2 = s16[16,64,128]{2,1,0:T(8,128)(2,1)S(1)} collective-permute-done((s16[16,64,128]{2,1,0:T(8,128)(2,1)S(1)}, s16[16,64,128]{2,1,0:T(8,128)(2,1)S(1)}, u32[]{:S(2)}, u32[]{:S(2)}) %collective-permute-start.2) | collective-permute-done | bytes 262176 | tf_op jit(solution)/shard_map/ppermute | solution.py:318
  30.2 7.6 %collective-permute-done.3 = s16[16,64,128]{2,1,0:T(8,128)(2,1)S(1)} collective-permute-done((s16[16,64,128]{2,1,0:T(8,128)(2,1)S(1)}, s16[16,64,128]{2,1,0:T(8,128)(2,1)S(1)}, u32[]{:S(2)}, u32[]{:S(2)}) %collective-permute-start.3) | collective-permute-done | bytes 262176 | tf_op jit(solution)/shard_map/ppermute | solution.py:318
  37.8 4.5 %collective-permute-done.4 = s16[16,64,128]{2,1,0:T(8,128)(2,1)S(1)} collective-permute-done((s16[16,64,128]{2,1,0:T(8,128)(2,1)S(1)}, s16[16,64,128]{2,1,0:T(8,128)(2,1)S(1)}, u32[]{:S(2)}, u32[]{:S(2)}) %collective-permute-start.4) | collective-permute-done | bytes 262176 | tf_op jit(solution)/shard_map/ppermute | solution.py:318
  42.5 13.5 %all-to-all-done.slot_ref = bf16[8,2048,128]{2,1,0:T(8,128)(2,1)} async-done(((bf16[8,2048,128]{2,1,0:T(8,128)(2,1)}), bf16[8,2048,128]{2,1,0:T(8,128)(2,1)}, u32[]{:S(2)}, u32[]{:S(2)}) %all-to-all-start) | async-done | bytes 4194336 | tf_op jit(solution)/shard_map/all_to_all | solution.py:300
  56.0 5.0 %all-to-all-start.1 = ((s16[16,8,64,128]{3,2,1,0:T(8,128)(2,1)}), s16[16,8,64,128]{3,2,1,0:T(8,128)(2,1)S(1)}, u32[]{:S(2)}, u32[]{:S(2)}) async-start(s16[16,8,64,128]{3,2,1,0:T(8,128)(2,1)} %bitcast.24), calls=%async_computation.1 | async-start | bytes 4194304 | tf_op jit(solution)/shard_map/all_to_all | solution.py:328
  61.1 3.5 %collective-permute-start.10 = (bf16[1,128,128]{2,1,0:T(8,128)(2,1)S(1)}, bf16[1,128,128]{2,1,0:T(8,128)(2,1)S(1)}, u32[]{:S(2)}, u32[]{:S(2)}) collective-permute-start(bf16[1,128,128]{2,1,0:T(8,128)(2,1)S(1)} %copy-done.2), channel_id=1, source_target_pairs={{0,4},{1,5},{2,6},{3,7},{4,0},{5,1},{6,2},{7,3},{8,12},{9,13},{10,... | collective-permute-start | bytes 98312 | tf_op jit(solution)/shard_map/ppermute | solution.py:306
  64.6 1.5 collective-permute-start.11
  66.0 5.1 %collective-permute-start.12 = (bf16[1,128,128]{2,1,0:T(8,128)(2,1)S(1)}, bf16[1,128,128]{2,1,0:T(8,128)(2,1)S(1)}, u32[]{:S(2)}, u32[]{:S(2)}) collective-permute-start(bf16[1,128,128]{2,1,0:T(8,128)(2,1)S(1)} %copy-done.2), channel_id=1, source_target_pairs={{0,6},{1,7},{2,4},{3,5},{4,2},{5,3},{6,0},{7,1},{8,14},{9,15},{10,... | collective-permute-start | bytes 98312 | tf_op jit(solution)/shard_map/ppermute | solution.py:306
  71.9 18.0 %collective-permute-done.10.refs_4_ = bf16[1,128,128]{2,1,0:T(8,128)(2,1)S(1)} collective-permute-done((bf16[1,128,128]{2,1,0:T(8,128)(2,1)S(1)}, bf16[1,128,128]{2,1,0:T(8,128)(2,1)S(1)}, u32[]{:S(2)}, u32[]{:S(2)}) %collective-permute-start.10) | collective-permute-done | bytes 32800 | tf_op jit(solution)/shard_map/ppermute | solution.py:306
  90.0 3.3 %collective-permute-start.8 = (bf16[1,128,128]{2,1,0:T(8,128)(2,1)S(1)}, bf16[1,128,128]{2,1,0:T(8,128)(2,1)S(1)}, u32[]{:S(2)}, u32[]{:S(2)}) collective-permute-start(bf16[1,128,128]{2,1,0:T(8,128)(2,1)S(1)} %copy-done.2), channel_id=1, source_target_pairs={{0,2},{1,3},{2,0},{3,1},{4,6},{5,7},{6,4},{7,5},{8,10},{9,11},{10,... | collective-permute-start | bytes 98312 | tf_op jit(solution)/shard_map/ppermute | solution.py:306
  93.3 0.8 collective-permute-start.9
  94.2 1.3 collective-permute-done.8.refs_2_
  95.5 2.9 %collective-permute-done.9.refs_3_ = bf16[1,128,128]{2,1,0:T(8,128)(2,1)S(1)} collective-permute-done((bf16[1,128,128]{2,1,0:T(8,128)(2,1)S(1)}, bf16[1,128,128]{2,1,0:T(8,128)(2,1)S(1)}, u32[]{:S(2)}, u32[]{:S(2)}) %collective-permute-start.9) | collective-permute-done | bytes 32800 | tf_op jit(solution)/shard_map/ppermute | solution.py:306
  98.4 4.7 %shard_map.55 = (f32[128,8,128]{2,1,0:T(8,128)S(1)}, bf16[2048,512]{1,0:T(8,128)(2,1)}, bf16[4,128,128]{2,1,0:T(8,128)(2,1)S(1)}) custom-call(s32[15]{0:T(128)S(1)} %concatenate.7.s_ref, bf16[8,2048,128]{2,1,0:T(8,128)(2,1)} %all-to-all-done.slot_ref, bf16[1,128,128]{2,1,0:T(8,128)(2,1)S(1)} %copy-done.2, ...), custom_call_target="tpu_custom_call" | custom-call | tf_op jit(solution)/shard_map/pallas_call | solution.py:146
  103.1 5.3 %shard_map.56 = (s16[128,24,128]{2,1,0:T(8,128)(2,1)S(1)}, bf16[512,2048]{1,0:T(8,128)(2,1)S(1)}, bf16[512,2048]{1,0:T(8,128)(2,1)S(1)}) custom-call(s32[15]{0:T(128)S(1)} %concatenate.7.s_ref, s16[16,8,64,128]{3,2,1,0:T(8,128)(2,1)S(1)} %all-to-all-done.1.code_ref, bf16[2048,512]{1,0:T(8,128)(2,1)} %get-tuple-element.15.refl_hbm.refl_ref, ...), custom_call_target="tpu_custom_call" | custom-call | tf_op jit(solution)/shard_map/pallas_call | solution.py:146
  108.5 21.4 %all_to_all.25.in_ref = s16[128,24,128]{2,1,0:T(8,128)(2,1)S(1)} all-to-all(s16[128,24,128]{2,1,0:T(8,128)(2,1)S(1)} %get-tuple-element.17), channel_id=1, replica_groups=mesh['row'=16,'col'=8] {'row','col'}, dimensions={0} | all-to-all | bytes 1572864 | tf_op jit(solution)/shard_map/all_to_all | solution.py:300
  129.9 0.8 shard_map.57
  130.7 16.9 %all_to_all.26.mine_ref = s16[64,24,128]{2,1,0:T(8,128)(2,1)S(1)} all-to-all(s16[64,24,128]{2,1,0:T(8,128)(2,1)S(1)} %shard_map.57), channel_id=1, replica_groups={{0,1,2,3,4,5,6,7,16,17,18,19,20,21,22,23,32,33,34,35,36,37,38,39,48,49,..., dimensions={0} | all-to-all | bytes 786432 | tf_op jit(solution)/shard_map/all_to_all | solution.py:328
  147.6 1.7 collective-permute-done.14.other_ref
  149.3 5.5 %shard_map.58 = s16[8,1056,128]{2,1,0:T(8,128)(2,1)S(1)} custom-call(s32[15]{0:T(128)S(1)} %concatenate.7.s_ref, s16[64,24,128]{2,1,0:T(8,128)(2,1)S(1)} %all_to_all.26.mine_ref, s16[64,24,128]{2,1,0:T(8,128)(2,1)S(1)} %collective-permute-done.14.other_ref, bf16[4,128,128]{2,1,0:T(8,128)(2,1)S(1)} %get-tuple-element.18.t_ref, ...), custom_call_target="tpu_custom_call" | custom-call | tf_op jit(solution)/shard_map/pallas_call | solution.py:146
  154.9 32.8 %all_to_all.27.code_ref = s16[8,1056,128]{2,1,0:T(8,128)(2,1)S(1)} all-to-all(s16[8,1056,128]{2,1,0:T(8,128)(2,1)S(1)} %shard_map.58), channel_id=1, replica_groups=mesh['row'=16,'col'=8] {'col'}, dimensions={0} | all-to-all | bytes 4325376 | tf_op jit(solution)/shard_map/all_to_all | solution.py:300
  187.7 2.2 %finish.1 = f32[64,16384]{1,0:T(8,128)} custom-call(s16[8,1056,128]{2,1,0:T(8,128)(2,1)S(1)} %all_to_all.27.code_ref), custom_call_target="tpu_custom_call" | custom-call | tf_op jit(solution)/shard_map/finish/pallas_call | solution.py:288
  (35 shorter events, 1.6 us)
Async XLA Ops:
  0.0 56.0 %all-to-all-start = ((bf16[8,2048,128]{2,1,0:T(8,128)(2,1)}), bf16[8,2048,128]{2,1,0:T(8,128)(2,1)}, u32[]{:S(2)}, u32[]{:S(2)}) async-start(bf16[8,2048,128]{2,1,0:T(8,128)(2,1)} %bitcast.23), calls=%async_computation | async-start | bytes 8388608 | tf_op jit(solution)/shard_map/all_to_all | solution.py:300
  7.1 2.2 %copy-start.1 = (f32[4,262144]{1,0:T(4,128)S(1)}, f32[4,262144]{1,0:T(4,128)}, u32[]{:S(2)}) copy-start(f32[4,262144]{1,0:T(4,128)} %e_ref.1) | copy-start | bytes 12582916
  13.7 7.0 %collective-permute-start = (s16[16,64,128]{2,1,0:T(8,128)(2,1)S(1)}, s16[16,64,128]{2,1,0:T(8,128)(2,1)S(1)}, u32[]{:S(2)}, u32[]{:S(2)}) collective-permute-start(s16[16,64,128]{2,1,0:T(8,128)(2,1)S(1)} %get-tuple-element.27), channel_id=1, source_target_pairs={{0,8},{8,0},{16,24},{24,16},{32,40},{40,32},{48,56},{56,48},{64,72... | collective-permute-start | bytes 786440 | tf_op jit(solution)/shard_map/ppermute | solution.py:318
  13.8 11.3 %collective-permute-start.1 = (s16[16,64,128]{2,1,0:T(8,128)(2,1)S(1)}, s16[16,64,128]{2,1,0:T(8,128)(2,1)S(1)}, u32[]{:S(2)}, u32[]{:S(2)}) collective-permute-start(s16[16,64,128]{2,1,0:T(8,128)(2,1)S(1)} %get-tuple-element.26), channel_id=1, source_target_pairs={{0,16},{8,24},{16,32},{24,40},{32,48},{40,56},{48,0},{56,8},{64,80... | collective-permute-start | bytes 786440 | tf_op jit(solution)/shard_map/ppermute | solution.py:318
  15.8 14.4 %collective-permute-start.2 = (s16[16,64,128]{2,1,0:T(8,128)(2,1)S(1)}, s16[16,64,128]{2,1,0:T(8,128)(2,1)S(1)}, u32[]{:S(2)}, u32[]{:S(2)}) collective-permute-start(s16[16,64,128]{2,1,0:T(8,128)(2,1)S(1)} %get-tuple-element.25), channel_id=1, source_target_pairs={{0,24},{8,16},{16,40},{24,32},{32,56},{40,48},{48,8},{56,0},{64,88... | collective-permute-start | bytes 786440 | tf_op jit(solution)/shard_map/ppermute | solution.py:318
  17.4 20.3 %collective-permute-start.3 = (s16[16,64,128]{2,1,0:T(8,128)(2,1)S(1)}, s16[16,64,128]{2,1,0:T(8,128)(2,1)S(1)}, u32[]{:S(2)}, u32[]{:S(2)}) collective-permute-start(s16[16,64,128]{2,1,0:T(8,128)(2,1)S(1)} %get-tuple-element.24), channel_id=1, source_target_pairs={{0,32},{8,40},{16,48},{24,56},{32,0},{40,8},{48,16},{56,24},{64,96... | collective-permute-start | bytes 786440 | tf_op jit(solution)/shard_map/ppermute | solution.py:318
  19.4 22.9 %collective-permute-start.4 = (s16[16,64,128]{2,1,0:T(8,128)(2,1)S(1)}, s16[16,64,128]{2,1,0:T(8,128)(2,1)S(1)}, u32[]{:S(2)}, u32[]{:S(2)}) collective-permute-start(s16[16,64,128]{2,1,0:T(8,128)(2,1)S(1)} %get-tuple-element.23), channel_id=1, source_target_pairs={{0,40},{8,32},{16,56},{24,48},{32,8},{40,0},{48,24},{56,16},{64,10... | collective-permute-start | bytes 786440 | tf_op jit(solution)/shard_map/ppermute | solution.py:318
  20.7 21.6 %collective-permute-start.5 = (s16[16,64,128]{2,1,0:T(8,128)(2,1)S(1)}, s16[16,64,128]{2,1,0:T(8,128)(2,1)S(1)}, u32[]{:S(2)}, u32[]{:S(2)}) collective-permute-start(s16[16,64,128]{2,1,0:T(8,128)(2,1)S(1)} %get-tuple-element.22), channel_id=1, source_target_pairs={{0,48},{8,56},{16,0},{24,8},{32,16},{40,24},{48,32},{56,40},{64,11... | collective-permute-start | bytes 786440 | tf_op jit(solution)/shard_map/ppermute | solution.py:318
  25.0 17.4 %collective-permute-start.6 = (s16[16,64,128]{2,1,0:T(8,128)(2,1)S(1)}, s16[16,64,128]{2,1,0:T(8,128)(2,1)S(1)}, u32[]{:S(2)}, u32[]{:S(2)}) collective-permute-start(s16[16,64,128]{2,1,0:T(8,128)(2,1)S(1)} %get-tuple-element.21), channel_id=1, source_target_pairs={{0,56},{8,48},{16,8},{24,0},{32,24},{40,16},{48,40},{56,32},{64,12... | collective-permute-start | bytes 786440 | tf_op jit(solution)/shard_map/ppermute | solution.py:318
  42.5 13.5 %copy-start.3 = (s16[16,512,128]{2,1,0:T(8,128)(2,1)}, s16[16,512,128]{2,1,0:T(8,128)(2,1)S(1)}, u32[]{:S(2)}) copy-start(s16[16,512,128]{2,1,0:T(8,128)(2,1)S(1)} %constant_dynamic-update-slice_fusion) | copy-start | bytes 6291460
  56.0 5.0 %copy-start.2 = (bf16[1,128,128]{2,1,0:T(8,128)(2,1)S(1)}, bf16[1,128,128]{2,1,0:T(8,128)(2,1)}, u32[]{:S(2)}) copy-start(bf16[1,128,128]{2,1,0:T(8,128)(2,1)} %refs_0_.1) | copy-start | bytes 98308
  56.0 38.1 %copy-start.4 = (s32[4]{0:T(128)S(1)}, s32[4]{0:T(128)}, u32[]{:S(2)}) copy-start(s32[4]{0:T(128)} %param.8) | copy-start | bytes 52
  56.0 38.1 %copy-start.5 = (s32[4]{0:T(128)S(1)}, s32[4]{0:T(128)}, u32[]{:S(2)}) copy-start(s32[4]{0:T(128)} %param.9) | copy-start | bytes 52
  56.0 47.1 %all-to-all-start.1 = ((s16[16,8,64,128]{3,2,1,0:T(8,128)(2,1)}), s16[16,8,64,128]{3,2,1,0:T(8,128)(2,1)S(1)}, u32[]{:S(2)}, u32[]{:S(2)}) async-start(s16[16,8,64,128]{3,2,1,0:T(8,128)(2,1)} %bitcast.24), calls=%async_computation.1 | async-start | bytes 4194304 | tf_op jit(solution)/shard_map/all_to_all | solution.py:328
  61.1 28.9 %collective-permute-start.10 = (bf16[1,128,128]{2,1,0:T(8,128)(2,1)S(1)}, bf16[1,128,128]{2,1,0:T(8,128)(2,1)S(1)}, u32[]{:S(2)}, u32[]{:S(2)}) collective-permute-start(bf16[1,128,128]{2,1,0:T(8,128)(2,1)S(1)} %copy-done.2), channel_id=1, source_target_pairs={{0,4},{1,5},{2,6},{3,7},{4,0},{5,1},{6,2},{7,3},{8,12},{9,13},{10,... | collective-permute-start | bytes 98312 | tf_op jit(solution)/shard_map/ppermute | solution.py:306
  64.6 28.7 %collective-permute-start.11 = (bf16[1,128,128]{2,1,0:T(8,128)(2,1)S(1)}, bf16[1,128,128]{2,1,0:T(8,128)(2,1)S(1)}, u32[]{:S(2)}, u32[]{:S(2)}) collective-permute-start(bf16[1,128,128]{2,1,0:T(8,128)(2,1)S(1)} %copy-done.2), channel_id=1, source_target_pairs={{0,5},{1,4},{2,7},{3,6},{4,1},{5,0},{6,3},{7,2},{8,13},{9,12},{10,... | collective-permute-start | bytes 98312 | tf_op jit(solution)/shard_map/ppermute | solution.py:306
  66.0 28.2 %collective-permute-start.12 = (bf16[1,128,128]{2,1,0:T(8,128)(2,1)S(1)}, bf16[1,128,128]{2,1,0:T(8,128)(2,1)S(1)}, u32[]{:S(2)}, u32[]{:S(2)}) collective-permute-start(bf16[1,128,128]{2,1,0:T(8,128)(2,1)S(1)} %copy-done.2), channel_id=1, source_target_pairs={{0,6},{1,7},{2,4},{3,5},{4,2},{5,3},{6,0},{7,1},{8,14},{9,15},{10,... | collective-permute-start | bytes 98312 | tf_op jit(solution)/shard_map/ppermute | solution.py:306
  71.1 23.1 %collective-permute-start.13 = (bf16[1,128,128]{2,1,0:T(8,128)(2,1)S(1)}, bf16[1,128,128]{2,1,0:T(8,128)(2,1)S(1)}, u32[]{:S(2)}, u32[]{:S(2)}) collective-permute-start(bf16[1,128,128]{2,1,0:T(8,128)(2,1)S(1)} %copy-done.2), channel_id=1, source_target_pairs={{0,7},{1,6},{2,5},{3,4},{4,3},{5,2},{6,1},{7,0},{8,15},{9,14},{10,... | collective-permute-start | bytes 98312 | tf_op jit(solution)/shard_map/ppermute | solution.py:306
  71.2 23.0 %collective-permute-start.7 = (bf16[1,128,128]{2,1,0:T(8,128)(2,1)S(1)}, bf16[1,128,128]{2,1,0:T(8,128)(2,1)S(1)}, u32[]{:S(2)}, u32[]{:S(2)}) collective-permute-start(bf16[1,128,128]{2,1,0:T(8,128)(2,1)S(1)} %copy-done.2), channel_id=1, source_target_pairs={{0,1},{1,0},{2,3},{3,2},{4,5},{5,4},{6,7},{7,6},{8,9},{9,8},{10,11... | collective-permute-start | bytes 98312 | tf_op jit(solution)/shard_map/ppermute | solution.py:306
  90.0 5.5 %collective-permute-start.8 = (bf16[1,128,128]{2,1,0:T(8,128)(2,1)S(1)}, bf16[1,128,128]{2,1,0:T(8,128)(2,1)S(1)}, u32[]{:S(2)}, u32[]{:S(2)}) collective-permute-start(bf16[1,128,128]{2,1,0:T(8,128)(2,1)S(1)} %copy-done.2), channel_id=1, source_target_pairs={{0,2},{1,3},{2,0},{3,1},{4,6},{5,7},{6,4},{7,5},{8,10},{9,11},{10,... | collective-permute-start | bytes 98312 | tf_op jit(solution)/shard_map/ppermute | solution.py:306
  93.3 5.1 %collective-permute-start.9 = (bf16[1,128,128]{2,1,0:T(8,128)(2,1)S(1)}, bf16[1,128,128]{2,1,0:T(8,128)(2,1)S(1)}, u32[]{:S(2)}, u32[]{:S(2)}) collective-permute-start(bf16[1,128,128]{2,1,0:T(8,128)(2,1)S(1)} %copy-done.2), channel_id=1, source_target_pairs={{0,3},{1,2},{2,1},{3,0},{4,7},{5,6},{6,5},{7,4},{8,11},{9,10},{10,... | collective-permute-start | bytes 98312 | tf_op jit(solution)/shard_map/ppermute | solution.py:306
  108.5 40.9 %copy-start = (bf16[2048,512]{1,0:T(8,128)(2,1)S(1)}, bf16[2048,512]{1,0:T(8,128)(2,1)}, u32[]{:S(2)}) copy-start(bf16[2048,512]{1,0:T(8,128)(2,1)} %get-tuple-element.15.refl_hbm.refl_ref) | copy-start | bytes 6291460
  147.6 1.7 collective-permute-start.14

commit v6 on v5

v6 whole, which is shorter than its diff:
```python
import math

import jax
import jax.numpy as jnp
from jax import lax
from jax.experimental import pallas as pl
from jax.experimental.pallas import tpu as pltpu
from jax.sharding import PartitionSpec as P


PANELS = 4
NB = 128
K = 512
DEVS = 128
COLS = 8
OWN = 4
SUB = 2048
STEP = 512
STEPS = SUB // STEP
TILES = SUB // 128
HALVES = 2
PLANES = 4
PEERS = DEVS // HALVES
MINE = K // HALVES
BOTH = SUB * HALVES
WIDE = MINE // COLS
SPAN = 1024
SPANS = SUB // SPAN
PACK = 32
PAIRS = [(q, p) for q in range(PANELS) for p in range(q)]
ALL = ("row", "col")
ROOM = 24 << 20

ASINH_TOP = 12.5
KNEE = 6.0 / math.sinh(ASINH_TOP)
ASINH_SCALE = 32767.0 / ASINH_TOP
GAIN = 2.0 / KNEE
LN2 = math.log(2.0)
SHARES = PLANES * HALVES
SHEET = DEVS // SHARES


def signed(level, like):
    return jnp.where(like < 0.0, -level, level)


def to_float(code):
    return code.astype(jnp.int32).astype(jnp.float32)


def encode_value(x):
    y = jnp.abs(x) * (1.0 / KNEE)
    level = jnp.log(y + jnp.sqrt(y * y + 1.0)) * ASINH_SCALE + 0.5
    return signed(jnp.minimum(level, 32767.0).astype(jnp.int32), x).astype(jnp.int16)


def decode_value(code):
    angle = to_float(code) * (1.0 / (ASINH_SCALE * LN2))
    return jnp.exp2(angle) - jnp.exp2(-angle)


def power_of(most):
    return jnp.ceil(jnp.log(jnp.maximum(most, 1e-30)) * (8.0 / LN2) + 0.01)


def levels(x, power):
    scaled = x * (jnp.exp(power * (-LN2 / 8.0)) * 32767.0**2)
    root = scaled * lax.rsqrt(jnp.abs(scaled) + 1e-30)
    return jnp.round(root).astype(jnp.int32)


def unit_of(power):
    return jnp.exp(power * (LN2 / 8.0)) * (1.0 / 32767.0**2)


def dot32(a, b, dims=((1,), (0,))):
    return lax.dot_general(a, b, (dims, ((), ())), preferred_element_type=jnp.float32)


def split(x):
    high = x.astype(jnp.bfloat16)
    return high, (x - high.astype(jnp.float32)).astype(jnp.bfloat16)


def encode_kernel(place_ref, e_ref, out_ref):
    for d in range(COLS):
        x = e_ref[:, d * SUB : (d + 1) * SUB]
        tall = jnp.concatenate([x[:, t * 128 : (t + 1) * 128] for t in range(TILES)], axis=0)
        out_ref[0, d, 0] = encode_value(tall)


def encode(eigvecs, place):
    size = COLS * SUB

    def source(k, a, h, place_ref):
        return 0, (a * PLANES + lax.rem(place_ref[0] + k, PLANES)) * HALVES + h

    return pl.pallas_call(
        encode_kernel,
        out_shape=jax.ShapeDtypeStruct((PLANES, SHEET, HALVES, OWN * TILES, 128), jnp.int16),
        grid_spec=pltpu.PrefetchScalarGridSpec(
            num_scalar_prefetch=1,
            grid=(PLANES, SHEET // COLS, HALVES),
            in_specs=[pl.BlockSpec((OWN, size), source)],
            out_specs=pl.BlockSpec((1, COLS, 1, OWN * TILES, 128), lambda k, a, h, place_ref: (k, a, h, 0, 0)),
        ),
        compiler_params=pltpu.CompilerParams(vmem_limit_bytes=ROOM),
        name="encode",
    )(place, eigvecs)


def mask_kernel(s_ref, slot_ref, out_ref, refl_ref, sems):
    copies = []
    for step in range(STEPS):
        row_ids = s_ref[8] + step * STEP + lax.broadcasted_iota(jnp.int32, (STEP, NB), 0)
        base = row_ids - lax.broadcasted_iota(jnp.int32, (STEP, NB), 1)
        rows = slice(step * STEP, (step + 1) * STEP)
        for p in range(PANELS):
            below = base - s_ref[4 + p]
            unit = jnp.where(below == 0, jnp.float32(1.0), jnp.float32(0.0))
            block = jnp.where(below > 0, slot_ref[s_ref[p], rows, :].astype(jnp.float32), unit)
            refl_ref[rows, p * NB : (p + 1) * NB] = block.astype(jnp.bfloat16)
        part = pl.ds(step * STEP, STEP)
        copies.append(pltpu.make_async_copy(refl_ref.at[part], out_ref.at[part], sems.at[step]))
        copies[-1].start()
    for copy in copies:
        copy.wait()


def fetch_both(refl_hbm, other_hbm, refl_ref, sems):
    fetches = []
    for h, source in enumerate((refl_hbm, other_hbm)):
        fetches.append(pltpu.make_async_copy(source, refl_ref.at[pl.ds(h * SUB, SUB)], sems.at[h]))
        fetches[-1].start()
    return fetches


def gram_kernel(s_ref, refl_hbm, other_hbm, *refs):
    arrived, (gram_ref, t_ref, held, refl_ref, sems) = refs[:COLS], refs[COLS:]
    fetches = fetch_both(refl_hbm, other_hbm, refl_ref, sems)
    for k in range(COLS):
        held[k] = arrived[k][0]
    for p in range(PANELS):
        t_ref[p] = held[s_ref[9 + p]]
    for fetch in fetches:
        fetch.wait()
    v = refl_ref[...]
    gram = dot32(v, v, ((0,), (0,)))
    blocks = [gram[q * NB : (q + 1) * NB, p * NB : (p + 1) * NB] for q, p in PAIRS]
    most = jnp.zeros((1, 1), jnp.float32)
    for block in blocks:
        most = jnp.maximum(most, jnp.max(jnp.abs(block), axis=(0, 1), keepdims=True))
    power = power_of(most)
    rows = []
    for block in blocks:
        level = levels(block, power).astype(jnp.float32)
        rows += [level[0:PEERS], level[PEERS:NB]]
    rows += [jnp.zeros((PEERS, NB), jnp.float32)] * 3 + [jnp.broadcast_to(power, (PEERS, NB))]
    gram_ref[...] = jnp.swapaxes(jnp.stack(rows), 0, 1)


def call(kernel, outs, ins, scalars=None, scratch=(), hbm_in=(), hbm_out=()):
    spec, raw = pl.BlockSpec(memory_space=pltpu.VMEM), pl.BlockSpec(memory_space=pltpu.HBM)
    kept = [pltpu.with_memory_space_constraint(x, pltpu.HBM if i in hbm_in else pltpu.VMEM) for i, x in enumerate(ins)]
    head = [] if scalars is None else [scalars]
    return pl.pallas_call(
        kernel,
        out_shape=tuple(pltpu.HBM(*out) if i in hbm_out else pltpu.VMEM(*out) for i, out in enumerate(outs)),
        in_specs=[pl.BlockSpec(memory_space=pltpu.SMEM)] * len(head) + [raw if i in hbm_in else spec for i in range(len(ins))],
        out_specs=tuple(raw if i in hbm_out else spec for i in range(len(outs))),
        scratch_shapes=list(scratch),
        compiler_params=pltpu.CompilerParams(vmem_limit_bytes=ROOM),
    )(*head, *kept)


def fetch_room():
    return pltpu.VMEM((BOTH, PANELS * NB), jnp.bfloat16), pltpu.SemaphoreType.DMA((HALVES,))


def mask(scalars, slots):
    outs = (((SUB, PANELS * NB), jnp.bfloat16),)
    scratch = [pltpu.VMEM((SUB, PANELS * NB), jnp.bfloat16), pltpu.SemaphoreType.DMA((STEPS,))]
    return call(mask_kernel, outs, (slots,), scalars, scratch, hbm_out=(0,))[0]


def gram_of(scalars, refl, other, triangles):
    outs = (((PEERS, 16, NB), jnp.float32), ((PANELS, NB, NB), jnp.bfloat16))
    scratch = [pltpu.VMEM((COLS, NB, NB), jnp.bfloat16), *fetch_room()]
    return call(gram_kernel, outs, (refl, other, *triangles), scalars, scratch, hbm_in=(0, 1))


def project_kernel(s_ref, code_ref, refl_hbm, other_hbm, gram_ref, pack_ref, high_ref, low_ref, refl_ref, sems):
    fetches = fetch_both(refl_hbm, other_hbm, refl_ref, sems)
    upper = lax.broadcasted_iota(jnp.int32, (COLS // 2, 8, 128), 1) < OWN
    for r in range(PEERS // COLS):
        a, source = r // PLANES, r % PLANES
        turn = lax.rem(s_ref[13] + (PLANES - source), PLANES) * HALVES
        rows = slice(r * COLS * OWN, (r + 1) * COLS * OWN)
        for h in range(HALVES):
            share = turn + lax.rem(s_ref[14] + h, HALVES)
            for t in range(0, TILES, 2):
                code = code_ref[a * COLS : (a + 1) * COLS, share, t * OWN : (t + 2) * OWN, :]
                x = decode_value(code).reshape(COLS // 2, 2, 8, 128)
                even, odd = x[:, 0], x[:, 1]
                first = jnp.where(upper, even, pltpu.roll(odd, OWN, 1))
                second = jnp.where(upper, pltpu.roll(even, OWN, 1), odd)
                for k, tile in ((h * TILES + t, first), (h * TILES + t + 1, second)):
                    high, low = split(tile.reshape(COLS * OWN, 128))
                    high_ref[rows, k * 128 : (k + 1) * 128] = high
                    low_ref[rows, k * 128 : (k + 1) * 128] = low
    for fetch in fetches:
        fetch.wait()
    v = refl_ref[...]
    part = dot32(high_ref[...], v) + dot32(low_ref[...], v)
    each = MINE // 16
    row = lax.broadcasted_iota(jnp.int32, (each, 16, NB), 1)
    for p in range(PANELS):
        block = part[:, p * NB : (p + 1) * NB].reshape(each, 16, NB)
        power = power_of(jnp.max(jnp.abs(block), axis=(1, 2), keepdims=True))
        where = slice(p * each, (p + 1) * each)
        pack_ref[where, 0:16, :] = levels(block, power).astype(jnp.int16)
        tail = jnp.where(row == 14, power, gram_ref[where])
        pack_ref[where, 16:32, :] = tail.astype(jnp.int32).astype(jnp.int16)


def project(scalars, codes, refl, other, gram):
    outs = (((PEERS, PACK, NB), jnp.int16),) + (((MINE, BOTH), jnp.bfloat16),) * 2
    return call(project_kernel, outs, (codes, refl, other, gram), scalars, fetch_room(), hbm_in=(1, 2))


def total_kernel(in_ref, out_ref):
    level = to_float(in_ref[...])
    value = level * jnp.abs(level)
    proj = jnp.sum(value[:, 0:16] * unit_of(level[:, 30:31]), axis=0)
    gram = jnp.sum(value[:, 16:32] * unit_of(level[:, 31:32]), axis=0)
    row = lax.broadcasted_iota(jnp.int32, (16, NB), 0)
    gram = jnp.where(row < 12, gram, 0.0)
    proj_power = power_of(jnp.max(jnp.abs(proj), axis=(0, 1), keepdims=True))
    gram_power = power_of(jnp.max(jnp.abs(gram), axis=(0, 1), keepdims=True))
    tail = levels(gram, gram_power).astype(jnp.float32)
    tail = jnp.where(row == 14, proj_power, jnp.where(row == 15, gram_power, tail))
    code = jnp.concatenate([levels(proj, proj_power), tail.astype(jnp.int32)], axis=0)
    out_ref[...] = jnp.broadcast_to(code[None], out_ref.shape).astype(jnp.int16)


def total(parts):
    return call(total_kernel, ((parts.shape, parts.dtype),), (parts,))[0]


def update_kernel(s_ref, sums_ref, t_ref, high_ref, low_ref, refl_ref, other_ref, out_ref, c_high, c_low):
    level = to_float(sums_ref[...])
    value = level * jnp.abs(level)
    proj = value[:, 0:16] * unit_of(level[:, 30:31])
    halves = jnp.swapaxes(value[:, 16:32] * unit_of(level[:, 31:32]), 0, 1)
    gram = {}
    for b, pair in enumerate(PAIRS):
        gram[pair] = split(jnp.concatenate([halves[2 * b], halves[2 * b + 1]], axis=0))
    found = {}
    for p in reversed(range(PANELS)):
        rest = proj[p * 16 : (p + 1) * 16].reshape(MINE, NB)
        for q in range(p + 1, PANELS):
            (c1, c2), (g1, g2) = found[q], gram[(q, p)]
            rest -= dot32(c1, g1) + (dot32(c1, g2) + dot32(c2, g1))
        triangle = t_ref[p]
        r1, r2 = split(rest)
        dims = ((1,), (1,))
        found[p] = split(dot32(r1, triangle, dims) + dot32(r2, triangle, dims))
        c_high[:, p * NB : (p + 1) * NB] = found[p][0]
        c_low[:, p * NB : (p + 1) * NB] = found[p][1]
    for step in range(HALVES * SPANS):
        h, k = step // SPANS, step % SPANS
        cols = slice(step * SPAN, (step + 1) * SPAN)
        v = (refl_ref, other_ref)[h][k * SPAN : (k + 1) * SPAN, :]
        change = dot32(c_high[...], v, ((1,), (1,))) + dot32(c_low[...], v, ((1,), (1,)))
        back = high_ref[:, cols].astype(jnp.float32) + (low_ref[:, cols].astype(jnp.float32) - change)
        to = lax.rem(s_ref[14] + h, HALVES) * COLS
        for c in range(COLS):
            block = back[c * WIDE : (c + 1) * WIDE]
            power = power_of(jnp.max(jnp.abs(block), axis=(0, 1), keepdims=True))
            code = levels(block, power).astype(jnp.int16)
            for t in range(SPAN // 128):
                at = (k * (SPAN // 128) + t) * WIDE
                out_ref[to + c, at : at + WIDE, :] = code[:, t * 128 : (t + 1) * 128]
            at = TILES * WIDE + k * 8
            out_ref[to + c, at : at + 8, :] = jnp.broadcast_to(power, (8, 128)).astype(jnp.int32).astype(jnp.int16)


def update(scalars, sums, triangles, high, low, refl, other):
    outs = (((HALVES * COLS, TILES * WIDE + 8 * SPANS, 128), jnp.int16),)
    scratch = [pltpu.VMEM((MINE, PANELS * NB), jnp.bfloat16)] * 2
    return call(update_kernel, outs, (sums, triangles, high, low, refl, other), scalars, scratch)[0]


def finish_kernel(code_ref, out_ref, rows, sems):
    copies = []
    for c in range(COLS):
        for h in range(HALVES):
            lines = slice(h * WIDE, (h + 1) * WIDE)
            for k in range(SPANS):
                at = TILES * WIDE + 8 * k
                unit = unit_of(to_float(code_ref[h * COLS + c, at : at + 8, :])) * (1.0 / GAIN)
                unit = jnp.concatenate([unit] * (WIDE // 8), axis=0)
                for t in range(k * (SPAN // 128), (k + 1) * (SPAN // 128)):
                    level = to_float(code_ref[h * COLS + c, t * WIDE : (t + 1) * WIDE, :])
                    rows[lines, c * SUB + t * 128 : c * SUB + (t + 1) * 128] = level * jnp.abs(level) * unit
        part = (slice(None), pl.ds(c * SUB, SUB))
        copies.append(pltpu.make_async_copy(rows.at[part], out_ref.at[part], sems.at[c]))
        copies[-1].start()
    for copy in copies:
        copy.wait()


def finish(codes):
    return pl.pallas_call(
        finish_kernel,
        out_shape=jax.ShapeDtypeStruct((K // COLS, COLS * SUB), jnp.float32),
        in_specs=[pl.BlockSpec(memory_space=pltpu.VMEM)],
        out_specs=pl.BlockSpec(memory_space=pl.ANY),
        scratch_shapes=[pltpu.VMEM((K // COLS, COLS * SUB), jnp.float32), pltpu.SemaphoreType.DMA((COLS,))],
        compiler_params=pltpu.CompilerParams(vmem_limit_bytes=ROOM),
        name="finish",
    )(pltpu.with_memory_space_constraint(codes, pltpu.VMEM))


def exchange(x, axis):
    return lax.all_to_all(x, axis, split_axis=0, concat_axis=0, tiled=True)


def spread(x):
    blocks = [x]
    for k in range(1, COLS):
        blocks.append(lax.ppermute(x, "col", [(c, c ^ k) for c in range(COLS)]))
    return blocks


def across(sent):
    sent = sent.reshape(PLANES, SHEET, HALVES * OWN * TILES, 128)
    shares = [sent[0]]
    for k in range(1, PLANES):
        pairs = []
        for r in range(DEVS // COLS):
            z = r // HALVES % PLANES
            pairs.append((r, r + ((z + k) % PLANES - z) * HALVES))
        shares.append(lax.ppermute(sent[k], "row", pairs))
    packed = jnp.concatenate(shares, axis=1)
    return packed.reshape(SHEET, SHARES, OWN * TILES, 128)


def to_owners(x):
    groups = [[(r + h) * COLS + c for h in range(HALVES) for c in range(COLS)] for r in range(0, DEVS // COLS, HALVES)]
    return lax.all_to_all(x, ALL, split_axis=0, concat_axis=0, tiled=True, axis_index_groups=groups)


def within(x, size):
    groups = []
    for share in range(size):
        rows = [r for r in range(DEVS // COLS) if r % size == share]
        groups.append([r * COLS + c for r in rows for c in range(COLS)])
    return lax.all_to_all(x, ALL, split_axis=0, concat_axis=0, tiled=True, axis_index_groups=groups)


def local(eigvecs, panels, tfactors, owners, offsets):
    row, col = lax.axis_index("row"), lax.axis_index("col")
    place = jnp.stack([row // HALVES % PLANES, row % HALVES])
    own = jnp.stack([(row * COLS + col) * SUB])
    scalars = jnp.concatenate([owners, offsets, own, owners ^ col, place])
    slots = exchange(panels.reshape(COLS, SUB, NB), "col")
    triangles = spread(tfactors)
    planes = encode(eigvecs, place)
    sent, slots = lax.optimization_barrier((across(planes), slots))
    codes = within(sent, SHARES)
    refl = mask(scalars, slots)
    other = lax.ppermute(refl, "row", [(r, r ^ 1) for r in range(DEVS // COLS)])
    gram, triangles = gram_of(scalars, refl, other, triangles)
    pack, high, low = project(scalars, codes, refl, other, gram)
    sums = within(total(within(pack, HALVES)), HALVES)
    out = update(scalars, sums, triangles, high, low, refl, other)
    return finish(to_owners(out))


def solution(mesh):
    in_specs = (P(ALL, None), P("col", "row", None), P("col", None, None), P(), P())
    out_specs = P("col", "row")
    return jax.shard_map(local, mesh=mesh, in_specs=in_specs, out_specs=out_specs, check_vma=False)
```

time: 190 us -> 200 us (1.053)
  Pallas kernels: 22.7 us -> 28.7 us
  waiting for transfers between devices: 56.9 us -> 62.9 us
  starting transfers between devices: 36.2 us -> 31.3 us
  other arithmetic: 0.08 us -> 2.6 us
  blocking collectives: 71.1 us -> 68.7 us
    all_to_all x2 -> x1, blocking collectives: 54.2 us -> 33.4 us  [to_owners(): lax.all_to_all(x, ALL, split_axis=0, concat_axis=0, tiled=True, axis_inde...]
    all_to_all x1 -> x2, blocking collectives: 16.9 us -> 35.3 us  [within(): lax.all_to_all(x, ALL, split_axis=0, concat_axis=0, tiled=True, axis_inde...]
    ppermute x7, waiting for transfers between devices: 22.2 us -> 28.8 us  [spread(): blocks.append(lax.ppermute(x, 'col', [(c, c ^ k) for c in range(COLS)]))]
    pallas_call x4 -> x5, Pallas kernels: 16.3 us -> 22.2 us  [call(): pl.pallas_call(kernel, out_shape=tuple((pltpu.HBM(*out) if i in hbm_out e...]
    all_to_all x1, waiting for transfers between devices: 13.5 us -> 9.84 us  [exchange(): return lax.all_to_all(x, axis, split_axis=0, concat_axis=0, tiled=True)]
    ppermute x8 -> x4, starting transfers between devices: 9.11 us -> 5.45 us  [the longest x3 5.37 us: across(): shares.append(lax.ppermute(sent[k], 'row', pairs))]
    ppermute x8 -> x4, waiting for transfers between devices: 21.1 us -> 24.3 us  [the longest x3 24.3 us: across(): shares.append(lax.ppermute(sent[k], 'row', pairs))]
    concatenate x0 -> x1, other arithmetic: none -> 2.52 us  [across(): packed = jnp.concatenate(shares, axis=1)]
  transfers between devices with their start and end apart: 17 -> 13, of which waited for: 10 -> 7; matrix products, arithmetic and copies ran while one was open for 0% -> 1% of each run, Pallas kernels for 5% -> 5%
where the time goes in v6:
time: 200 us; the launch traced here: 198 us
  blocking collectives  68.7 us (34%)
  waiting for transfers between devices  62.9 us (31%)
  starting transfers between devices  31.3 us (16%)
  Pallas kernels  28.7 us (14%)
  local copies, waits for them, and re-layouts  3.86 us (2%)
  other arithmetic  2.6 us (1%)
    all_to_all x2, blocking collectives, within(): lax.all_to_all(x, ALL, split_axis=0, concat_axis=0, tiled=True, axis_inde...  35.3 us
    all_to_all x1, blocking collectives, to_owners(): lax.all_to_all(x, ALL, split_axis=0, concat_axis=0, tiled=True, axis_inde...  33.4 us
    ppermute x7, waiting for transfers between devices, spread(): blocks.append(lax.ppermute(x, 'col', [(c, c ^ k) for c in range(COLS)]))  28.8 us
    ppermute x3, waiting for transfers between devices, across(): shares.append(lax.ppermute(sent[k], 'row', pairs))  24.3 us
    pallas_call x5, Pallas kernels, call(): pl.pallas_call(kernel, out_shape=tuple((pltpu.HBM(*out) if i in hbm_out e...  22.2 us
    ppermute x7, starting transfers between devices, spread(): blocks.append(lax.ppermute(x, 'col', [(c, c ^ k) for c in range(COLS)]))  13.9 us
    all_to_all x1, waiting for transfers between devices, exchange(): return lax.all_to_all(x, axis, split_axis=0, concat_axis=0, tiled=True)  9.84 us
    all_to_all x1, starting transfers between devices, exchange(): return lax.all_to_all(x, axis, split_axis=0, concat_axis=0, tiled=True)  7.04 us
  transfers between devices with their start and end apart: 13, of which 7 were waited for; matrix products, arithmetic and copies ran while one was open for 1% of the time, Pallas kernels for 5%

profile of v6, /device:TPU:0, one launch (start us, length us, event | category | flops | bytes accessed | tf_op | source)
XLA Modules:
  0.0 198.4 jit_solution(6626485186319118668)
XLA Ops:
  0.0 7.0 %all-to-all-start = ((bf16[8,2048,128]{2,1,0:T(8,128)(2,1)}), bf16[8,2048,128]{2,1,0:T(8,128)(2,1)}, u32[]{:S(2)}, u32[]{:S(2)}) async-start(bf16[8,2048,128]{2,1,0:T(8,128)(2,1)} %bitcast.10), calls=%async_computation | async-start | bytes 8388608 | tf_op jit(solution)/shard_map/all_to_all | solution.py:326
  7.1 2.2 %copy-done.3 = f32[4,262144]{1,0:T(4,128)S(1)} copy-done((f32[4,262144]{1,0:T(4,128)S(1)}, f32[4,262144]{1,0:T(4,128)}, u32[]{:S(2)}) %copy-start.3) | copy-done | bytes 4194328
  9.3 4.3 %encode.1 = s16[4,16,2,64,128]{4,3,2,1,0:T(8,128)(2,1)S(1)} custom-call(s32[2]{0:T(128)S(1)} %pad_add_fusion.1.place_ref, f32[4,262144]{1,0:T(4,128)S(1)} %copy-done.3), custom_call_target="tpu_custom_call" | custom-call | tf_op jit(solution)/shard_map/encode/pallas_call | solution.py:98
  13.6 0.3 fusion
  13.9 4.1 %collective-permute-start.2 = (s16[16,128,128]{2,1,0:T(8,128)(2,1)S(1)}, s16[16,128,128]{2,1,0:T(8,128)(2,1)S(1)}, u32[]{:S(2)}, u32[]{:S(2)}) collective-permute-start(s16[16,128,128]{2,1,0:T(8,128)(2,1)S(1)} %bitcast.14), channel_id=1, source_target_pairs={{0,48},{8,56},{16,0},{24,8},{32,16},{40,24},{48,32},{56,40},{64,11... | collective-permute-start | bytes 1572872 | tf_op jit(solution)/shard_map/ppermute | solution.py:344
  18.0 1.3 collective-permute-start
  19.4 20.8 %collective-permute-done.2 = s16[16,128,128]{2,1,0:T(8,128)(2,1)S(1)} collective-permute-done((s16[16,128,128]{2,1,0:T(8,128)(2,1)S(1)}, s16[16,128,128]{2,1,0:T(8,128)(2,1)S(1)}, u32[]{:S(2)}, u32[]{:S(2)}) %collective-permute-start.2) | collective-permute-done | bytes 524320 | tf_op jit(solution)/shard_map/ppermute | solution.py:344
  40.2 3.5 %collective-permute-done = s16[16,128,128]{2,1,0:T(8,128)(2,1)} collective-permute-done((s16[16,128,128]{2,1,0:T(8,128)(2,1)S(1)}, s16[16,128,128]{2,1,0:T(8,128)(2,1)}, u32[]{:S(2)}, u32[]{:S(2)}) %collective-permute-start) | collective-permute-done | bytes 524320 | tf_op jit(solution)/shard_map/ppermute | solution.py:344
  43.7 2.5 %pad_add_fusion = s16[16,512,128]{2,1,0:T(8,128)(2,1)} fusion(s16[16,128,128]{2,1,0:T(8,128)(2,1)S(1)} %collective-permute-done.2, s16[16,128,128]{2,1,0:T(8,128)(2,1)S(1)} %collective-permute-done.1, s16[16,128,128]{2,1,0:T(8,128)(2,1)} %collective-permute-done, s16[16,128,128]{2,1,0:T(8,128)(2,1)S(1)} %bitcast.11), kind=kLoop, calls=%fused_computation | loop fusion | flops 3145728 | bytes 4194304 | tf_op jit(solution)/shard_map/concatenate | solution.py:345
  46.2 9.8 %all-to-all-done.slot_ref = bf16[8,2048,128]{2,1,0:T(8,128)(2,1)} async-done(((bf16[8,2048,128]{2,1,0:T(8,128)(2,1)}), bf16[8,2048,128]{2,1,0:T(8,128)(2,1)}, u32[]{:S(2)}, u32[]{:S(2)}) %all-to-all-start) | async-done | bytes 4194336 | tf_op jit(solution)/shard_map/all_to_all | solution.py:326
  56.0 4.1 %shard_map.55.refl_hbm.refl_ref = bf16[2048,512]{1,0:T(8,128)(2,1)} custom-call(s32[15]{0:T(128)S(1)} %concatenate.7.s_ref, bf16[8,2048,128]{2,1,0:T(8,128)(2,1)} %all-to-all-done.slot_ref), custom_call_target="tpu_custom_call" | custom-call | tf_op jit(solution)/shard_map/pallas_call | solution.py:166
  60.2 0.1 collective-permute-start.3
  60.2 4.9 %all-to-all-start.1 = ((s16[16,8,64,128]{3,2,1,0:T(8,128)(2,1)}), s16[16,8,64,128]{3,2,1,0:T(8,128)(2,1)}, u32[]{:S(2)}, u32[]{:S(2)}) async-start(s16[16,8,64,128]{3,2,1,0:T(8,128)(2,1)} %bitcast.9), calls=%async_computation.1 | async-start | bytes 4194304 | tf_op jit(solution)/shard_map/all_to_all | solution.py:359
  65.2 5.9 %collective-permute-start.9 = (bf16[1,128,128]{2,1,0:T(8,128)(2,1)S(1)}, bf16[1,128,128]{2,1,0:T(8,128)(2,1)S(1)}, u32[]{:S(2)}, u32[]{:S(2)}) collective-permute-start(bf16[1,128,128]{2,1,0:T(8,128)(2,1)S(1)} %copy-done.4), channel_id=1, source_target_pairs={{0,6},{1,7},{2,4},{3,5},{4,2},{5,3},{6,0},{7,1},{8,14},{9,15},{10,... | collective-permute-start | bytes 98312 | tf_op jit(solution)/shard_map/ppermute | solution.py:332
  71.1 0.6 collective-permute-start.8
  71.6 3.0 %collective-permute-start.7 = (bf16[1,128,128]{2,1,0:T(8,128)(2,1)S(1)}, bf16[1,128,128]{2,1,0:T(8,128)(2,1)S(1)}, u32[]{:S(2)}, u32[]{:S(2)}) collective-permute-start(bf16[1,128,128]{2,1,0:T(8,128)(2,1)S(1)} %copy-done.4), channel_id=1, source_target_pairs={{0,4},{1,5},{2,6},{3,7},{4,0},{5,1},{6,2},{7,3},{8,12},{9,13},{10,... | collective-permute-start | bytes 98312 | tf_op jit(solution)/shard_map/ppermute | solution.py:332
  74.6 0.6 collective-permute-start.6
  75.1 22.2 %collective-permute-done.9.refs_6_ = bf16[1,128,128]{2,1,0:T(8,128)(2,1)S(1)} collective-permute-done((bf16[1,128,128]{2,1,0:T(8,128)(2,1)S(1)}, bf16[1,128,128]{2,1,0:T(8,128)(2,1)S(1)}, u32[]{:S(2)}, u32[]{:S(2)}) %collective-permute-start.9) | collective-permute-done | bytes 32800 | tf_op jit(solution)/shard_map/ppermute | solution.py:332
  97.3 1.6 collective-permute-start.5
  98.9 1.4 collective-permute-start.4
  100.4 0.9 collective-permute-start.10
  101.3 1.5 collective-permute-done.5.refs_2_
  102.8 5.1 %collective-permute-done.10.refs_7_ = bf16[1,128,128]{2,1,0:T(8,128)(2,1)S(1)} collective-permute-done((bf16[1,128,128]{2,1,0:T(8,128)(2,1)S(1)}, bf16[1,128,128]{2,1,0:T(8,128)(2,1)S(1)}, u32[]{:S(2)}, u32[]{:S(2)}) %collective-permute-start.10) | collective-permute-done | bytes 32800 | tf_op jit(solution)/shard_map/ppermute | solution.py:332
  107.9 1.3 copy-done.1
  109.2 5.5 %shard_map.56 = (f32[64,16,128]{2,1,0:T(8,128)S(1)}, bf16[4,128,128]{2,1,0:T(8,128)(2,1)S(1)}) custom-call(s32[15]{0:T(128)S(1)} %concatenate.7.s_ref, bf16[2048,512]{1,0:T(8,128)(2,1)} %shard_map.55.refl_hbm.refl_ref, bf16[2048,512]{1,0:T(8,128)(2,1)} %copy-done.1, bf16[1,128,128]{2,1,0:T(8,128)(2,1)S(1)} %copy-done.4, ...), custom_call_target="tpu_custom_call" | custom-call | tf_op jit(solution)/shard_map/pallas_call | solution.py:166
  114.7 6.7 %shard_map.57 = (s16[64,32,128]{2,1,0:T(8,128)(2,1)S(1)}, bf16[256,4096]{1,0:T(8,128)(2,1)S(1)}, bf16[256,4096]{1,0:T(8,128)(2,1)S(1)}) custom-call(s32[15]{0:T(128)S(1)} %concatenate.7.s_ref, s16[16,8,64,128]{3,2,1,0:T(8,128)(2,1)} %all-to-all-done.1.code_ref, bf16[2048,512]{1,0:T(8,128)(2,1)} %shard_map.55.refl_hbm.refl_ref, bf16[2048,512]{1,0:T(8,128)(2,1)} %copy-done.1, ...), custom_call_target="tpu_custom_call" | custom-call | tf_op jit(solution)/shard_map/pallas_call | solution.py:166
  121.4 18.7 %all_to_all.25.in_ref = s16[64,32,128]{2,1,0:T(8,128)(2,1)S(1)} all-to-all(s16[64,32,128]{2,1,0:T(8,128)(2,1)S(1)} %get-tuple-element.15), channel_id=1, replica_groups={{0,1,2,3,4,5,6,7,16,17,18,19,20,21,22,23,32,33,34,35,36,37,38,39,48,49,..., dimensions={0} | all-to-all | bytes 1048576 | tf_op jit(solution)/shard_map/all_to_all | solution.py:359
  140.1 0.6 shard_map.58
  140.7 16.5 %all_to_all.26.sums_ref = s16[64,32,128]{2,1,0:T(8,128)(2,1)S(1)} all-to-all(s16[64,32,128]{2,1,0:T(8,128)(2,1)S(1)} %shard_map.58), channel_id=1, replica_groups={{0,1,2,3,4,5,6,7,16,17,18,19,20,21,22,23,32,33,34,35,36,37,38,39,48,49,..., dimensions={0} | all-to-all | bytes 1048576 | tf_op jit(solution)/shard_map/all_to_all | solution.py:359
  157.3 5.4 %shard_map.59 = s16[16,528,128]{2,1,0:T(8,128)(2,1)S(1)} custom-call(s32[15]{0:T(128)S(1)} %concatenate.7.s_ref, s16[64,32,128]{2,1,0:T(8,128)(2,1)S(1)} %all_to_all.26.sums_ref, bf16[4,128,128]{2,1,0:T(8,128)(2,1)S(1)} %get-tuple-element.16.t_ref, bf16[256,4096]{1,0:T(8,128)(2,1)S(1)} %get-tuple-element.17.high_ref, ...), custom_call_target="tpu_custom_call" | custom-call | tf_op jit(solution)/shard_map/pallas_call | solution.py:166
  162.6 33.4 %all_to_all.27.code_ref = s16[16,528,128]{2,1,0:T(8,128)(2,1)S(1)} all-to-all(s16[16,528,128]{2,1,0:T(8,128)(2,1)S(1)} %shard_map.59), channel_id=1, replica_groups={{0,1,2,3,4,5,6,7,8,9,10,11,12,13,14,15},{16,17,18,19,20,21,22,23,24,25,..., dimensions={0} | all-to-all | bytes 4325376 | tf_op jit(solution)/shard_map/all_to_all | solution.py:351
  196.0 2.2 %finish.1 = f32[64,16384]{1,0:T(8,128)} custom-call(s16[16,528,128]{2,1,0:T(8,128)(2,1)S(1)} %all_to_all.27.code_ref), custom_call_target="tpu_custom_call" | custom-call | tf_op jit(solution)/shard_map/finish/pallas_call | solution.py:314
  (23 shorter events, 0.3 us)
Async XLA Ops:
  0.0 56.0 %all-to-all-start = ((bf16[8,2048,128]{2,1,0:T(8,128)(2,1)}), bf16[8,2048,128]{2,1,0:T(8,128)(2,1)}, u32[]{:S(2)}, u32[]{:S(2)}) async-start(bf16[8,2048,128]{2,1,0:T(8,128)(2,1)} %bitcast.10), calls=%async_computation | async-start | bytes 8388608 | tf_op jit(solution)/shard_map/all_to_all | solution.py:326
  7.1 2.2 %copy-start.3 = (f32[4,262144]{1,0:T(4,128)S(1)}, f32[4,262144]{1,0:T(4,128)}, u32[]{:S(2)}) copy-start(f32[4,262144]{1,0:T(4,128)} %e_ref.1) | copy-start | bytes 12582916
  13.6 5.7 %copy-start.5 = (s32[4]{0:T(128)S(1)}, s32[4]{0:T(128)}, u32[]{:S(2)}) copy-start(s32[4]{0:T(128)} %param.8) | copy-start | bytes 52
  13.6 5.7 %copy-start.6 = (s32[4]{0:T(128)S(1)}, s32[4]{0:T(128)}, u32[]{:S(2)}) copy-start(s32[4]{0:T(128)} %param.9) | copy-start | bytes 52
  13.9 26.2 %collective-permute-start.2 = (s16[16,128,128]{2,1,0:T(8,128)(2,1)S(1)}, s16[16,128,128]{2,1,0:T(8,128)(2,1)S(1)}, u32[]{:S(2)}, u32[]{:S(2)}) collective-permute-start(s16[16,128,128]{2,1,0:T(8,128)(2,1)S(1)} %bitcast.14), channel_id=1, source_target_pairs={{0,48},{8,56},{16,0},{24,8},{32,16},{40,24},{48,32},{56,40},{64,11... | collective-permute-start | bytes 1572872 | tf_op jit(solution)/shard_map/ppermute | solution.py:344
  18.0 22.1 %collective-permute-start.1 = (s16[16,128,128]{2,1,0:T(8,128)(2,1)S(1)}, s16[16,128,128]{2,1,0:T(8,128)(2,1)S(1)}, u32[]{:S(2)}, u32[]{:S(2)}) collective-permute-start(s16[16,128,128]{2,1,0:T(8,128)(2,1)S(1)} %bitcast.13), channel_id=1, source_target_pairs={{0,32},{8,40},{16,48},{24,56},{32,0},{40,8},{48,16},{56,24},{64,96... | collective-permute-start | bytes 1572872 | tf_op jit(solution)/shard_map/ppermute | solution.py:344
  18.0 25.7 %collective-permute-start = (s16[16,128,128]{2,1,0:T(8,128)(2,1)S(1)}, s16[16,128,128]{2,1,0:T(8,128)(2,1)}, u32[]{:S(2)}, u32[]{:S(2)}) collective-permute-start(s16[16,128,128]{2,1,0:T(8,128)(2,1)S(1)} %bitcast.12), channel_id=1, source_target_pairs={{0,16},{8,24},{16,32},{24,40},{32,48},{40,56},{48,0},{56,8},{64,80... | collective-permute-start | bytes 1572872 | tf_op jit(solution)/shard_map/ppermute | solution.py:344
  60.1 5.0 %copy-start.4 = (bf16[1,128,128]{2,1,0:T(8,128)(2,1)S(1)}, bf16[1,128,128]{2,1,0:T(8,128)(2,1)}, u32[]{:S(2)}) copy-start(bf16[1,128,128]{2,1,0:T(8,128)(2,1)} %refs_0_.1) | copy-start | bytes 98308
  60.2 47.7 %collective-permute-start.3 = (bf16[2048,512]{1,0:T(8,128)(2,1)}, bf16[2048,512]{1,0:T(8,128)(2,1)S(1)}, u32[]{:S(2)}, u32[]{:S(2)}) collective-permute-start(bf16[2048,512]{1,0:T(8,128)(2,1)} %shard_map.55.refl_hbm.refl_ref), channel_id=1, source_target_pairs={{0,8},{8,0},{16,24},{24,16},{32,40},{40,32},{48,56},{56,48},{64,72... | collective-permute-start | bytes 6291464 | tf_op jit(solution)/shard_map/ppermute | solution.py:373
  60.2 54.4 %all-to-all-start.1 = ((s16[16,8,64,128]{3,2,1,0:T(8,128)(2,1)}), s16[16,8,64,128]{3,2,1,0:T(8,128)(2,1)}, u32[]{:S(2)}, u32[]{:S(2)}) async-start(s16[16,8,64,128]{3,2,1,0:T(8,128)(2,1)} %bitcast.9), calls=%async_computation.1 | async-start | bytes 4194304 | tf_op jit(solution)/shard_map/all_to_all | solution.py:359
  65.2 32.1 %collective-permute-start.9 = (bf16[1,128,128]{2,1,0:T(8,128)(2,1)S(1)}, bf16[1,128,128]{2,1,0:T(8,128)(2,1)S(1)}, u32[]{:S(2)}, u32[]{:S(2)}) collective-permute-start(bf16[1,128,128]{2,1,0:T(8,128)(2,1)S(1)} %copy-done.4), channel_id=1, source_target_pairs={{0,6},{1,7},{2,4},{3,5},{4,2},{5,3},{6,0},{7,1},{8,14},{9,15},{10,... | collective-permute-start | bytes 98312 | tf_op jit(solution)/shard_map/ppermute | solution.py:332
  71.1 27.9 %collective-permute-start.8 = (bf16[1,128,128]{2,1,0:T(8,128)(2,1)S(1)}, bf16[1,128,128]{2,1,0:T(8,128)(2,1)S(1)}, u32[]{:S(2)}, u32[]{:S(2)}) collective-permute-start(bf16[1,128,128]{2,1,0:T(8,128)(2,1)S(1)} %copy-done.4), channel_id=1, source_target_pairs={{0,5},{1,4},{2,7},{3,6},{4,1},{5,0},{6,3},{7,2},{8,13},{9,12},{10,... | collective-permute-start | bytes 98312 | tf_op jit(solution)/shard_map/ppermute | solution.py:332
  71.6 28.7 %collective-permute-start.7 = (bf16[1,128,128]{2,1,0:T(8,128)(2,1)S(1)}, bf16[1,128,128]{2,1,0:T(8,128)(2,1)S(1)}, u32[]{:S(2)}, u32[]{:S(2)}) collective-permute-start(bf16[1,128,128]{2,1,0:T(8,128)(2,1)S(1)} %copy-done.4), channel_id=1, source_target_pairs={{0,4},{1,5},{2,6},{3,7},{4,0},{5,1},{6,2},{7,3},{8,12},{9,13},{10,... | collective-permute-start | bytes 98312 | tf_op jit(solution)/shard_map/ppermute | solution.py:332
  74.6 26.7 %collective-permute-start.6 = (bf16[1,128,128]{2,1,0:T(8,128)(2,1)S(1)}, bf16[1,128,128]{2,1,0:T(8,128)(2,1)S(1)}, u32[]{:S(2)}, u32[]{:S(2)}) collective-permute-start(bf16[1,128,128]{2,1,0:T(8,128)(2,1)S(1)} %copy-done.4), channel_id=1, source_target_pairs={{0,3},{1,2},{2,1},{3,0},{4,7},{5,6},{6,5},{7,4},{8,11},{9,10},{10,... | collective-permute-start | bytes 98312 | tf_op jit(solution)/shard_map/ppermute | solution.py:332
  97.3 5.4 %collective-permute-start.5 = (bf16[1,128,128]{2,1,0:T(8,128)(2,1)S(1)}, bf16[1,128,128]{2,1,0:T(8,128)(2,1)S(1)}, u32[]{:S(2)}, u32[]{:S(2)}) collective-permute-start(bf16[1,128,128]{2,1,0:T(8,128)(2,1)S(1)} %copy-done.4), channel_id=1, source_target_pairs={{0,2},{1,3},{2,0},{3,1},{4,6},{5,7},{6,4},{7,5},{8,10},{9,11},{10,... | collective-permute-start | bytes 98312 | tf_op jit(solution)/shard_map/ppermute | solution.py:332
  98.9 3.9 %collective-permute-start.4 = (bf16[1,128,128]{2,1,0:T(8,128)(2,1)S(1)}, bf16[1,128,128]{2,1,0:T(8,128)(2,1)S(1)}, u32[]{:S(2)}, u32[]{:S(2)}) collective-permute-start(bf16[1,128,128]{2,1,0:T(8,128)(2,1)S(1)} %copy-done.4), channel_id=1, source_target_pairs={{0,1},{1,0},{2,3},{3,2},{4,5},{5,4},{6,7},{7,6},{8,9},{9,8},{10,11... | collective-permute-start | bytes 98312 | tf_op jit(solution)/shard_map/ppermute | solution.py:332
  100.4 7.5 %collective-permute-start.10 = (bf16[1,128,128]{2,1,0:T(8,128)(2,1)S(1)}, bf16[1,128,128]{2,1,0:T(8,128)(2,1)S(1)}, u32[]{:S(2)}, u32[]{:S(2)}) collective-permute-start(bf16[1,128,128]{2,1,0:T(8,128)(2,1)S(1)} %copy-done.4), channel_id=1, source_target_pairs={{0,7},{1,6},{2,5},{3,4},{4,3},{5,2},{6,1},{7,0},{8,15},{9,14},{10,... | collective-permute-start | bytes 98312 | tf_op jit(solution)/shard_map/ppermute | solution.py:332
  107.9 1.3 copy-start.1
  114.7 42.6 %copy-start.2 = (bf16[2048,512]{1,0:T(8,128)(2,1)S(1)}, bf16[2048,512]{1,0:T(8,128)(2,1)}, u32[]{:S(2)}) copy-start(bf16[2048,512]{1,0:T(8,128)(2,1)} %copy-done.1) | copy-start | bytes 6291460
  121.4 35.9 %copy-start = (bf16[2048,512]{1,0:T(8,128)(2,1)S(1)}, bf16[2048,512]{1,0:T(8,128)(2,1)}, u32[]{:S(2)}) copy-start(bf16[2048,512]{1,0:T(8,128)(2,1)} %shard_map.55.refl_hbm.refl_ref) | copy-start | bytes 6291460
